TPU v7x, 32 devices: a whole 2x2x4 slice. The times are simulated.
32 devices in a mesh: seq: 2 (over x), shard: 16 (over z, y, core).
Axes of the slice: x: 2, y: 2, z: 4, core: 2. Of those that a mesh axis runs over, the one named last changes fastest.
Arguments:
- tokens: bfloat16 [2, 16, 1024, 768], P(None, 'shard', 'seq'), may hold values from -6 to 6
- kinds: int32 [2, 16, 1024], P(None, 'shard', 'seq'), may hold values 0 or 1
- groups: int32 [2, 16, 1024], P(None, 'shard', 'seq'), may hold values from 0 to 7, never falling along the last dimension, each value on 1 to 512 neighbouring positions
- query_weight: bfloat16 [768, 3072], P('shard'), may hold values from -0.21875 to 0.21875
- query_bias: bfloat16 [3072], P('shard'), may hold values from -3 to 3
- key_weight: bfloat16 [768, 768], P('shard'), may hold values from -0.21875 to 0.21875
- key_bias: bfloat16 [768], P('shard'), may hold values from -3 to 3
- value_weight: bfloat16 [768, 768], P('shard'), may hold values from -0.21875 to 0.21875
- value_bias: bfloat16 [768], P('shard'), may hold values from -3 to 3
- output_weight: bfloat16 [768, 768], P('shard'), may hold values from -0.875 to 0.875
- output_bias: bfloat16 [768], P('shard'), may hold values from -2 to 2
- norm1_gain: bfloat16 [768], P('shard'), may hold values from 0.5 to 1.5
- norm1_shift: bfloat16 [768], P('shard'), may hold values from -2 to 2
- up_weight: bfloat16 [768, 3072], P('shard'), may hold values from -0.21875 to 0.21875
- up_bias: bfloat16 [3072], P('shard'), may hold values from -3 to 3
- down_weight: bfloat16 [3072, 768], P('shard'), may hold values from -0.109375 to 0.109375
- down_bias: bfloat16 [768], P('shard'), may hold values from -2 to 2
- norm2_gain: bfloat16 [768], P('shard'), may hold values from 0.5 to 1.5
- norm2_shift: bfloat16 [768], P('shard'), may hold values from -2 to 2
- cotangent: bfloat16 [2, 16, 1024, 768], P(None, 'shard', 'seq'), may hold values from -6 to 6
Outputs:
- mixed: bfloat16 [2, 16, 1024, 768], P(None, 'shard', 'seq')
- input_grad: float32 [2, 16, 1024, 768], P(None, 'shard', 'seq')
- query_weight_grad: float32 [768, 3072], P('shard')
- query_bias_grad: float32 [3072], P('shard')
- key_weight_grad: float32 [768, 768], P('shard')
- key_bias_grad: float32 [768], P('shard')
- value_weight_grad: float32 [768, 768], P('shard')
- value_bias_grad: float32 [768], P('shard')
- output_weight_grad: float32 [768, 768], P('shard')
- output_bias_grad: float32 [768], P('shard')
- norm1_gain_grad: float32 [768], P('shard')
- norm1_shift_grad: float32 [768], P('shard')
- up_weight_grad: float32 [768, 3072], P('shard')
- up_bias_grad: float32 [3072], P('shard')
- down_weight_grad: float32 [3072, 768], P('shard')
- down_bias_grad: float32 [768], P('shard')
- norm2_gain_grad: float32 [768], P('shard')
- norm2_shift_grad: float32 [768], P('shard')
Inputs may be any that keep to these rules, and one draw needn't show every extreme that they name: `kinds`: 1 marks an entity token, 0 a word token. `groups`: document numbers never fall along a sequence; every document holds 1 to 512 tokens.
All inputs are finite; a program needn't handle non-finite values. No bound on the sum of `kinds` on one device may be relied on, other than what follows from the above.
Results may differ from a plain program's by a relative error of at most 0.02.
Values may be sent and summed in bfloat16 or wider, within the bound.
A program may use at most 192 MiB of HBM per device.

v0:
```python
import jax
import jax.numpy as jnp
from jax import lax
from jax.sharding import PartitionSpec as P

HEADS = 12


masked_score = -1e30
layer_eps = 1e-12


def inner_rows(left_side, right_side):
    return lax.dot_general(
        left_side, right_side, (((0,), (0,)), ((), ())), preferred_element_type=jnp.float32
    )


def against(left_side, right_side):
    return lax.dot_general(
        left_side, right_side, (((1,), (1,)), ((), ())), preferred_element_type=jnp.float32
    )


def column_sum(values):
    return jnp.sum(values.astype(jnp.float32), axis=0)


def forward_norm(hidden, norm_gain, norm_shift):
    center = hidden - jnp.mean(hidden, axis=-1, keepdims=True)
    rescale = lax.rsqrt(jnp.mean(center * center, axis=-1, keepdims=True) + layer_eps)
    normed = center * rescale
    return (
        normed * norm_gain.astype(jnp.float32) + norm_shift.astype(jnp.float32),
        normed,
        rescale,
    )


def backward_norm(upstream, normed, rescale, norm_gain):
    scaled = upstream * norm_gain.astype(jnp.float32)
    return rescale * (
        scaled
        - jnp.mean(scaled, axis=-1, keepdims=True)
        - normed * jnp.mean(scaled * normed, axis=-1, keepdims=True)
    )


def gelu_slope(values):
    cumulative = 0.5 * (1.0 + jax.scipy.special.erf(values * 0.7071067811865476))
    return cumulative + values * jnp.exp(-0.5 * values * values) * 0.3989422804014327


def split_keys(head_key_values, entity_seq, head_dim):
    keys_by_head = jnp.transpose(head_key_values[:, :, :head_dim], (1, 0, 2))
    values_by_head = jnp.transpose(head_key_values[:, :, head_dim:], (1, 0, 2))
    zero_keys = jnp.zeros_like(keys_by_head)
    key_mixed = jnp.concatenate(
        [
            jnp.where(entity_seq, zero_keys, keys_by_head),
            jnp.where(entity_seq, keys_by_head, zero_keys),
        ],
        axis=2,
    )
    return (key_mixed, values_by_head)


def head_forward(pieces, seq_groups, row_block, score_scale):
    query_head, key_mixed, value_head = pieces
    length = query_head.shape[0]
    block_count = length // row_block

    def one_block(block_pieces):
        query_rows, group_rows = block_pieces
        scores = against(query_rows, key_mixed) * score_scale
        allowed = group_rows[:, None] == seq_groups[None, :]
        scores = jnp.where(allowed, scores, masked_score)
        row_max = jnp.max(scores, axis=-1, keepdims=True)
        exp_scores = jnp.exp(scores - row_max)
        row_total = jnp.sum(exp_scores, axis=-1, keepdims=True)
        weights = (exp_scores / row_total).astype(jnp.bfloat16)
        context = jnp.dot(weights, value_head, preferred_element_type=jnp.float32).astype(
            jnp.bfloat16
        )
        return (context, row_max[:, 0] + jnp.log(row_total[:, 0]))

    context, logsum = lax.map(
        one_block,
        (
            query_head.reshape(block_count, row_block, -1),
            seq_groups.reshape(block_count, row_block),
        ),
    )
    return (context.reshape(length, -1), logsum.reshape(length))


def head_backward(pieces, seq_groups, entity_seq, row_block, score_scale):
    query_head, key_mixed, value_head, grad_head, logsum = pieces
    length = query_head.shape[0]
    pair_dim = query_head.shape[1]
    head_dim = value_head.shape[1]
    block_count = length // row_block

    def one_block(running, block_pieces):
        key_acc, value_acc = running
        query_rows, group_rows, grad_rows, logsum_rows = block_pieces
        scores = against(query_rows, key_mixed) * score_scale
        allowed = group_rows[:, None] == seq_groups[None, :]
        weights = jnp.where(allowed, jnp.exp(scores - logsum_rows[:, None]), 0.0)
        grad_weights = against(grad_rows, value_head)
        row_inner = jnp.sum(weights * grad_weights, axis=-1, keepdims=True)
        grad_scores = (weights * (grad_weights - row_inner)).astype(jnp.bfloat16)
        grad_query = (
            jnp.dot(grad_scores, key_mixed, preferred_element_type=jnp.float32) * score_scale
        ).astype(jnp.bfloat16)
        key_acc = key_acc + inner_rows(grad_scores, query_rows) * score_scale
        value_acc = value_acc + inner_rows(weights.astype(jnp.bfloat16), grad_rows)
        return ((key_acc, value_acc), grad_query)

    initial = (
        jnp.zeros((length, pair_dim), jnp.float32),
        jnp.zeros((length, head_dim), jnp.float32),
    )
    (key_acc, value_acc), grad_query = lax.scan(
        one_block,
        initial,
        (
            query_head.reshape(block_count, row_block, pair_dim),
            seq_groups.reshape(block_count, row_block),
            grad_head.reshape(block_count, row_block, head_dim),
            logsum.reshape(block_count, row_block),
        ),
    )
    grad_key = jnp.where(entity_seq, key_acc[:, head_dim:], key_acc[:, :head_dim])
    grad_pair = jnp.concatenate(
        [grad_key.astype(jnp.bfloat16), value_acc.astype(jnp.bfloat16)], axis=1
    )
    return (grad_query.reshape(length, pair_dim), grad_pair)


def gather_attention(
    query_weight,
    query_bias,
    key_weight,
    key_bias,
    value_weight,
    value_bias,
    output_weight,
    output_bias,
    norm1_gain,
    norm1_shift,
):
    return (
        lax.all_gather(query_weight, "shard", axis=0, tiled=True),
        lax.all_gather(query_bias, "shard", axis=0, tiled=True),
        lax.all_gather(key_weight, "shard", axis=0, tiled=True),
        lax.all_gather(key_bias, "shard", axis=0, tiled=True),
        lax.all_gather(value_weight, "shard", axis=0, tiled=True),
        lax.all_gather(value_bias, "shard", axis=0, tiled=True),
        lax.all_gather(output_weight, "shard", axis=0, tiled=True),
        lax.all_gather(output_bias, "shard", axis=0, tiled=True),
        lax.all_gather(norm1_gain, "shard", axis=0, tiled=True),
        lax.all_gather(norm1_shift, "shard", axis=0, tiled=True),
    )


def gather_feed(up_weight, up_bias, down_weight, down_bias, norm2_gain, norm2_shift):
    return (
        lax.all_gather(up_weight, "shard", axis=0, tiled=True),
        lax.all_gather(up_bias, "shard", axis=0, tiled=True),
        lax.all_gather(down_weight, "shard", axis=0, tiled=True),
        lax.all_gather(down_bias, "shard", axis=0, tiled=True),
        lax.all_gather(norm2_gain, "shard", axis=0, tiled=True),
        lax.all_gather(norm2_shift, "shard", axis=0, tiled=True),
    )


def gather_attention_again(
    query_weight,
    query_bias,
    key_weight,
    key_bias,
    value_weight,
    value_bias,
    output_weight,
    output_bias,
    norm1_gain,
    norm1_shift,
):
    return (
        lax.all_gather(query_weight, "shard", axis=0, tiled=True),
        lax.all_gather(query_bias, "shard", axis=0, tiled=True),
        lax.all_gather(key_weight, "shard", axis=0, tiled=True),
        lax.all_gather(key_bias, "shard", axis=0, tiled=True),
        lax.all_gather(value_weight, "shard", axis=0, tiled=True),
        lax.all_gather(value_bias, "shard", axis=0, tiled=True),
        lax.all_gather(output_weight, "shard", axis=0, tiled=True),
        lax.all_gather(output_bias, "shard", axis=0, tiled=True),
        lax.all_gather(norm1_gain, "shard", axis=0, tiled=True),
        lax.all_gather(norm1_shift, "shard", axis=0, tiled=True),
    )


def gather_feed_again(up_weight, up_bias, down_weight, down_bias, norm2_gain, norm2_shift):
    return (
        lax.all_gather(up_weight, "shard", axis=0, tiled=True),
        lax.all_gather(up_bias, "shard", axis=0, tiled=True),
        lax.all_gather(down_weight, "shard", axis=0, tiled=True),
        lax.all_gather(down_bias, "shard", axis=0, tiled=True),
        lax.all_gather(norm2_gain, "shard", axis=0, tiled=True),
        lax.all_gather(norm2_shift, "shard", axis=0, tiled=True),
    )


def scatter_attention(
    grad_qw, grad_qb, grad_kw, grad_kb, grad_vw, grad_vb, grad_ow, grad_ob, grad_gain, grad_shift
):
    return (
        lax.psum_scatter(grad_qw, "shard", scatter_dimension=0, tiled=True),
        lax.psum_scatter(grad_qb, "shard", scatter_dimension=0, tiled=True),
        lax.psum_scatter(grad_kw, "shard", scatter_dimension=0, tiled=True),
        lax.psum_scatter(grad_kb, "shard", scatter_dimension=0, tiled=True),
        lax.psum_scatter(grad_vw, "shard", scatter_dimension=0, tiled=True),
        lax.psum_scatter(grad_vb, "shard", scatter_dimension=0, tiled=True),
        lax.psum_scatter(grad_ow, "shard", scatter_dimension=0, tiled=True),
        lax.psum_scatter(grad_ob, "shard", scatter_dimension=0, tiled=True),
        lax.psum_scatter(grad_gain, "shard", scatter_dimension=0, tiled=True),
        lax.psum_scatter(grad_shift, "shard", scatter_dimension=0, tiled=True),
    )


def scatter_feed(grad_uw, grad_ub, grad_dw, grad_db, grad_gain, grad_shift):
    return (
        lax.psum_scatter(grad_uw, "shard", scatter_dimension=0, tiled=True),
        lax.psum_scatter(grad_ub, "shard", scatter_dimension=0, tiled=True),
        lax.psum_scatter(grad_dw, "shard", scatter_dimension=0, tiled=True),
        lax.psum_scatter(grad_db, "shard", scatter_dimension=0, tiled=True),
        lax.psum_scatter(grad_gain, "shard", scatter_dimension=0, tiled=True),
        lax.psum_scatter(grad_shift, "shard", scatter_dimension=0, tiled=True),
    )


def on_device(
    tokens,
    kinds,
    groups,
    query_weight,
    query_bias,
    key_weight,
    key_bias,
    value_weight,
    value_bias,
    output_weight,
    output_bias,
    norm1_gain,
    norm1_shift,
    up_weight,
    up_bias,
    down_weight,
    down_bias,
    norm2_gain,
    norm2_shift,
    cotangent,
):
    micro_count = tokens.shape[0]
    local_tokens = tokens.shape[2]
    model_width = tokens.shape[3]
    head_dim = model_width // HEADS
    score_scale = head_dim ** (-0.5)
    seq_devices = lax.axis_size("seq")
    group_heads = HEADS // seq_devices
    seq_length = local_tokens * seq_devices
    row_block = min(512, seq_length)
    attn_local = (
        query_weight,
        query_bias,
        key_weight,
        key_bias,
        value_weight,
        value_bias,
        output_weight,
        output_bias,
        norm1_gain,
        norm1_shift,
    )
    feed_local = (up_weight, up_bias, down_weight, down_bias, norm2_gain, norm2_shift)
    outputs = []
    input_grads = []
    attn_shards = None
    feed_shards = None
    for batch_index in range(micro_count):
        (
            full_query,
            full_query_bias,
            full_key,
            full_key_bias,
            full_value,
            full_value_bias,
            full_output,
            full_output_bias,
            first_gain,
            first_shift,
        ) = gather_attention(*attn_local)
        full_up, full_up_bias, full_down, full_down_bias, second_gain, second_shift = gather_feed(
            *feed_local
        )
        inputs = tokens[batch_index, 0]
        inputs_wide = inputs.astype(jnp.float32)
        own_kinds = kinds[batch_index, 0]
        own_groups = groups[batch_index, 0]
        seq_kinds, seq_groups = (
            lax.all_gather(own_kinds, "seq", axis=0, tiled=True),
            lax.all_gather(own_groups, "seq", axis=0, tiled=True),
        )
        entity_own = (own_kinds == 1)[:, None]
        entity_seq = (seq_kinds == 1)[:, None]
        queries = jnp.dot(inputs, full_query, preferred_element_type=jnp.float32) + full_query_bias
        query_word = jnp.where(
            entity_own, queries[:, 2 * model_width : 3 * model_width], queries[:, :model_width]
        )
        query_entity = jnp.where(
            entity_own, queries[:, 3 * model_width :], queries[:, model_width : 2 * model_width]
        )
        query_pairs = jnp.concatenate(
            [
                query_word.reshape(local_tokens, seq_devices, group_heads, head_dim),
                query_entity.reshape(local_tokens, seq_devices, group_heads, head_dim),
            ],
            axis=3,
        ).astype(jnp.bfloat16)
        keys = jnp.dot(inputs, full_key, preferred_element_type=jnp.float32) + full_key_bias
        values = jnp.dot(inputs, full_value, preferred_element_type=jnp.float32) + full_value_bias
        key_values = jnp.concatenate(
            [
                keys.reshape(local_tokens, seq_devices, group_heads, head_dim),
                values.reshape(local_tokens, seq_devices, group_heads, head_dim),
            ],
            axis=3,
        ).astype(jnp.bfloat16)
        head_queries = lax.all_to_all(query_pairs, "seq", split_axis=1, concat_axis=0, tiled=True)
        head_key_values = lax.all_to_all(key_values, "seq", split_axis=1, concat_axis=0, tiled=True)
        query_items = head_queries[:, 0]
        key_items = head_key_values[:, 0]
        key_mixed, values_by_head = split_keys(key_items, entity_seq, head_dim)
        queries_by_head = jnp.transpose(query_items, (1, 0, 2))
        context, logsum = lax.map(
            lambda pieces: head_forward(pieces, seq_groups, row_block, score_scale),
            (queries_by_head, key_mixed, values_by_head),
        )
        context_heads = jnp.transpose(context, (1, 0, 2))[:, None]
        logsum_heads = jnp.transpose(logsum)[:, None]
        context_tokens = lax.all_to_all(
            context_heads, "seq", split_axis=0, concat_axis=1, tiled=True
        ).reshape(local_tokens, model_width)
        attended = (
            jnp.dot(context_tokens, full_output, preferred_element_type=jnp.float32)
            + full_output_bias
        )
        first_out, normed_first, rescale_first = forward_norm(
            inputs_wide + attended, first_gain, first_shift
        )
        first_low = first_out.astype(jnp.bfloat16)
        pre_act = jnp.dot(first_low, full_up, preferred_element_type=jnp.float32) + full_up_bias
        activated = jax.nn.gelu(pre_act, approximate=False).astype(jnp.bfloat16)
        down_out = (
            jnp.dot(activated, full_down, preferred_element_type=jnp.float32) + full_down_bias
        )
        layer_out, normed_second, rescale_second = forward_norm(
            first_out + down_out, second_gain, second_shift
        )
        outputs.append(layer_out.astype(jnp.bfloat16))
        (
            full_query,
            full_query_bias,
            full_key,
            full_key_bias,
            full_value,
            full_value_bias,
            full_output,
            full_output_bias,
            first_gain,
            first_shift,
        ) = gather_attention_again(*attn_local)
        full_up, full_up_bias, full_down, full_down_bias, second_gain, second_shift = (
            gather_feed_again(*feed_local)
        )
        upstream = cotangent[batch_index, 0].astype(jnp.float32)
        grad_gain_two = jnp.sum(upstream * normed_second, axis=0)
        grad_shift_two = jnp.sum(upstream, axis=0)
        grad_second = backward_norm(upstream, normed_second, rescale_second, second_gain)
        grad_down_out = grad_second.astype(jnp.bfloat16)
        grad_down_w = inner_rows(activated, grad_down_out)
        grad_down_b = column_sum(grad_down_out)
        grad_activated = against(grad_down_out, full_down)
        grad_pre = (grad_activated * gelu_slope(pre_act)).astype(jnp.bfloat16)
        grad_up_w = inner_rows(first_low, grad_pre)
        grad_up_b = column_sum(grad_pre)
        grad_first = grad_second + against(grad_pre, full_up)
        grad_gain_one = jnp.sum(grad_first * normed_first, axis=0)
        grad_shift_one = jnp.sum(grad_first, axis=0)
        grad_resid = backward_norm(grad_first, normed_first, rescale_first, first_gain)
        grad_attn = grad_resid.astype(jnp.bfloat16)
        grad_output_w = inner_rows(context_tokens, grad_attn)
        grad_output_b = column_sum(grad_attn)
        grad_context = (
            against(grad_attn, full_output)
            .astype(jnp.bfloat16)
            .reshape(local_tokens, seq_devices, group_heads, head_dim)
        )
        grad_context_heads = lax.all_to_all(
            grad_context, "seq", split_axis=1, concat_axis=0, tiled=True
        )[:, 0]
        key_mixed, values_by_head = split_keys(head_key_values[:, 0], entity_seq, head_dim)
        grad_query_heads, grad_pair_heads = lax.map(
            lambda pieces: head_backward(pieces, seq_groups, entity_seq, row_block, score_scale),
            (
                jnp.transpose(head_queries[:, 0], (1, 0, 2)),
                key_mixed,
                values_by_head,
                jnp.transpose(grad_context_heads, (1, 0, 2)),
                jnp.transpose(logsum_heads[:, 0]),
            ),
        )
        back_query, back_pair = (
            lax.all_to_all(
                jnp.transpose(grad_query_heads, (1, 0, 2))[:, None],
                "seq",
                split_axis=0,
                concat_axis=1,
                tiled=True,
            ),
            lax.all_to_all(
                jnp.transpose(grad_pair_heads, (1, 0, 2))[:, None],
                "seq",
                split_axis=0,
                concat_axis=1,
                tiled=True,
            ),
        )
        back_query = back_query.reshape(local_tokens, HEADS, 2 * head_dim)
        back_pair = back_pair.reshape(local_tokens, HEADS, 2 * head_dim)
        grad_word = back_query[:, :, :head_dim].reshape(local_tokens, model_width)
        grad_entity = back_query[:, :, head_dim:].reshape(local_tokens, model_width)
        zero_block = jnp.zeros_like(grad_word)
        grad_queries = jnp.concatenate(
            [
                jnp.where(entity_own, zero_block, grad_word),
                jnp.where(entity_own, zero_block, grad_entity),
                jnp.where(entity_own, grad_word, zero_block),
                jnp.where(entity_own, grad_entity, zero_block),
            ],
            axis=1,
        )
        grad_keys = back_pair[:, :, :head_dim].reshape(local_tokens, model_width)
        grad_values = back_pair[:, :, head_dim:].reshape(local_tokens, model_width)
        grad_query_w = inner_rows(inputs, grad_queries)
        grad_query_b = column_sum(grad_queries)
        grad_key_w = inner_rows(inputs, grad_keys)
        grad_key_b = column_sum(grad_keys)
        grad_value_w = inner_rows(inputs, grad_values)
        grad_value_b = column_sum(grad_values)
        input_grads.append(
            grad_resid
            + against(grad_queries, full_query)
            + against(grad_keys, full_key)
            + against(grad_values, full_value)
        )
        attn_grads = (
            grad_query_w,
            grad_query_b,
            grad_key_w,
            grad_key_b,
            grad_value_w,
            grad_value_b,
            grad_output_w,
            grad_output_b,
            grad_gain_one,
            grad_shift_one,
        )
        feed_grads = (grad_up_w, grad_up_b, grad_down_w, grad_down_b, grad_gain_two, grad_shift_two)
        attn_part = scatter_attention(*attn_grads)
        feed_part = scatter_feed(*feed_grads)
        attn_shards = (
            attn_part if attn_shards is None else jax.tree.map(jnp.add, attn_shards, attn_part)
        )
        feed_shards = (
            feed_part if feed_shards is None else jax.tree.map(jnp.add, feed_shards, feed_part)
        )
    summed = (
        lax.psum(attn_shards[0].astype(jnp.bfloat16), "seq").astype(jnp.float32),
        lax.psum(attn_shards[1].astype(jnp.bfloat16), "seq").astype(jnp.float32),
        lax.psum(attn_shards[2].astype(jnp.bfloat16), "seq").astype(jnp.float32),
        lax.psum(attn_shards[3].astype(jnp.bfloat16), "seq").astype(jnp.float32),
        lax.psum(attn_shards[4].astype(jnp.bfloat16), "seq").astype(jnp.float32),
        lax.psum(attn_shards[5].astype(jnp.bfloat16), "seq").astype(jnp.float32),
        lax.psum(attn_shards[6].astype(jnp.bfloat16), "seq").astype(jnp.float32),
        lax.psum(attn_shards[7].astype(jnp.bfloat16), "seq").astype(jnp.float32),
        lax.psum(attn_shards[8].astype(jnp.bfloat16), "seq").astype(jnp.float32),
        lax.psum(attn_shards[9].astype(jnp.bfloat16), "seq").astype(jnp.float32),
        lax.psum(feed_shards[0].astype(jnp.bfloat16), "seq").astype(jnp.float32),
        lax.psum(feed_shards[1].astype(jnp.bfloat16), "seq").astype(jnp.float32),
        lax.psum(feed_shards[2].astype(jnp.bfloat16), "seq").astype(jnp.float32),
        lax.psum(feed_shards[3].astype(jnp.bfloat16), "seq").astype(jnp.float32),
        lax.psum(feed_shards[4].astype(jnp.bfloat16), "seq").astype(jnp.float32),
        lax.psum(feed_shards[5].astype(jnp.bfloat16), "seq").astype(jnp.float32),
    )
    mixed = jnp.stack(outputs)[:, None]
    input_grad = jnp.stack(input_grads)[:, None]
    return (
        mixed,
        input_grad,
        summed[0],
        summed[1],
        summed[2],
        summed[3],
        summed[4],
        summed[5],
        summed[6],
        summed[7],
        summed[8],
        summed[9],
        summed[10],
        summed[11],
        summed[12],
        summed[13],
        summed[14],
        summed[15],
    )


def solution(mesh):
    return jax.shard_map(
        on_device,
        mesh=mesh,
        in_specs=(
            P(None, "shard", "seq", None),
            P(None, "shard", "seq"),
            P(None, "shard", "seq"),
            P("shard", None),
            P("shard"),
            P("shard", None),
            P("shard"),
            P("shard", None),
            P("shard"),
            P("shard", None),
            P("shard"),
            P("shard"),
            P("shard"),
            P("shard", None),
            P("shard"),
            P("shard", None),
            P("shard"),
            P("shard"),
            P("shard"),
            P(None, "shard", "seq", None),
        ),
        out_specs=(
            P(None, "shard", "seq", None),
            P(None, "shard", "seq", None),
            P("shard", None),
            P("shard"),
            P("shard", None),
            P("shard"),
            P("shard", None),
            P("shard"),
            P("shard", None),
            P("shard"),
            P("shard"),
            P("shard"),
            P("shard", None),
            P("shard"),
            P("shard", None),
            P("shard"),
            P("shard"),
            P("shard"),
        ),
        check_vma=False,
    )
```

profile of v0, /device:TPU:0, one launch (start us, length us, event | category | flops | bytes accessed | tf_op | source)
XLA Modules:
  0.0 1389.4 jit_solution(8055826443786584276)
XLA Ops:
  22.2 63.2 %all-reduce.21 = (bf16[3072]{0:T(1024)(128)(2,1)S(1)}, bf16[768]{0:T(1024)(128)(2,1)S(1)}, bf16[768]{0:T(1024)(128)(2,1)S(1)}, bf16[768]{0:T(1024)(128)(2,1)S(1)...) all-reduce(bf16[3072]{0:T(1024)(128)(2,1)S(1)} %dynamic-update-slic, ...), channel_id=1, replica_groups=mesh['seq'=2,'shard'=16] {'shard'}, use_global_device_ids=true, to_apply=%add | all-reduce | flops 12288 | bytes 49152
  100.3 20.0 %all-gather = s32[1,1,1024]{2,1,0:T(1,128)S(1)} all-gather(s32[1,1,512]{2,1,0:T(1,128)S(1)} %get-tuple-element.899), channel_id=2, replica_groups=mesh['seq'=2,'shard'=16] {'seq'}, dimensions={2}, use_global_device_ids=true | all-gather | bytes 6144 | tf_op jit(solution)/shard_map/all_gather | solution.py:313
  141.0 4.8 all-to-all-start.4
  145.8 18.2 %all-gather.1 = s32[1,1,1024]{2,1,0:T(1,128)S(1)} all-gather(s32[1,1,512]{2,1,0:T(1,128)S(1)} %get-tuple-element.897), channel_id=3, replica_groups=mesh['seq'=2,'shard'=16] {'seq'}, dimensions={2}, use_global_device_ids=true | all-gather | bytes 6144 | tf_op jit(solution)/shard_map/all_gather | solution.py:312
  175.4 5.3 convolution_add_fusion.4
  210.2 5.0 all-to-all-start.3
  218.1 44.4 %while.111 = (s32[]{:T(128)}, bf16[6,1024,64]{2,1,0:T(8,128)(2,1)}, f32[6,1024]{1,0:T(8,128)S(1)}, bf16[6,1024,128]{2,1,0:T(8,128)(2,1)}, s32[1024]{0:T(1024)S(1...) while((s32[]{:T(128)}, bf16[6,1024,64]{2,1,0:T(8,128)(2,1)}, ...), condition=%wide.wide.region_5.6_spmd, body=%wide.wide.region_0.5_spmd.sunk | while | flops 206077440 | bytes 9026386 | solution.py:346
  275.5 44.3 %while.113 = (s32[]{:T(128)}, bf16[6,1024,64]{2,1,0:T(8,128)(2,1)}, f32[6,1024]{1,0:T(8,128)S(1)}, bf16[6,1024,128]{2,1,0:T(8,128)(2,1)}, s32[1024]{0:T(1024)S(1...) while((s32[]{:T(128)}, bf16[6,1024,64]{2,1,0:T(8,128)(2,1)}, ...), condition=%wide.wide.region_15.16_spmd, body=%wide.wide.region_10.15_spmd.sunk | while | flops 206077440 | bytes 9026386 | solution.py:346
  347.9 4.9 fusion.148
  355.5 31.8 %fusion.54 = (bf16[512,3072]{1,0:T(8,128)(2,1)}, bf16[512,3072]{1,0:T(8,128)(2,1)}, f32[512,3072]{1,0:T(8,128)}) fusion(f32[3072]{0:T(1024)S(1)} %copy-done.106, f32[512,3072]{1,0:T(8,128)S(1)} %fusion.148, bf16[768,3072]{1,0:T(8,128)(2,1)S(1)} %copy-done.126, f32[512,768]{1,0:T(8,128)S(1)} %copy-done.75, f32[768]{0:T(1024)S(1)} %copy-done.88, ...), kind=kOutput, calls=%fused_computation.111 | convolution fusion | flops 2625503232 | bytes 25188352 | tf_op jit(solution)/shard_map/dot_general | solution.py:363
  387.3 6.2 fusion.170
  403.2 8.2 convert_reduce_fusion.1
  411.4 4.7 multiply_reduce_fusion.3
  416.2 5.2 convert_reduce_fusion
  421.4 7.2 convert_reduce_fusion.13
  455.3 160.6 %while.115 = (s32[]{:T(128)}, bf16[6,1024,128]{2,1,0:T(8,128)(2,1)}, bf16[6,1024,128]{1,2,0:T(8,128)(2,1)}, bf16[6,1024,128]{2,1,0:T(8,128)(2,1)}, s32[1024]{0:T...) while((s32[]{:T(128)}, bf16[6,1024,128]{2,1,0:T(8,128)(2,1)}, ...), condition=%wide.wide.region_28.29_spmd, body=%wide.wide.region_24.28_spmd.sunk | while | flops 543424000 | bytes 34776712 | solution.py:414
  460.9 17.5 %while.120 = (s32[]{:T(128)}, f32[1024,128]{1,0:T(8,128)}, f32[1024,64]{0,1:T(8,128)}, bf16[2,512,128]{2,1,0:T(8,128)(2,1)}, s32[2,512]{1,0:T(2,128)S(1)}, /*ind...) while((s32[]{:T(128)}, f32[1024,128]{1,0:T(8,128)}, ...), condition=%wide.region_27.27_spmd.clone, body=%wide.region_25.26_spmd.clone.sunk | while | flops 542768640 | bytes 22959372 | solution.py:124
  487.6 17.5 %while.120 = (s32[]{:T(128)}, f32[1024,128]{1,0:T(8,128)}, f32[1024,64]{0,1:T(8,128)}, bf16[2,512,128]{2,1,0:T(8,128)(2,1)}, s32[2,512]{1,0:T(2,128)S(1)}, /*ind...) while((s32[]{:T(128)}, f32[1024,128]{1,0:T(8,128)}, ...), condition=%wide.region_27.27_spmd.clone, body=%wide.region_25.26_spmd.clone.sunk | while | flops 542768640 | bytes 22959372 | solution.py:124
  514.4 17.5 %while.120 = (s32[]{:T(128)}, f32[1024,128]{1,0:T(8,128)}, f32[1024,64]{0,1:T(8,128)}, bf16[2,512,128]{2,1,0:T(8,128)(2,1)}, s32[2,512]{1,0:T(2,128)S(1)}, /*ind...) while((s32[]{:T(128)}, f32[1024,128]{1,0:T(8,128)}, ...), condition=%wide.region_27.27_spmd.clone, body=%wide.region_25.26_spmd.clone.sunk | while | flops 542768640 | bytes 22959372 | solution.py:124
  541.2 17.5 %while.120 = (s32[]{:T(128)}, f32[1024,128]{1,0:T(8,128)}, f32[1024,64]{0,1:T(8,128)}, bf16[2,512,128]{2,1,0:T(8,128)(2,1)}, s32[2,512]{1,0:T(2,128)S(1)}, /*ind...) while((s32[]{:T(128)}, f32[1024,128]{1,0:T(8,128)}, ...), condition=%wide.region_27.27_spmd.clone, body=%wide.region_25.26_spmd.clone.sunk | while | flops 542768640 | bytes 22959372 | solution.py:124
  567.9 17.5 %while.120 = (s32[]{:T(128)}, f32[1024,128]{1,0:T(8,128)}, f32[1024,64]{0,1:T(8,128)}, bf16[2,512,128]{2,1,0:T(8,128)(2,1)}, s32[2,512]{1,0:T(2,128)S(1)}, /*ind...) while((s32[]{:T(128)}, f32[1024,128]{1,0:T(8,128)}, ...), condition=%wide.region_27.27_spmd.clone, body=%wide.region_25.26_spmd.clone.sunk | while | flops 542768640 | bytes 22959372 | solution.py:124
  594.6 17.5 %while.120 = (s32[]{:T(128)}, f32[1024,128]{1,0:T(8,128)}, f32[1024,64]{0,1:T(8,128)}, bf16[2,512,128]{2,1,0:T(8,128)(2,1)}, s32[2,512]{1,0:T(2,128)S(1)}, /*ind...) while((s32[]{:T(128)}, f32[1024,128]{1,0:T(8,128)}, ...), condition=%wide.region_27.27_spmd.clone, body=%wide.region_25.26_spmd.clone.sunk | while | flops 542768640 | bytes 22959372 | solution.py:124
  620.0 5.2 all-to-all-start.8
  630.5 139.7 %while.117 = (s32[]{:T(128)}, bf16[6,1024,128]{2,1,0:T(8,128)(2,1)}, bf16[6,1024,128]{1,2,0:T(8,128)(2,1)}, bf16[6,1024,128]{2,1,0:T(8,128)(2,1)}, s32[1024]{0:T...) while((s32[]{:T(128)}, bf16[6,1024,128]{2,1,0:T(8,128)(2,1)}, ...), condition=%wide.wide.region_37.38_spmd, body=%wide.wide.region_33.37_spmd.sunk | while | flops 543424000 | bytes 36873468 | solution.py:414
  634.6 15.5 %while.121 = (s32[]{:T(128)}, f32[1024,128]{1,0:T(8,128)}, f32[1024,64]{0,1:T(8,128)}, bf16[2,512,128]{2,1,0:T(8,128)(2,1)}, s32[2,512]{1,0:T(2,128)S(1)}, /*ind...) while((s32[]{:T(128)}, f32[1024,128]{1,0:T(8,128)}, ...), condition=%wide.region_36.36_spmd.clone, body=%wide.region_34.35_spmd.clone.sunk | while | flops 542768640 | bytes 25056128 | solution.py:124
  657.9 15.5 %while.121 = (s32[]{:T(128)}, f32[1024,128]{1,0:T(8,128)}, f32[1024,64]{0,1:T(8,128)}, bf16[2,512,128]{2,1,0:T(8,128)(2,1)}, s32[2,512]{1,0:T(2,128)S(1)}, /*ind...) while((s32[]{:T(128)}, f32[1024,128]{1,0:T(8,128)}, ...), condition=%wide.region_36.36_spmd.clone, body=%wide.region_34.35_spmd.clone.sunk | while | flops 542768640 | bytes 25056128 | solution.py:124
  681.2 15.5 %while.121 = (s32[]{:T(128)}, f32[1024,128]{1,0:T(8,128)}, f32[1024,64]{0,1:T(8,128)}, bf16[2,512,128]{2,1,0:T(8,128)(2,1)}, s32[2,512]{1,0:T(2,128)S(1)}, /*ind...) while((s32[]{:T(128)}, f32[1024,128]{1,0:T(8,128)}, ...), condition=%wide.region_36.36_spmd.clone, body=%wide.region_34.35_spmd.clone.sunk | while | flops 542768640 | bytes 25056128 | solution.py:124
  704.5 15.5 %while.121 = (s32[]{:T(128)}, f32[1024,128]{1,0:T(8,128)}, f32[1024,64]{0,1:T(8,128)}, bf16[2,512,128]{2,1,0:T(8,128)(2,1)}, s32[2,512]{1,0:T(2,128)S(1)}, /*ind...) while((s32[]{:T(128)}, f32[1024,128]{1,0:T(8,128)}, ...), condition=%wide.region_36.36_spmd.clone, body=%wide.region_34.35_spmd.clone.sunk | while | flops 542768640 | bytes 25056128 | solution.py:124
  727.8 15.5 %while.121 = (s32[]{:T(128)}, f32[1024,128]{1,0:T(8,128)}, f32[1024,64]{0,1:T(8,128)}, bf16[2,512,128]{2,1,0:T(8,128)(2,1)}, s32[2,512]{1,0:T(2,128)S(1)}, /*ind...) while((s32[]{:T(128)}, f32[1024,128]{1,0:T(8,128)}, ...), condition=%wide.region_36.36_spmd.clone, body=%wide.region_34.35_spmd.clone.sunk | while | flops 542768640 | bytes 25056128 | solution.py:124
  751.0 15.5 %while.121 = (s32[]{:T(128)}, f32[1024,128]{1,0:T(8,128)}, f32[1024,64]{0,1:T(8,128)}, bf16[2,512,128]{2,1,0:T(8,128)(2,1)}, s32[2,512]{1,0:T(2,128)S(1)}, /*ind...) while((s32[]{:T(128)}, f32[1024,128]{1,0:T(8,128)}, ...), condition=%wide.region_36.36_spmd.clone, body=%wide.region_34.35_spmd.clone.sunk | while | flops 542768640 | bytes 25056128 | solution.py:124
  774.3 4.8 all-to-all-start.11
  781.1 19.1 %all-to-all-done.11 = bf16[1024,1,6,128]{3,2,1,0:T(8,128)(2,1)} async-done(((bf16[1024,1,6,128]{3,2,1,0:T(8,128)(2,1)}), bf16[1024,1,6,128]{3,2,1,0:T(8,128)(2,1)}, u32[]{:S(2)}, u32[]{:S(2)}) %all-to-all-start.11) | async-done | bytes 1572896 | tf_op jit(solution)/shard_map/all_to_all | solution.py:432
  832.0 5.4 fusion.144
  837.4 5.4 convolution_add_fusion.2
  843.4 5.6 fusion.150
  849.0 5.8 convolution_add_fusion.3
  858.7 4.9 all-to-all-start.10
  867.4 16.1 %all-to-all-done.10 = bf16[1024,1,6,128]{3,2,1,0:T(8,128)(2,1)} async-done(((bf16[1024,1,6,128]{3,2,1,0:T(8,128)(2,1)}), bf16[1024,1,6,128]{3,2,1,0:T(8,128)(2,1)}, u32[]{:S(2)}, u32[]{:S(2)}) %all-to-all-start.10) | async-done | bytes 1572896 | tf_op jit(solution)/shard_map/all_to_all | solution.py:425
  883.5 4.8 all-to-all-start.7
  902.4 5.0 all-to-all-done.7
  928.4 5.8 add_bitcast_fusion
  934.1 9.6 copy.222
  961.9 6.7 fusion.155
  977.4 83.9 %reduce-scatter.17.cloned.1.call-done = f32[192,768]{1,0:T(8,128)} async-done(((f32[3072,768]{1,0:T(8,128)}), f32[192,768]{1,0:T(8,128)}) %reduce-scatter.17.cloned.1.call-update) | async-done | bytes 589840 | tf_op jit(solution)/shard_map/reduce_scatter | solution.py:236
  1063.1 113.2 %reduce-scatter.15.cloned.1.call-done = f32[48,3072]{1,0:T(8,128)} async-done(((f32[768,3072]{1,0:T(8,128)}), f32[48,3072]{1,0:T(8,128)}) %reduce-scatter.15.cloned.1.call-update) | async-done | bytes 589840 | tf_op jit(solution)/shard_map/reduce_scatter | solution.py:234
  1178.0 113.0 %reduce-scatter.19.cloned.1.call-done = f32[48,3072]{1,0:T(8,128)} async-done(((f32[768,3072]{1,0:T(8,128)}), f32[48,3072]{1,0:T(8,128)}) %reduce-scatter.19.cloned.1.call-update) | async-done | bytes 589840
  1296.5 60.8 %all-reduce.20 = (bf16[3072]{0:T(1024)(128)(2,1)S(1)}, bf16[768]{0:T(1024)(128)(2,1)S(1)}, bf16[768]{0:T(1024)(128)(2,1)S(1)}, bf16[768]{0:T(1024)(128)(2,1)S(1)...) all-reduce(f32[3072]{0:T(1024)S(1)} %add.459, ...), channel_id=23, replica_groups=mesh['seq'=2,'shard'=16] {'shard'}, use_global_device_ids=true, to_apply=%region_42.43.clone | all-reduce | flops 12288 | bytes 73728
  1358.0 5.3 all-reduce.22
  (1519 shorter events, 742.1 us)
Async XLA Ops:
  7.2 78.2 %all-gather.13.cloned.1.call-start = ((), (), s32[]{:S(2)}) async-start(), calls=%async_computation.19 | async-start | bytes 1253376 | tf_op jit(solution)/shard_map/all_gather | solution.py:156
  7.9 82.8 %all-gather.15.cloned.1.call-start = ((), (), s32[]{:S(2)}) async-start(), calls=%async_computation.20 | async-start | bytes 1253376 | tf_op jit(solution)/shard_map/all_gather | solution.py:158
  8.7 166.8 %all-gather.11.cloned.1.call-start = ((), (), s32[]{:S(2)}) async-start(), calls=%async_computation.18 | async-start | bytes 5013504 | tf_op jit(solution)/shard_map/all_gather | solution.py:154
  9.4 325.6 %all-gather.17.cloned.1.call-start = ((), (), s32[]{:S(2)}) async-start(), calls=%async_computation.21 | async-start | bytes 1253376 | tf_op jit(solution)/shard_map/all_gather | solution.py:160
  10.0 337.9 %all-gather.19.cloned.1.call-start = ((), (), s32[]{:S(2)}) async-start(), calls=%async_computation.22 | async-start | bytes 5013504 | tf_op jit(solution)/shard_map/all_gather | solution.py:169
  10.6 376.7 %all-gather.21.cloned.1.call-start = ((), (), s32[]{:S(2)}) async-start(), calls=%async_computation.23 | async-start | bytes 5013504 | tf_op jit(solution)/shard_map/all_gather | solution.py:171
  96.4 44.6 %all-to-all-start.1 = ((bf16[512,2,6,128]{0,3,2,1:T(8,128)(2,1)}), bf16[512,2,6,128]{0,3,2,1:T(8,128)(2,1)S(1)}, u32[]{:S(2)}, u32[]{:S(2)}) async-start(bf16[512,2,6,128]{0,3,2,1:T(8,128)(2,1)} %pad_maximum_fusion.3), calls=%async_computation.1 | async-start | bytes 3145728 | tf_op jit(solution)/shard_map/all_to_all | solution.py:341
  141.0 29.7 %all-to-all-start.4 = ((bf16[512,2,6,128]{0,3,2,1:T(8,128)(2,1)}), bf16[512,2,6,128]{0,3,2,1:T(8,128)(2,1)}, u32[]{:S(2)}, u32[]{:S(2)}) async-start(bf16[512,2,6,128]{0,3,2,1:T(8,128)(2,1)} %pad_maximum_fusion.6), calls=%async_computation.4 | async-start | bytes 3145728 | tf_op jit(solution)/shard_map/all_to_all | solution.py:341
  168.6 15.1 %copy-start.111 = (pred[512]{0:T(512)(128)(4,1)}, pred[512]{0:T(512)(128)(4,1)S(1)}, u32[]{:S(2)}) copy-start(pred[512]{0:T(512)(128)(4,1)S(1)} %get-tuple-element.658) | copy-start | bytes 1540
  168.6 15.1 %copy-start.113 = (pred[512]{0:T(512)(128)(4,1)}, pred[512]{0:T(512)(128)(4,1)S(1)}, u32[]{:S(2)}) copy-start(pred[512]{0:T(512)(128)(4,1)S(1)} %get-tuple-element.659) | copy-start | bytes 1540
  190.2 20.0 %all-to-all-start = ((bf16[512,2,6,128]{0,3,2,1:T(8,128)(2,1)}), bf16[512,2,6,128]{0,3,2,1:T(8,128)(2,1)S(1)}, u32[]{:S(2)}, u32[]{:S(2)}) async-start(bf16[512,2,6,128]{0,3,2,1:T(8,128)(2,1)} %pad_maximum_fusion.2), calls=%async_computation | async-start | bytes 3145728 | tf_op jit(solution)/shard_map/all_to_all | solution.py:340
  210.2 57.1 %all-to-all-start.3 = ((bf16[512,2,6,128]{0,3,2,1:T(8,128)(2,1)}), bf16[512,2,6,128]{0,3,2,1:T(8,128)(2,1)}, u32[]{:S(2)}, u32[]{:S(2)}) async-start(bf16[512,2,6,128]{0,3,2,1:T(8,128)(2,1)} %pad_maximum_fusion.5), calls=%async_computation.3 | async-start | bytes 3145728 | tf_op jit(solution)/shard_map/all_to_all | solution.py:340
  267.2 57.3 %all-to-all-start.2 = ((bf16[2,2,98304]{2,1,0:T(2,128)(2,1)}), bf16[2,2,98304]{2,1,0:T(2,128)(2,1)}, u32[]{:S(2)}, u32[]{:S(2)}) async-start(bf16[2,2,98304]{2,1,0:T(2,128)(2,1)} %reshape.470), calls=%async_computation.2 | async-start | bytes 1572864 | tf_op jit(solution)/shard_map/all_to_all | solution.py:352
  324.5 14.4 %all-to-all-start.5 = ((bf16[2,2,98304]{2,1,0:T(2,128)(2,1)}), bf16[2,2,98304]{2,1,0:T(2,128)(2,1)}, u32[]{:S(2)}, u32[]{:S(2)}) async-start(bf16[2,2,98304]{2,1,0:T(2,128)(2,1)} %reshape.472), calls=%async_computation.5 | async-start | bytes 1572864 | tf_op jit(solution)/shard_map/all_to_all | solution.py:352
  337.5 84.0 %copy-start.109 = (f32[512]{0:T(512)}, f32[512]{0:T(512)S(1)}, u32[]{:S(2)}) copy-start(f32[512]{0:T(512)S(1)} %broadcast_multiply_fusion.11) | copy-start | bytes 6148
  338.9 82.5 %copy-start.123 = (f32[512]{0:T(512)}, f32[512]{0:T(512)S(1)}, u32[]{:S(2)}) copy-start(f32[512]{0:T(512)S(1)} %add_rsqrt_fusion.3) | copy-start | bytes 6148
  347.5 89.7 %copy-start.8 = (f32[512,768]{1,0:T(8,128)}, f32[512,768]{1,0:T(8,128)S(1)}, u32[]{:S(2)}) copy-start(f32[512,768]{1,0:T(8,128)S(1)} %get-tuple-element.910) | copy-start | bytes 4718596
  347.5 89.7 %copy-start.93 = (f32[512]{0:T(512)}, f32[512]{0:T(512)S(1)}, u32[]{:S(2)}) copy-start(f32[512]{0:T(512)S(1)} %broadcast_multiply_fusion.9) | copy-start | bytes 6148
  347.8 89.4 %copy-start.96 = (f32[512]{0:T(512)}, f32[512]{0:T(512)S(1)}, u32[]{:S(2)}) copy-start(f32[512]{0:T(512)S(1)} %add_rsqrt_fusion.1) | copy-start | bytes 6148
  347.8 7.6 copy-start.106
  347.9 7.6 copy-start.75
  347.9 7.5 copy-start.126
  355.5 31.8 %copy-start.120 = (f32[768]{0:T(1024)S(1)}, f32[768]{0:T(1024)}, u32[]{:S(2)}) copy-start(f32[768]{0:T(1024)} %convert_element_type.296) | copy-start | bytes 9220
  387.3 6.5 copy-start.37
  400.2 11.2 slice-start.2
  400.3 15.9 %slice-start.4 = ((s8[6291456]{0:T(1024)(128)(4,1)}), s8[4194304]{0:T(1024)(128)(4,1)S(1)}, s32[]{:S(2)}) async-start(s8[6291456]{0:T(1024)(128)(4,1)} %bitcast.601), calls=%async_computation.35 | async-start | bytes 8388608
  403.2 8.2 copy-start.25
  403.2 18.2 %copy-start.23 = (f32[512,768]{1,0:T(8,128)}, f32[512,768]{1,0:T(8,128)S(1)}, u32[]{:S(2)}) copy-start(f32[512,768]{1,0:T(8,128)S(1)} %get-tuple-element.841) | copy-start | bytes 4718596
  403.2 8.2 slice-start.3
  403.2 12.9 slice-start.5
  421.4 7.2 copy-start.38
  432.8 12.9 all-to-all-start.6
  437.1 535.2 %reduce-scatter.13.cloned.1.call-start = ((), (), s32[]{:S(2)}) async-start(), calls=%async_computation.24 | async-start | bytes 2506752 | tf_op jit(solution)/shard_map/reduce_scatter | solution.py:225
  445.7 174.2 %all-to-all-start.9 = ((bf16[512,2,6,64]{0,3,2,1:T(8,128)(2,1)}), bf16[512,2,6,64]{0,3,2,1:T(8,128)(2,1)}, u32[]{:S(2)}, u32[]{:S(2)}) async-start(bf16[512,2,6,64]{0,3,2,1:T(8,128)(2,1)} %bitcast.100), calls=%async_computation.9 | async-start | bytes 1572864 | tf_op jit(solution)/shard_map/all_to_all | solution.py:410
  620.0 154.3 %all-to-all-start.8 = ((bf16[1024,1,6,128]{3,2,1,0:T(8,128)(2,1)}), bf16[1024,1,6,128]{3,2,1,0:T(8,128)(2,1)}, u32[]{:S(2)}, u32[]{:S(2)}) async-start(bf16[1024,1,6,128]{3,2,1,0:T(8,128)(2,1)} %bitcast.91), calls=%async_computation.8 | async-start | bytes 4194304 | tf_op jit(solution)/shard_map/all_to_all | solution.py:432
  774.3 25.9 %all-to-all-start.11 = ((bf16[1024,1,6,128]{3,2,1,0:T(8,128)(2,1)}), bf16[1024,1,6,128]{3,2,1,0:T(8,128)(2,1)}, u32[]{:S(2)}, u32[]{:S(2)}) async-start(bf16[1024,1,6,128]{3,2,1,0:T(8,128)(2,1)} %bitcast.113), calls=%async_computation.11 | async-start | bytes 4194304 | tf_op jit(solution)/shard_map/all_to_all | solution.py:432
  779.1 194.8 %reduce-scatter.23.cloned.1.call-start = ((), (), s32[]{:S(2)}) async-start(), calls=%async_computation.29 | async-start | bytes 2506752
  819.1 156.6 %reduce-scatter.21.cloned.1.call-start = ((), (), s32[]{:S(2)}) async-start(), calls=%async_computation.28 | async-start | bytes 2506752
  831.7 229.5 %reduce-scatter.17.cloned.1.call-start = ((), (), s32[]{:S(2)}) async-start(), calls=%async_computation.26 | async-start | bytes 10027008 | tf_op jit(solution)/shard_map/reduce_scatter | solution.py:236
  842.8 333.4 %reduce-scatter.15.cloned.1.call-start = ((), (), s32[]{:S(2)}) async-start(), calls=%async_computation.25 | async-start | bytes 10027008 | tf_op jit(solution)/shard_map/reduce_scatter | solution.py:234
  858.7 24.8 %all-to-all-start.10 = ((bf16[1024,1,6,128]{3,2,1,0:T(8,128)(2,1)}), bf16[1024,1,6,128]{3,2,1,0:T(8,128)(2,1)}, u32[]{:S(2)}, u32[]{:S(2)}) async-start(bf16[1024,1,6,128]{3,2,1,0:T(8,128)(2,1)} %bitcast.536), calls=%async_computation.10 | async-start | bytes 4194304 | tf_op jit(solution)/shard_map/all_to_all | solution.py:425
  883.5 23.9 %all-to-all-start.7 = ((bf16[1024,1,6,128]{3,2,1,0:T(8,128)(2,1)}), bf16[1024,1,6,128]{3,2,1,0:T(8,128)(2,1)}, u32[]{:S(2)}, u32[]{:S(2)}) async-start(bf16[1024,1,6,128]{3,2,1,0:T(8,128)(2,1)} %bitcast.535), calls=%async_computation.7 | async-start | bytes 4194304 | tf_op jit(solution)/shard_map/all_to_all | solution.py:425
  888.3 402.7 %reduce-scatter.19.cloned.1.call-start = ((), (), s32[]{:S(2)}) async-start(), calls=%async_computation.27 | async-start | bytes 10027008
  943.8 431.4 %all-reduce.26.cloned.1.call-start = ((), (), s32[]{:S(2)}) async-start(), calls=%async_computation.30 | async-start | bytes 3686400 | tf_op jit(solution)/shard_map/psum | solution.py:490
  957.9 10.7 slice-start
  961.9 6.7 slice-start.1
  1293.4 75.1 %copy-start.16 = (bf16[512,12,64]{0,2,1:T(8,128)(2,1)S(1)}, bf16[512,12,64]{0,2,1:T(8,128)(2,1)}, u32[]{:S(2)}) copy-start(bf16[512,12,64]{0,2,1:T(8,128)(2,1)} %copy.196) | copy-start | bytes 2359300
  1293.4 75.1 %copy-start.32 = (bf16[768,768]{1,0:T(8,128)(2,1)S(1)}, bf16[768,768]{1,0:T(8,128)(2,1)}, u32[]{:S(2)}) copy-start(bf16[768,768]{1,0:T(8,128)(2,1)} %all-gather.15.cloned.1.call-done) | copy-start | bytes 3538948
  (278 other events, 726.3 us)
Sparse Core Ops, SparseCore 0:
  10.3 41.1 all-gather.12
  53.7 36.9 all-gather.14
  93.0 51.9 all-gather.10
  147.2 36.7 all-gather.16
  186.1 51.9 all-gather.18
  240.3 51.5 all-gather.20
  445.9 62.6 reduce-scatter.12
  819.2 61.7 reduce-scatter.22
  884.8 62.1 reduce-scatter.20
  951.0 110.2 reduce-scatter.16
  1065.4 110.8 reduce-scatter.14
  1180.2 110.8 reduce-scatter.18
  1294.9 57.1 all-reduce.25
where the time goes:
time: 1400 us; the launch traced here: 1390 us
  waiting for transfers between devices  360 us (26%)
  matrix products  360 us (26%)
  local copies, waits for them, and re-layouts  309 us (22%)
  blocking collectives  176 us (13%)
  other arithmetic  104 us (7%)
  starting transfers between devices  55.8 us (4%)
  between operations  18.6 us (1%)
    dot_general x60, matrix products, inner_rows(): lax.dot_general(left_side, right_side, (((0,), (0,)), ((), ())), preferre...  139 us
    unnamed x2, blocking collectives  124 us
    unnamed x16, waiting for transfers between devices  117 us
    reduce_scatter x1, waiting for transfers between devices, scatter_feed(): lax.psum_scatter(grad_uw, 'shard', scatter_dimension=0, tiled=True)  113 us
    dot_general x84, matrix products, against(): lax.dot_general(left_side, right_side, (((1,), (1,)), ((), ())), preferre...  102 us
    reduce_scatter x1, waiting for transfers between devices, scatter_feed(): lax.psum_scatter(grad_dw, 'shard', scatter_dimension=0, tiled=True)  83.9 us
    unnamed x286, local copies, waits for them, and re-layouts  55 us
    squeeze x48, local copies, waits for them, and re-layouts, on_device(): lax.map(lambda pieces: head_forward(pieces, seq_groups, row_block, score_...  51 us
  transfers between devices with their start and end apart: 25, of which 8 were waited for; matrix products, arithmetic and copies ran while one was open for 50% of the time, Pallas kernels for 0%

commit v1 on v0

v1 whole, which is shorter than its diff:
```python
import functools

import jax
import jax.numpy as jnp
from jax import lax
from jax.experimental import pallas as pl
from jax.experimental.pallas import tpu as pltpu
from jax.sharding import PartitionSpec as P

HEADS = 12
GROUPS = 16
BLOCK = 256
masked_score = -1e30
layer_eps = 1e-12
bf16 = jnp.bfloat16
f32 = jnp.float32
VMEM_LIMIT = 60 * 1024 * 1024


def nn(a, b):
    return lax.dot_general(a, b, (((1,), (0,)), ((), ())), preferred_element_type=f32)


def nt(a, b):
    return lax.dot_general(a, b, (((1,), (1,)), ((), ())), preferred_element_type=f32)


def tn(a, b):
    return lax.dot_general(a, b, (((0,), (0,)), ((), ())), preferred_element_type=f32)


def swap(value):
    return lax.ppermute(value, "seq", [(0, 1), (1, 0)])


def cost(flops, moved, trans=0):
    return pl.CostEstimate(flops=flops, bytes_accessed=moved, transcendentals=trans)


def low_lanes(shape):
    return lax.broadcasted_iota(jnp.int32, shape, len(shape) - 1) % 128 < 64


def pack_kernel(side_ref, q_ref, k_ref, v_ref, vec_ref, out_ref):
    rows, width = k_ref.shape
    half = width // 2
    first = side_ref[0] == 0

    def own(ref, base):
        return jnp.where(
            first,
            ref[:, base : base + half].astype(f32),
            ref[:, base + half : base + width].astype(f32),
        )

    lo = low_lanes((rows, 128))
    for e in range(2):
        word = own(q_ref, 2 * e * width)
        entity = own(q_ref, (2 * e + 1) * width)
        for t in range(half // 128):
            a = word[:, 128 * t : 128 * t + 128]
            b = entity[:, 128 * t : 128 * t + 128]
            even = jnp.where(lo, a, pltpu.roll(b, 64, 1))
            odd = jnp.where(lo, pltpu.roll(a, 64, 1), b)
            out_ref[e * rows : e * rows + rows, 256 * t : 256 * t + 128] = even.astype(bf16)
            out_ref[e * rows : e * rows + rows, 256 * t + 128 : 256 * t + 256] = odd.astype(bf16)
    out_ref[2 * rows : 3 * rows, :half] = own(k_ref, 0).astype(bf16)
    out_ref[2 * rows : 3 * rows, half:] = own(v_ref, 0).astype(bf16)
    out_ref[3 * rows :, :] = jnp.broadcast_to(vec_ref[...], (16, width))


def pair_columns(columns, side, head_dim):
    lead = columns.shape[:-1]
    per = columns.shape[-1] // (8 * head_dim)
    view = columns.reshape(lead + (2, 2, 2, per, head_dim))
    view = jnp.where(side == 0, view[..., 0, :, :], view[..., 1, :, :])
    return jnp.swapaxes(view, -3, -2).reshape(lead + (2, -1))


def unpair_columns(pairs, head_dim):
    lead = pairs.shape[:-2]
    per = pairs.shape[-1] // (2 * head_dim)
    view = pairs.reshape(lead + (2, per, 2, head_dim))
    return jnp.swapaxes(view, -3, -2).reshape(lead + (2, 2, per * head_dim))


def own_half(columns, side):
    half = columns.shape[-1] // 2
    return jnp.where(side == 0, columns[..., :half], columns[..., half:])


def pack_attention(query_weight, key_weight, value_weight, vector, side, head_dim):
    rows, width = key_weight.shape
    if rows % 16 == 0:
        return pl.pallas_call(
            pack_kernel,
            out_shape=jax.ShapeDtypeStruct((3 * rows + 16, width), bf16),
            in_specs=[pl.BlockSpec(memory_space=pltpu.SMEM)]
            + [pl.BlockSpec(memory_space=pltpu.VMEM)] * 4,
            out_specs=pl.BlockSpec(memory_space=pltpu.VMEM),
            name="pack",
        )(side[None], query_weight, key_weight, value_weight, vector)
    pairs = pair_columns(query_weight, side, head_dim)
    key_value = jnp.concatenate([own_half(key_weight, side), own_half(value_weight, side)], axis=1)
    return jnp.concatenate(
        [pairs[:, 0], pairs[:, 1], key_value, jnp.broadcast_to(vector, (16, width))], axis=0
    )


def regroup(gathered, sizes):
    devices, _, width = gathered.shape
    pieces = []
    start = 0
    for size in sizes:
        piece = gathered[:, start : start + size].reshape(GROUPS, -1, width)
        pieces.append(piece)
        start += size
    return jnp.concatenate(pieces, axis=1)


def ungroup(grouped, sizes, devices):
    _, _, width = grouped.shape
    pieces = []
    start = 0
    for size in sizes:
        wide = size * devices // GROUPS
        pieces.append(grouped[:, start : start + wide].reshape(devices, size, width))
        start += wide
    return jnp.concatenate(pieces, axis=1)


def project_kernel(x_ref, w_ref, bias_ref, kind_ref, qp_ref, km_ref, kmt_ref, v_ref, vt_ref):
    width = x_ref.shape[1]
    half = width // 2
    rows = width // GROUPS
    x = x_ref[...]
    kind = kind_ref[...]
    wa = w_ref[:, 0:rows, :].reshape(width, width)
    wb = w_ref[:, rows : 2 * rows, :].reshape(width, width)
    wkv = w_ref[:, 2 * rows : 3 * rows, :].reshape(width, width)
    qa = nn(x, wa) + bias_ref[0:1, :]
    qb = nn(x, wb) + bias_ref[1:2, :]
    qp_ref[...] = (jnp.where(kind == 1, qb, qa) * 0.125).astype(bf16)
    kv = nn(x, wkv) + bias_ref[2:3, :]
    lane_high = (lax.broadcasted_iota(jnp.int32, (BLOCK, 128), 1) >= 64).astype(jnp.int32)
    keep = lane_high == kind
    lo = lane_high == 0
    for t in range(half // 128):
        k = kv[:, 128 * t : 128 * t + 128]
        r = pltpu.roll(k, 64, 1)
        even = jnp.where(keep, jnp.where(lo, k, r), 0.0)
        odd = jnp.where(keep, jnp.where(lo, r, k), 0.0)
        km_ref[:, 256 * t : 256 * t + 128] = even.astype(bf16)
        km_ref[:, 256 * t + 128 : 256 * t + 256] = odd.astype(bf16)
        kmt_ref[256 * t : 256 * t + 128, :] = even.T.astype(bf16)
        kmt_ref[256 * t + 128 : 256 * t + 256, :] = odd.T.astype(bf16)
    v = kv[:, half:]
    v_ref[...] = v.astype(bf16)
    vt_ref[...] = v.T.astype(bf16)


def project(xs, weights, bias_rows, kind_col):
    halves, micro, local, width = xs.shape
    half = width // 2
    sub = local // BLOCK

    def rows_spec(cols):
        return pl.BlockSpec((None, None, BLOCK, cols), lambda a, m, i: (a, m, i, 0))

    def cols_spec(count):
        return pl.BlockSpec((None, None, count, BLOCK), lambda a, m, i: (a, m, 0, i))

    def shape(*dims):
        return jax.ShapeDtypeStruct((halves, micro) + dims, bf16)

    tokens = halves * micro * local
    return pl.pallas_call(
        project_kernel,
        grid=(halves, micro, sub),
        in_specs=[
            rows_spec(width),
            pl.BlockSpec(weights.shape, lambda a, m, i: (0, 0, 0)),
            pl.BlockSpec(bias_rows.shape, lambda a, m, i: (0, 0)),
            rows_spec(1),
        ],
        out_specs=[rows_spec(width), rows_spec(width), cols_spec(width), rows_spec(half), cols_spec(half)],
        out_shape=[
            shape(local, width),
            shape(local, width),
            shape(width, local),
            shape(local, half),
            shape(half, local),
        ],
        compiler_params=pltpu.CompilerParams(vmem_limit_bytes=VMEM_LIMIT),
        cost_estimate=cost(2 * tokens * width * 3 * width, tokens * width * 10),
        name="project",
    )(xs, weights, bias_rows, kind_col)


def place(block, per):
    return block // per, pl.multiple_of(lax.rem(block, per) * BLOCK, BLOCK)


def attend_kernel(
    low_ref, high_ref, qp_ref, km_ref, vt_ref, gk_ref, gq_ref, c_ref, ct_ref, lse_ref, m_sc, l_sc, acc_sc
):
    micro_at = pl.program_id(0)
    local = qp_ref.shape[1]
    per = local // BLOCK
    blocks = 2 * per
    heads = qp_ref.shape[2] // 128
    base = micro_at * blocks

    @pl.loop(0, blocks)
    def _(qb):
        qh, qo = place(qb, per)
        m_sc[...] = jnp.full_like(m_sc, masked_score)
        l_sc[...] = jnp.zeros_like(l_sc)
        acc_sc[...] = jnp.zeros_like(acc_sc)
        q_low, q_high = low_ref[base + qb], high_ref[base + qb]

        @pl.loop(0, blocks)
        def _(kb):
            @pl.when((q_low <= high_ref[base + kb]) & (low_ref[base + kb] <= q_high))
            def _():
                kh, ko = place(kb, per)
                same = gk_ref[kh, pl.ds(ko, BLOCK), :] == gq_ref[qh, :, pl.ds(qo, BLOCK)]
                bias = jnp.where(same, 0.0, masked_score)
                for h in range(heads):
                    at = slice(128 * h, 128 * h + 128)
                    vat = slice(64 * h, 64 * h + 64)
                    s = nt(km_ref[kh, pl.ds(ko, BLOCK), at], qp_ref[qh, pl.ds(qo, BLOCK), at]) + bias
                    m_old = m_sc[h : h + 1, :]
                    m_new = jnp.maximum(m_old, jnp.max(s, axis=0, keepdims=True))
                    alpha = jnp.exp(m_old - m_new)
                    p = jnp.exp(s - m_new)
                    m_sc[h : h + 1, :] = m_new
                    l_sc[h : h + 1, :] = alpha * l_sc[h : h + 1, :] + jnp.sum(p, axis=0, keepdims=True)
                    acc_sc[vat, :] = alpha * acc_sc[vat, :] + nn(
                        vt_ref[kh, vat, pl.ds(ko, BLOCK)], p.astype(bf16)
                    )

        cols = pl.ds(pl.multiple_of(qb * BLOCK, BLOCK), BLOCK)
        for h in range(heads):
            vat = slice(64 * h, 64 * h + 64)
            total = l_sc[h : h + 1, :]
            ct_ref[vat, cols] = acc_sc[vat, :] / total
            lse_ref[h : h + 1, cols] = m_sc[h : h + 1, :] + jnp.log(total)
        c_ref[qh, pl.ds(qo, BLOCK), :] = ct_ref[:, cols].T.astype(bf16)


def whole_micro(array):
    rest = array.shape[2:]
    return pl.BlockSpec((array.shape[0], None) + rest, lambda m, *_: (0, m) + (0,) * len(rest))


def attend(low, high, qp, km, vt, gk, gq):
    halves, micro, local, width = qp.shape
    half = width // 2
    heads = width // 128
    length = halves * local
    return pl.pallas_call(
        attend_kernel,
        grid_spec=pltpu.PrefetchScalarGridSpec(
            num_scalar_prefetch=2,
            grid=(micro,),
            in_specs=[whole_micro(a) for a in (qp, km, vt, gk, gq)],
            out_specs=[
                pl.BlockSpec((halves, None, local, half), lambda m, *_: (0, m, 0, 0)),
                pl.BlockSpec((None, half, length), lambda m, *_: (m, 0, 0)),
                pl.BlockSpec((None, 8, length), lambda m, *_: (m, 0, 0)),
            ],
            scratch_shapes=[
                pltpu.VMEM((8, BLOCK), f32),
                pltpu.VMEM((8, BLOCK), f32),
                pltpu.VMEM((half, BLOCK), f32),
            ],
        ),
        out_shape=[
            jax.ShapeDtypeStruct((halves, micro, local, half), bf16),
            jax.ShapeDtypeStruct((micro, half, length), f32),
            jax.ShapeDtypeStruct((micro, 8, length), f32),
        ],
        compiler_params=pltpu.CompilerParams(vmem_limit_bytes=VMEM_LIMIT),
        cost_estimate=cost(
            micro * heads * length * length * 512, micro * length * width * 8, micro * heads * length * length
        ),
        name="attend",
    )(low, high, qp, km, vt, gk, gq)


def attend_back_kernel(
    low_ref,
    high_ref,
    qp_ref,
    km_ref,
    kmt_ref,
    v_ref,
    dc_ref,
    ct_ref,
    lse_ref,
    gk_ref,
    gq_ref,
    kind_ref,
    d_ref,
    db_ref,
    dqt_sc,
    dk_sc,
    dv_sc,
    delta_sc,
):
    micro_at = pl.program_id(0)
    local, width = qp_ref.shape[1], qp_ref.shape[2]
    half = width // 2
    per = local // BLOCK
    blocks = 2 * per
    tiles = half // 128
    base = micro_at * blocks
    dk_sc[...] = jnp.zeros_like(dk_sc)
    dv_sc[...] = jnp.zeros_like(dv_sc)

    @pl.when(micro_at == 0)
    def _():
        db_ref[...] = jnp.zeros_like(db_ref)

    lo = low_lanes((BLOCK, 128))

    @pl.loop(0, blocks)
    def _(qb):
        qh, qo = place(qb, per)
        qrows = pl.ds(qo, BLOCK)
        cols = pl.ds(pl.multiple_of(qb * BLOCK, BLOCK), BLOCK)
        dct = dc_ref[qh, qrows, :].astype(f32).T
        inner = dct * ct_ref[:, cols]
        for h in range(2 * tiles):
            delta_sc[h : h + 1, :] = jnp.sum(inner[64 * h : 64 * h + 64, :], axis=0, keepdims=True)
        dqt_sc[...] = jnp.zeros_like(dqt_sc)
        q_low, q_high = low_ref[base + qb], high_ref[base + qb]

        @pl.loop(0, blocks)
        def _(kb):
            @pl.when((q_low <= high_ref[base + kb]) & (low_ref[base + kb] <= q_high))
            def _():
                kh, ko = place(kb, per)
                krows = pl.ds(ko, BLOCK)
                drows = pl.ds(pl.multiple_of(kb * BLOCK, BLOCK), BLOCK)
                same = gk_ref[kh, krows, :] == gq_ref[qh, :, qrows]
                bias = jnp.where(same, 0.0, masked_score)
                for t in range(tiles):
                    tat = slice(128 * t, 128 * t + 128)
                    v = v_ref[kh, krows, tat]
                    dc = dc_ref[qh, qrows, tat]
                    from_pair = []
                    for side in range(2):
                        h = 2 * t + side
                        at = slice(128 * h, 128 * h + 128)
                        q = qp_ref[qh, qrows, at]
                        s = nt(km_ref[kh, krows, at], q) + bias
                        p = jnp.exp(s - lse_ref[h : h + 1, cols])
                        zero = jnp.zeros_like(v)
                        vm = jnp.where(lo, v, zero) if side == 0 else jnp.where(lo, zero, v)
                        dp = nt(vm, dc)
                        ds = (p * (dp - delta_sc[h : h + 1, :])).astype(bf16)
                        dk_sc[drows, at] += nn(ds, q)
                        dqt_sc[at, :] += nn(kmt_ref[kh, at, krows], ds)
                        from_pair.append(nn(p.astype(bf16), dc))
                    dv_sc[drows, tat] += jnp.where(lo, from_pair[0], from_pair[1])

        dq = dqt_sc[...].T * 0.125
        entity = kind_ref[qh, qrows, :] == 1
        d_ref[qh, qrows, 0:width] = jnp.where(entity, 0.0, dq).astype(bf16)
        d_ref[qh, qrows, width : 2 * width] = jnp.where(entity, dq, 0.0).astype(bf16)

    @pl.loop(0, blocks)
    def _(kb):
        kh, ko = place(kb, per)
        krows = pl.ds(ko, BLOCK)
        drows = pl.ds(pl.multiple_of(kb * BLOCK, BLOCK), BLOCK)
        entity = kind_ref[kh, krows, :] == 1
        for t in range(tiles):
            even = dk_sc[drows, 256 * t : 256 * t + 128]
            odd = dk_sc[drows, 256 * t + 128 : 256 * t + 256]
            left = jnp.where(entity, pltpu.roll(even, 64, 1), even)
            right = jnp.where(entity, odd, pltpu.roll(odd, 64, 1))
            d_ref[kh, krows, 2 * width + 128 * t : 2 * width + 128 * t + 128] = jnp.where(
                lo, left, right
            ).astype(bf16)
        d_ref[kh, krows, 2 * width + half : 3 * width] = dv_sc[drows, :].astype(bf16)
        db_ref[0:1, :] += jnp.sum(d_ref[kh, krows, :].astype(f32), axis=0, keepdims=True)


def attend_back(low, high, qp, km, kmt, v, dc, ct, lse, gk, gq, kind_col):
    halves, micro, local, width = qp.shape
    half = width // 2
    heads = width // 128
    length = halves * local
    return pl.pallas_call(
        attend_back_kernel,
        grid_spec=pltpu.PrefetchScalarGridSpec(
            num_scalar_prefetch=2,
            grid=(micro,),
            in_specs=[whole_micro(a) for a in (qp, km, kmt, v, dc)]
            + [
                pl.BlockSpec((None, half, length), lambda m, *_: (m, 0, 0)),
                pl.BlockSpec((None, 8, length), lambda m, *_: (m, 0, 0)),
            ]
            + [whole_micro(a) for a in (gk, gq, kind_col)],
            out_specs=[
                pl.BlockSpec((halves, None, local, 3 * width), lambda m, *_: (0, m, 0, 0)),
                pl.BlockSpec((8, 3 * width), lambda m, *_: (0, 0)),
            ],
            scratch_shapes=[
                pltpu.VMEM((width, BLOCK), f32),
                pltpu.VMEM((length, width), f32),
                pltpu.VMEM((length, half), f32),
                pltpu.VMEM((8, BLOCK), f32),
            ],
        ),
        out_shape=[
            jax.ShapeDtypeStruct((halves, micro, local, 3 * width), bf16),
            jax.ShapeDtypeStruct((8, 3 * width), f32),
        ],
        compiler_params=pltpu.CompilerParams(vmem_limit_bytes=VMEM_LIMIT),
        cost_estimate=cost(
            micro * heads * length * length * 1280, micro * length * width * 16, micro * heads * length * length
        ),
        name="attend_back",
    )(low, high, qp, km, kmt, v, dc, ct, lse, gk, gq, kind_col)


def norm_forward(hidden):
    center = hidden - jnp.mean(hidden, axis=-1, keepdims=True)
    rescale = lax.rsqrt(jnp.mean(center * center, axis=-1, keepdims=True) + layer_eps)
    return center * rescale, rescale


def norm_backward(upstream, normed, rescale, gain):
    scaled = upstream * gain
    return rescale * (
        scaled
        - jnp.mean(scaled, axis=-1, keepdims=True)
        - normed * jnp.mean(scaled * normed, axis=-1, keepdims=True)
    )


def column_sum(values):
    return jnp.sum(values.astype(f32), axis=0, keepdims=True)


def chain_kernel(
    side_ref,
    x_ref,
    own_ref,
    other_ref,
    cot_ref,
    w_ref,
    vec_ref,
    mixed_ref,
    dh_ref,
    left_ref,
    right_ref,
    dco_ref,
    dcx_ref,
    sums_ref,
    slope_sc,
    z_sc,
):
    width = x_ref.shape[1]
    half = width // 2
    rows = width // GROUPS
    chunks = 4
    first = side_ref[0] == 0

    @pl.when(pl.program_id(0) == 0)
    def _():
        sums_ref[...] = jnp.zeros_like(sums_ref)

    def vector(at):
        return vec_ref[at : at + 1, :]

    def up_chunk(j):
        at = pl.multiple_of(5 * rows + j * rows, 16)
        return w_ref[:, pl.ds(at, rows), :].reshape(width, width)

    def down_chunk(j):
        return w_ref[pl.ds(j * (GROUPS // chunks), GROUPS // chunks), 0 : 4 * rows, :].reshape(width, width)

    def out_weight():
        return w_ref[:, 4 * rows : 5 * rows, :].reshape(width, width)

    own = own_ref[...].astype(f32)
    other = other_ref[...].astype(f32)
    context = jnp.concatenate(
        [jnp.where(first, own, other), jnp.where(first, other, own)], axis=1
    ).astype(bf16)
    left_ref[:, 0:width] = context
    hidden = x_ref[...].astype(f32) + (nn(context, out_weight()) + vector(0))
    n1, r1 = norm_forward(hidden)
    y1 = n1 * vector(1) + vector(2)
    left_ref[:, width : 2 * width] = y1.astype(bf16)
    z_sc[...] = y1 + vector(7)

    @pl.loop(0, chunks)
    def _(j):
        u = nn(left_ref[:, width : 2 * width], up_chunk(j)) + vec_ref[pl.ds(j + 3, 1), :]
        cumulative = 0.5 * (1.0 + lax.erf(u * 0.7071067811865476))
        at = pl.multiple_of(j * width, 128)
        slope_sc[:, pl.ds(at, width)] = (
            cumulative + u * jnp.exp(-0.5 * u * u) * 0.3989422804014327
        )
        g = (u * cumulative).astype(bf16)
        left_ref[:, pl.ds(pl.multiple_of(at + 2 * width, 128), width)] = g
        z_sc[...] += nn(g, down_chunk(j))

    n2, r2 = norm_forward(z_sc[...])
    mixed_ref[...] = (n2 * vector(8) + vector(9)).astype(bf16)
    upstream = cot_ref[...].astype(f32)
    sums_ref[0:1, :] += column_sum(upstream * n2)
    sums_ref[1:2, :] += column_sum(upstream)
    dh2 = norm_backward(upstream, n2, r2, vector(8))
    dz = dh2.astype(bf16)
    right_ref[:, 5 * width :] = dz
    sums_ref[2:3, :] += column_sum(dz)
    z_sc[...] = dh2

    @pl.loop(0, chunks)
    def _(j):
        at = pl.multiple_of(j * width, 128)
        du = (
            nt(right_ref[:, 5 * width :], down_chunk(j)) * slope_sc[:, pl.ds(at, width)]
        ).astype(bf16)
        right_ref[:, pl.ds(pl.multiple_of(at + width, 128), width)] = du
        sums_ref[pl.ds(j + 8, 1), :] += column_sum(du)
        z_sc[...] += nt(du, up_chunk(j))

    dy1 = z_sc[...]
    hidden = x_ref[...].astype(f32) + (nn(left_ref[:, 0:width], out_weight()) + vector(0))
    n1, r1 = norm_forward(hidden)
    sums_ref[3:4, :] += column_sum(dy1 * n1)
    sums_ref[4:5, :] += column_sum(dy1)
    dh1 = norm_backward(dy1, n1, r1, vector(1))
    dh_ref[...] = dh1
    da = dh1.astype(bf16)
    right_ref[:, 0:width] = da
    sums_ref[5:6, :] += column_sum(da)
    dc = nt(da, out_weight())
    dco_ref[...] = jnp.where(first, dc[:, :half], dc[:, half:]).astype(bf16)
    dcx_ref[...] = jnp.where(first, dc[:, half:], dc[:, :half]).astype(bf16)


def chain(side, x, c_own, c_other, cot, weights, vectors):
    tokens, width = x.shape
    half = width // 2

    def rows_spec(cols):
        return pl.BlockSpec((BLOCK, cols), lambda i, *_: (i, 0))

    def shape(cols, kind):
        return jax.ShapeDtypeStruct((tokens, cols), kind)

    return pl.pallas_call(
        chain_kernel,
        grid_spec=pltpu.PrefetchScalarGridSpec(
            num_scalar_prefetch=1,
            grid=(tokens // BLOCK,),
            in_specs=[
                rows_spec(width),
                rows_spec(half),
                rows_spec(half),
                rows_spec(width),
                pl.BlockSpec(weights.shape, lambda i, *_: (0, 0, 0), pipeline_mode=pl.Buffered(1)),
                pl.BlockSpec(vectors.shape, lambda i, *_: (0, 0)),
            ],
            out_specs=[
                rows_spec(width),
                rows_spec(width),
                rows_spec(6 * width),
                rows_spec(6 * width),
                rows_spec(half),
                rows_spec(half),
                pl.BlockSpec((16, width), lambda i, *_: (0, 0)),
            ],
            scratch_shapes=[pltpu.VMEM((BLOCK, 4 * width), f32), pltpu.VMEM((BLOCK, width), f32)],
        ),
        out_shape=[
            shape(width, bf16),
            shape(width, f32),
            shape(6 * width, bf16),
            shape(6 * width, bf16),
            shape(half, bf16),
            shape(half, bf16),
            jax.ShapeDtypeStruct((16, width), f32),
        ],
        compiler_params=pltpu.CompilerParams(vmem_limit_bytes=VMEM_LIMIT),
        cost_estimate=cost(2 * tokens * width * width * 19, tokens * width * 36 + weights.size * 2),
        name="chain",
    )(side[None], x, c_own, c_other, cot, weights, vectors)


def feed_grad_kernel(l_ref, r_ref, out_ref):
    width = l_ref.shape[1]
    rows = width // GROUPS
    at = pl.program_id(0)
    grad = tn(l_ref[...], r_ref[...]).astype(bf16)

    @pl.when(at == 0)
    def _():
        out_ref[:, 4 * rows : 5 * rows, :] = grad.reshape(GROUPS, rows, width)

    @pl.when((at >= 1) & (at < 5))
    def _():
        start = pl.multiple_of(5 * rows + (at - 1) * rows, 16)
        out_ref[:, pl.ds(start, rows), :] = grad.reshape(GROUPS, rows, width)

    @pl.when(at >= 5)
    def _():
        out_ref[pl.ds((at - 5) * 4, 4), 0 : 4 * rows, :] = grad.reshape(4, 4 * rows, width)


def feed_grad(left, right):
    tokens = left.shape[0]
    width = left.shape[1] // 6
    rows = width // GROUPS

    def left_at(i):
        return (0, jnp.where(i == 0, 0, jnp.where(i < 5, 1, i - 3)))

    def right_at(i):
        return (0, jnp.minimum(i, 5))

    return pl.pallas_call(
        feed_grad_kernel,
        grid=(9,),
        in_specs=[
            pl.BlockSpec((tokens, width), left_at),
            pl.BlockSpec((tokens, width), right_at),
        ],
        out_specs=pl.BlockSpec((GROUPS, 9 * rows, width), lambda i: (0, 0, 0)),
        out_shape=jax.ShapeDtypeStruct((GROUPS, 9 * rows, width), bf16),
        compiler_params=pltpu.CompilerParams(vmem_limit_bytes=VMEM_LIMIT),
        cost_estimate=cost(2 * tokens * width * width * 9, tokens * width * 24 + width * width * 18),
        name="feed_grad",
    )(left, right)


def attn_grad_kernel(x_ref, d_ref, vec_ref, out_ref):
    width = x_ref.shape[1]
    rows = width // GROUPS
    at = pl.program_id(0)
    grad = tn(x_ref[...], d_ref[...]).astype(bf16)
    start = pl.multiple_of(at * rows, 16)
    out_ref[:, pl.ds(start, rows), :] = grad.reshape(GROUPS, rows, width)
    out_ref[:, 3 * rows :, :] = vec_ref[...]


def attn_grad(x, d, vectors):
    tokens, width = x.shape
    rows = width // GROUPS
    return pl.pallas_call(
        attn_grad_kernel,
        grid=(3,),
        in_specs=[
            pl.BlockSpec((tokens, width), lambda i: (0, 0)),
            pl.BlockSpec((tokens, width), lambda i: (0, i)),
            pl.BlockSpec((GROUPS, 16, width), lambda i: (0, 0, 0)),
        ],
        out_specs=pl.BlockSpec((GROUPS, 3 * rows + 16, width), lambda i: (0, 0, 0)),
        out_shape=jax.ShapeDtypeStruct((GROUPS, 3 * rows + 16, width), bf16),
        compiler_params=pltpu.CompilerParams(vmem_limit_bytes=VMEM_LIMIT),
        cost_estimate=cost(2 * tokens * width * width * 3, tokens * width * 8 + width * width * 6),
        name="attn_grad",
    )(x, d, vectors)


def input_grad_kernel(d_ref, w_ref, out_ref):
    width = out_ref.shape[1]
    rows = width // GROUPS
    total = None
    for i in range(3):
        part = nt(
            d_ref[:, i * width : i * width + width],
            w_ref[:, i * rows : i * rows + rows, :].reshape(width, width),
        )
        total = part if total is None else total + part
    out_ref[...] = total.astype(out_ref.dtype)


def input_grad_part(d, weights, side_at, kind):
    _, micro, local, wide = d.shape
    width = wide // 3
    sub = local // BLOCK
    return pl.pallas_call(
        input_grad_kernel,
        grid=(micro, sub),
        in_specs=[
            pl.BlockSpec((None, None, BLOCK, wide), lambda m, i: (side_at, m, i, 0)),
            pl.BlockSpec(weights.shape, lambda m, i: (0, 0, 0)),
        ],
        out_specs=pl.BlockSpec((None, BLOCK, width), lambda m, i: (m, i, 0)),
        out_shape=jax.ShapeDtypeStruct((micro, local, width), kind),
        compiler_params=pltpu.CompilerParams(vmem_limit_bytes=VMEM_LIMIT),
        cost_estimate=cost(2 * micro * local * wide * width, micro * local * wide * 2 + weights.size * 2),
        name="input_grad",
    )(d, weights)


def on_device(
    tokens,
    kinds,
    groups,
    query_weight,
    query_bias,
    key_weight,
    key_bias,
    value_weight,
    value_bias,
    output_weight,
    output_bias,
    norm1_gain,
    norm1_shift,
    up_weight,
    up_bias,
    down_weight,
    down_bias,
    norm2_gain,
    norm2_shift,
    cotangent,
):
    micro, _, local, width = tokens.shape
    half = width // 2
    head_dim = width // HEADS
    devices = lax.axis_size("shard")
    rows = width // devices
    side = lax.axis_index("seq").astype(jnp.int32)
    per = local // BLOCK

    vector = jnp.concatenate(
        [
            query_bias,
            key_bias,
            value_bias,
            output_bias,
            norm1_gain,
            norm1_shift,
            up_bias,
            down_bias,
            norm2_gain,
            norm2_shift,
        ]
    )
    piece = vector.shape[0]
    vector_row = jnp.pad(vector, (0, width - piece))[None]
    attn_sizes = (rows, rows, rows)
    feed_sizes = (4 * rows,) + (rows,) * 5
    packed = pack_attention(query_weight, key_weight, value_weight, vector_row, side, head_dim)
    attn_gathered = lax.all_gather(packed[None], "shard", axis=0, tiled=True)
    feed_local = jnp.concatenate(
        [down_weight, output_weight] + [up_weight[:, j * width : j * width + width] for j in range(4)],
        axis=0,
    )
    feed_gathered = lax.all_gather(feed_local[None], "shard", axis=0, tiled=True)
    vectors = attn_gathered[:, 3 * rows, :piece]
    if devices == GROUPS:
        attn_w, feed_w = attn_gathered, feed_gathered
    else:
        attn_w = regroup(attn_gathered, attn_sizes)
        feed_w = regroup(feed_gathered, feed_sizes)

    def whole_vector(start, size):
        return vectors[:, start : start + size].reshape(-1).astype(f32)

    full_query_bias = whole_vector(0, 4 * rows)
    full_key_bias = whole_vector(4 * rows, rows)
    full_value_bias = whole_vector(5 * rows, rows)
    bias_rows = jnp.concatenate(
        [
            pair_columns(full_query_bias, side, head_dim),
            jnp.concatenate([own_half(full_key_bias, side), own_half(full_value_bias, side)])[None],
        ],
        axis=0,
    )
    full_up_bias = whole_vector(9 * rows, 4 * rows).reshape(4, width)
    chain_vectors = jnp.concatenate(
        [
            whole_vector(6 * rows, rows)[None],
            whole_vector(7 * rows, rows)[None],
            whole_vector(8 * rows, rows)[None],
            full_up_bias,
            whole_vector(13 * rows, rows)[None],
            whole_vector(14 * rows, rows)[None],
            whole_vector(15 * rows, rows)[None],
        ],
        axis=0,
    )

    own_tokens = tokens[:, 0]
    marks = jnp.stack([kinds[:, 0], groups[:, 0]])
    xs = jnp.stack([own_tokens, swap(own_tokens)])
    both_marks = jnp.stack([marks, swap(marks)])
    kind_all, group_all = both_marks[:, 0], both_marks[:, 1]
    kind_col = kind_all[..., None]
    gk = group_all[..., None]
    gq = group_all[:, :, None, :]
    by_block = group_all.reshape(2, micro, per, BLOCK)
    low = jnp.swapaxes(by_block[..., 0], 0, 1).reshape(-1)
    high = jnp.swapaxes(by_block[..., BLOCK - 1], 0, 1).reshape(-1)

    qp, km, kmt, v, vt = project(xs, attn_w, bias_rows, kind_col)
    c, ct, lse = attend(low, high, qp, km, vt, gk, gq)
    c_other = swap(c[1])
    flat = micro * local
    mixed, dh1, left, right, dc_own, dc_other, sums = chain(
        side,
        own_tokens.reshape(flat, width),
        c[0].reshape(flat, half),
        c_other.reshape(flat, half),
        cotangent.reshape(flat, width),
        feed_w,
        chain_vectors,
    )

    dc = jnp.stack([dc_own, swap(dc_other)]).reshape(2, micro, local, half)
    feed_part = feed_grad(left, right)
    if devices != GROUPS:
        feed_part = ungroup(feed_part, feed_sizes, devices)
    feed_sum = lax.psum_scatter(feed_part, "shard", scatter_dimension=0, tiled=True)[0]
    d, db = attend_back(low, high, qp, km, kmt, v, dc, ct, lse, gk, gq, kind_col)

    query_own = unpair_columns(db[0, : 2 * width].reshape(2, width), head_dim)
    zero = jnp.zeros((half,), f32)

    def spread(own):
        return jnp.where(side == 0, jnp.concatenate([own, zero]), jnp.concatenate([zero, own]))

    query_spread = jnp.concatenate([spread(query_own[e, w]) for e in range(2) for w in range(2)])
    key_spread = spread(db[0, 2 * width : 2 * width + half])
    value_spread = spread(db[0, 2 * width + half :])
    grad_vectors = jnp.concatenate(
        [
            query_spread.reshape(devices, 4 * rows),
            key_spread.reshape(devices, rows),
            value_spread.reshape(devices, rows),
            sums[5].reshape(devices, rows),
            sums[3].reshape(devices, rows),
            sums[4].reshape(devices, rows),
            sums[8:12].reshape(devices, 4 * rows),
            sums[2].reshape(devices, rows),
            sums[0].reshape(devices, rows),
            sums[1].reshape(devices, rows),
        ],
        axis=1,
    ).astype(bf16)
    grad_vectors = jnp.pad(grad_vectors[:, None, :], ((0, 0), (0, 15), (0, width - piece)))
    if devices == GROUPS:
        attn_part = attn_grad(xs.reshape(2 * flat, width), d.reshape(2 * flat, 3 * width), grad_vectors)
    else:
        zeros = jnp.zeros((GROUPS, 16, width), bf16)
        attn_part = attn_grad(xs.reshape(2 * flat, width), d.reshape(2 * flat, 3 * width), zeros)
        attn_part = jnp.concatenate(
            [ungroup(attn_part[:, : 3 * (width // GROUPS)], attn_sizes, devices), grad_vectors], axis=1
        )
    attn_sum = lax.psum_scatter(attn_part, "shard", scatter_dimension=0, tiled=True)[0]

    dx_other = input_grad_part(d, attn_w, 1, bf16)
    dx_own = input_grad_part(d, attn_w, 0, f32)
    input_grad = dh1.reshape(micro, local, width) + dx_own + swap(dx_other).astype(f32)

    feed_total = feed_sum.astype(f32) + swap(feed_sum).astype(f32)
    grad_down = feed_total[: 4 * rows]
    grad_output = feed_total[4 * rows : 5 * rows]
    grad_up = jnp.concatenate(
        [feed_total[(5 + j) * rows : (6 + j) * rows] for j in range(4)], axis=1
    )
    attn_own = attn_sum.astype(f32)
    attn_other = swap(attn_sum).astype(f32)
    vec_total = attn_own[3 * rows, :piece] + attn_other[3 * rows, :piece]

    def by_side(own, other, axis):
        return jnp.where(
            side == 0,
            jnp.concatenate([own, other], axis=axis),
            jnp.concatenate([other, own], axis=axis),
        )

    def query_parts(block):
        pairs = jnp.stack([block[:rows], block[rows : 2 * rows]], axis=1)
        return unpair_columns(pairs, head_dim)

    grad_query = by_side(query_parts(attn_own), query_parts(attn_other), 3).reshape(rows, 4 * width)
    kv_own, kv_other = attn_own[2 * rows : 3 * rows], attn_other[2 * rows : 3 * rows]
    grad_key = by_side(kv_own[:, :half], kv_other[:, :half], 1)
    grad_value = by_side(kv_own[:, half:], kv_other[:, half:], 1)

    def piece_of(start, size):
        return vec_total[start : start + size]

    return (
        mixed.reshape(micro, 1, local, width),
        input_grad[:, None],
        grad_query,
        piece_of(0, 4 * rows),
        grad_key,
        piece_of(4 * rows, rows),
        grad_value,
        piece_of(5 * rows, rows),
        grad_output,
        piece_of(6 * rows, rows),
        piece_of(7 * rows, rows),
        piece_of(8 * rows, rows),
        grad_up,
        piece_of(9 * rows, 4 * rows),
        grad_down,
        piece_of(13 * rows, rows),
        piece_of(14 * rows, rows),
        piece_of(15 * rows, rows),
    )


def solution(mesh):
    weight = P("shard", None)
    vector = P("shard")
    tokens = P(None, "shard", "seq", None)
    marks = P(None, "shard", "seq")
    return jax.shard_map(
        on_device,
        mesh=mesh,
        in_specs=(tokens, marks, marks)
        + (weight, vector) * 4
        + (vector, vector)
        + (weight, vector) * 2
        + (vector, vector)
        + (tokens,),
        out_specs=(tokens, tokens)
        + (weight, vector) * 4
        + (vector, vector)
        + (weight, vector) * 2
        + (vector, vector),
        check_vma=False,
    )
```

time: 1400 us -> 527 us (0.38)
  matrix products: 360 us -> 0 us
  local copies, waits for them, and re-layouts: 309 us -> 32.4 us
  Pallas kernels: 0 us -> 226 us
  blocking collectives: 176 us -> 0 us
  waiting for transfers between devices: 360 us -> 226 us
  other arithmetic: 104 us -> 16.7 us
  starting transfers between devices: 55.8 us -> 10.6 us
    dot_general x204 -> x0, matrix products: 360 us -> none  [the longest x60 139 us: inner_rows(): lax.dot_general(left_side, right_side, (((0,), (0,)), ((), ())), preferre...]
    pallas_call x0 -> x9, Pallas kernels: none -> 226 us  [the longest x1 59.4 us: attend_back(): pl.pallas_call(attend_back_kernel, grid_spec=pltpu.PrefetchScalarGridSpec...]
    unnamed x2 -> x0, blocking collectives: 124 us -> none
    unnamed x16 -> x4, waiting for transfers between devices: 117 us -> 0.07 us
    ppermute x0 -> x7, waiting for transfers between devices: none -> 111 us  [swap(): return lax.ppermute(value, 'seq', [(0, 1), (1, 0)])]
    reduce_scatter x3 -> x2, waiting for transfers between devices: 197 us -> 112 us  [the longest x1 112 us: on_device(): lax.psum_scatter(feed_part, 'shard', scatter_dimension=0, tiled=True)[0]]
    while x402 -> x0, local copies, waits for them, and re-layouts: 55.5 us -> none
    all_to_all x12 -> x0, starting transfers between devices: 54.6 us -> none  [the longest x2 10.1 us: on_device(): lax.all_to_all(jnp.transpose(grad_pair_heads, (1, 0, 2))[:, None], 'seq',...]
  transfers between devices with their start and end apart: 25 -> 11, of which waited for: 8 -> 9; matrix products, arithmetic and copies ran while one was open for 50% -> 6% of each run, Pallas kernels for 0% -> 19%
where the time goes in v1:
time: 527 us; the launch traced here: 526 us
  Pallas kernels  226 us (43%)
  waiting for transfers between devices  226 us (43%)
  local copies, waits for them, and re-layouts  32.4 us (6%)
  other arithmetic  16.7 us (3%)
  between operations  14.1 us (3%)
  starting transfers between devices  10.6 us (2%)
    reduce_scatter x1, waiting for transfers between devices, on_device(): lax.psum_scatter(feed_part, 'shard', scatter_dimension=0, tiled=True)[0]  112 us
    ppermute x7, waiting for transfers between devices, swap(): return lax.ppermute(value, 'seq', [(0, 1), (1, 0)])  111 us
    pallas_call x1, Pallas kernels, attend_back(): pl.pallas_call(attend_back_kernel, grid_spec=pltpu.PrefetchScalarGridSpec...  59.4 us
    pallas_call x1, Pallas kernels, chain(): pl.pallas_call(chain_kernel, grid_spec=pltpu.PrefetchScalarGridSpec(num_s...  50.6 us
    pallas_call x1, Pallas kernels, attend(): pl.pallas_call(attend_kernel, grid_spec=pltpu.PrefetchScalarGridSpec(num_...  49.7 us
    pallas_call x1, Pallas kernels, feed_grad(): pl.pallas_call(feed_grad_kernel, grid=(9,), in_specs=[pl.BlockSpec((token...  20.5 us
    pallas_call x2, Pallas kernels, input_grad_part(): pl.pallas_call(input_grad_kernel, grid=(micro, sub), in_specs=[pl.BlockSp...  16.6 us
    pallas_call x1, Pallas kernels, project(): pl.pallas_call(project_kernel, grid=(halves, micro, sub), in_specs=[rows_...  14.5 us
  transfers between devices with their start and end apart: 11, of which 9 were waited for; matrix products, arithmetic and copies ran while one was open for 6% of the time, Pallas kernels for 19%

profile of v1, /device:TPU:0, one launch (start us, length us, event | category | flops | bytes accessed | tf_op | source)
XLA Modules:
  0.0 525.7 jit_solution(7317897896359526298)
XLA Ops:
  7.3 6.9 %concatenate.121 = bf16[768]{0:T(1024)(128)(2,1)S(1)} concatenate(bf16[192]{0:T(256)(128)(2,1)} %param.24, bf16[48]{0:T(256)(128)(2,1)} %param.26, bf16[48]{0:T(256)(128)(2,1)} %param.28, bf16[48]{0:T(256)(128)(2,1)} %param.30, bf16[48]{0:T(256)(128)(2,1)} %param.31, bf16[48]{0:T(256)(128)(2,1)} %param.32, bf16[192]{0:T(256)(128)(2,1)} %param.34, bf16[48]{0:T(256)(128)(2,1)} %param.36, ...), dimensions={0} | concatenate | bytes 3072 | tf_op jit(solution)/shard_map/concatenate | solution.py:737
  14.7 1.8 pack.1
  16.6 1.0 constant_dynamic-update-slice_fusion.1
  17.6 0.9 constant_dynamic-update-slice_fusion
  18.5 0.9 slice_dynamic-update-slice_fusion.3
  19.4 0.9 slice_dynamic-update-slice_fusion.2
  20.3 0.9 slice_dynamic-update-slice_fusion.1
  21.1 0.9 slice_dynamic-update-slice_fusion
  22.0 0.8 copy-done.2
  22.9 3.0 collective-permute-start.1
  26.8 34.0 %collective-permute-done = s32[2,2,512]{2,0,1:T(2,128)S(1)} collective-permute-done((s32[2,2,512]{2,0,1:T(2,128)S(1)}, s32[2,2,512]{2,0,1:T(2,128)S(1)}, u32[]{:S(2)}, u32[]{:S(2)}) %collective-permute-start) | collective-permute-done | bytes 8224 | tf_op jit(solution)/shard_map/ppermute | solution.py:33
  62.3 1.3 broadcast_in_dim_squeeze.12.kind_ref
  63.7 1.3 copy.82.gk_ref
  65.0 1.9 pad_maximum_fusion.x_ref
  67.0 1.5 all-gather.5.cloned.1.call-done
  68.5 1.0 slice.329
  70.6 14.5 %project.1 = (bf16[2,2,512,768]{3,2,1,0:T(8,128)(2,1)}, bf16[2,2,512,768]{3,2,1,0:T(8,128)(2,1)}, bf16[2,2,768,512]{3,2,1,0:T(8,128)(2,1)}, bf16[2,2,512,384]{3,2,1,0:T(8,128)(2,1)}, bf16[2,2,384,512]{3,2,1,0:T(8,128)(2,1)}) custom-call(bf16[2,2,512,768]{3,2,1,0:T(8,128)(2,1)} %pad_maximum_fusion.x_ref, bf16[16,160,768]{2,1,0:T(8,128)(2,1)} %bitcast.83, ...), custom_call_target="tpu_custom_call" | custom-call | flops 7247757312 | bytes 15728640 | tf_op jit(solution)/shard_map/project/pallas_call | solution.py:177
  85.1 49.7 %attend.1 = (bf16[2,2,512,384]{3,2,1,0:T(8,128)(2,1)}, f32[2,384,1024]{2,1,0:T(8,128)}, f32[2,8,1024]{2,1,0:T(8,128)}) custom-call(s32[8]{0:T(128)} %reshape.369.low_ref, s32[8]{0:T(128)} %reshape.370.high_ref, bf16[2,2,512,768]{3,2,1,0:T(8,128)(2,1)} %get-tuple-element.35.qp_ref, bf16[2,2,512,768]{3,2,1,0:T(8,128)(2,1)} %get-tuple-element.36.km_ref, ...), custom_call_target="tpu_custom_call" | custom-call | flops 6442450944 | bytes 12582912 | tf_op jit(solution)/shard_map/attend/pallas_call | solution.py:262
  134.8 2.4 slice_bitcast_fusion
  137.2 1.4 collective-permute-start.2
  140.0 16.9 %collective-permute-done.2 = bf16[2,512,384]{2,1,0:T(8,128)(2,1)S(1)} collective-permute-done((bf16[2,512,384]{2,1,0:T(8,128)(2,1)S(1)}, bf16[2,512,384]{2,1,0:T(8,128)(2,1)S(1)}, u32[]{:S(2)}, u32[]{:S(2)}) %collective-permute-start.2) | collective-permute-done | bytes 786464 | tf_op jit(solution)/shard_map/ppermute | solution.py:33
  156.9 1.0 all-gather.7.cloned.1.call-done
  157.9 50.6 %chain.1 = (bf16[1024,768]{1,0:T(8,128)(2,1)}, f32[1024,768]{1,0:T(8,128)}, bf16[1024,4608]{1,0:T(8,128)(2,1)}, bf16[1024,4608]{1,0:T(8,128)(2,1)}, bf16[1024,38...) custom-call(s32[1]{0:T(128)} %bitcast.side_ref, bf16[1024,768]{1,0:T(8,128)(2,1)} %bitcast.89, ...), custom_call_target="tpu_custom_call" | custom-call | flops 22951231488 | bytes 38928384 | tf_op jit(solution)/shard_map/chain/pallas_call | solution.py:561
  208.4 1.5 collective-permute-start.3
  210.0 0.8 convert.64
  211.5 16.9 %collective-permute-done.3 = bf16[1024,384]{1,0:T(8,128)(2,1)S(1)} collective-permute-done((bf16[1024,384]{1,0:T(8,128)(2,1)}, bf16[1024,384]{1,0:T(8,128)(2,1)S(1)}, u32[]{:S(2)}, u32[]{:S(2)}) %collective-permute-start.3) | collective-permute-done | bytes 786464 | tf_op jit(solution)/shard_map/ppermute | solution.py:33
  228.4 2.5 pad_maximum_fusion.1.dc_ref
  230.9 59.4 %attend_back.1 = (bf16[2,2,512,2304]{3,2,1,0:T(8,128)(2,1)}, f32[8,2304]{1,0:T(8,128)}) custom-call(s32[8]{0:T(128)} %reshape.369.low_ref, s32[8]{0:T(128)} %reshape.370.high_ref, bf16[2,2,512,768]{3,2,1,0:T(8,128)(2,1)} %get-tuple-element.35.qp_ref, bf16[2,2,512,768]{3,2,1,0:T(8,128)(2,1)} %get-tuple-element.36.km_ref, ...), custom_call_target="tpu_custom_call" | custom-call | flops 16106127360 | bytes 25165824 | tf_op jit(solution)/shard_map/attend_back/pallas_call | solution.py:397
  290.3 0.7 slice_reduce_fusion.11
  291.0 0.8 slice_reduce_fusion
  293.0 0.8 pad.16.vec_ref
  293.8 12.9 %attn_grad.1 = bf16[16,160,768]{2,1,0:T(8,128)(2,1)} custom-call(bf16[2048,768]{1,0:T(8,128)(2,1)} %bitcast.86, bf16[2048,2304]{1,0:T(8,128)(2,1)} %bitcast.81, bf16[16,16,768]{2,1,0:T(8,128)(2,1)} %pad.16.vec_ref), custom_call_target="tpu_custom_call" | custom-call | flops 7247757312 | bytes 16121856 | tf_op jit(solution)/shard_map/attn_grad/pallas_call | solution.py:659
  306.7 20.5 %feed_grad.1 = bf16[16,432,768]{2,1,0:T(8,128)(2,1)} custom-call(bf16[1024,4608]{1,0:T(8,128)(2,1)} %get-tuple-element.50.l_ref, bf16[1024,4608]{1,0:T(8,128)(2,1)} %get-tuple-element.51.r_ref), custom_call_target="tpu_custom_call" | custom-call | flops 10871635968 | bytes 29491200 | tf_op jit(solution)/shard_map/feed_grad/pallas_call | solution.py:631
  327.2 8.2 %input_grad.3 = bf16[2,512,768]{2,1,0:T(8,128)(2,1)} custom-call(bf16[2,2,512,2304]{3,2,1,0:T(8,128)(2,1)} %get-tuple-element.47.d_ref, bf16[16,160,768]{2,1,0:T(8,128)(2,1)} %bitcast.84), custom_call_target="tpu_custom_call" | custom-call | flops 3623878656 | bytes 8650752 | tf_op jit(solution)/shard_map/input_grad/pallas_call | solution.py:692
  335.4 1.4 collective-permute-start.4
  336.8 8.4 %input_grad.2 = f32[2,512,768]{2,1,0:T(8,128)} custom-call(bf16[2,2,512,2304]{3,2,1,0:T(8,128)(2,1)} %get-tuple-element.47.d_ref, bf16[16,160,768]{2,1,0:T(8,128)(2,1)} %bitcast.85), custom_call_target="tpu_custom_call" | custom-call | flops 3623878656 | bytes 8650752 | tf_op jit(solution)/shard_map/input_grad/pallas_call | solution.py:692
  345.2 26.2 %collective-permute-done.4 = bf16[2,512,768]{2,1,0:T(8,128)(2,1)} collective-permute-done((bf16[2,512,768]{2,1,0:T(8,128)(2,1)}, bf16[2,512,768]{2,1,0:T(8,128)(2,1)}, u32[]{:S(2)}, u32[]{:S(2)}) %collective-permute-start.4) | collective-permute-done | bytes 1572896 | tf_op jit(solution)/shard_map/ppermute | solution.py:33
  371.4 4.5 add_bitcast_fusion
  375.9 1.5 collective-permute-start.5
  377.4 1.0 bitcast_convert_fusion
  379.3 3.3 collective-permute-done.5
  383.9 1.3 select_n.98
  386.6 112.4 %reduce-scatter.5.cloned.1.call-done = bf16[1,432,768]{2,1,0:T(8,128)(2,1)} async-done(((bf16[16,432,768]{2,1,0:T(8,128)(2,1)}), bf16[1,432,768]{2,1,0:T(8,128)(2,1)}) %reduce-scatter.5.cloned.1.call-update) | async-done | bytes 663568 | tf_op jit(solution)/shard_map/reduce_scatter | solution.py:826
  499.0 1.5 collective-permute-start.6
  501.8 13.8 %collective-permute-done.6 = bf16[432,768]{1,0:T(8,128)(2,1)S(1)} collective-permute-done((bf16[432,768]{1,0:T(8,128)(2,1)}, bf16[432,768]{1,0:T(8,128)(2,1)S(1)}, u32[]{:S(2)}, u32[]{:S(2)}) %collective-permute-start.6) | collective-permute-done | bytes 663584 | tf_op jit(solution)/shard_map/ppermute | solution.py:33
  515.5 1.2 convert_add_fusion
  516.8 0.9 slice.379
  518.3 0.9 pad_maximum_fusion.2
  (104 shorter events, 12.9 us)
Async XLA Ops:
  7.2 57.8 %copy-start.1 = (bf16[2,1,512,768]{3,2,1,0:T(8,128)(2,1)S(1)}, bf16[2,1,512,768]{3,2,1,0:T(8,128)(2,1)}, u32[]{:S(2)}) copy-start(bf16[2,1,512,768]{3,2,1,0:T(8,128)(2,1)} %param.20) | copy-start | bytes 4718596
  7.2 61.3 %all-gather.5.cloned.1.call-start = ((), (), s32[]{:S(2)}) async-start(), calls=%async_computation.4 | async-start | bytes 4177920 | tf_op jit(solution)/shard_map/all_gather | solution.py:756
  16.5 141.3 %all-gather.7.cloned.1.call-start = ((), (), s32[]{:S(2)}) async-start(), calls=%async_computation.5 | async-start | bytes 11280384 | tf_op jit(solution)/shard_map/all_gather | solution.py:761
  22.0 0.8 copy-start.2
  22.9 353.0 %reduce-scatter.3.cloned.1.call-start = ((), (), s32[]{:S(2)}) async-start(), calls=%async_computation.2 | async-start | bytes 4177920 | tf_op jit(solution)/shard_map/reduce_scatter | solution.py:862
  22.9 42.1 %collective-permute-start.1 = (bf16[2,512,768]{2,1,0:T(8,128)(2,1)}, bf16[2,512,768]{2,1,0:T(8,128)(2,1)S(1)}, u32[]{:S(2)}, u32[]{:S(2)}) collective-permute-start(bf16[2,512,768]{2,1,0:T(8,128)(2,1)} %bitcast.88), channel_id=1, source_target_pairs={{0,16},{16,0},{1,17},{17,1},{2,18},{18,2},{3,19},{19,3},{4,20},{20... | collective-permute-start | bytes 4718600 | tf_op jit(solution)/shard_map/ppermute | solution.py:33
  26.7 34.1 %collective-permute-start = (s32[2,2,512]{2,0,1:T(2,128)S(1)}, s32[2,2,512]{2,0,1:T(2,128)S(1)}, u32[]{:S(2)}, u32[]{:S(2)}) collective-permute-start(s32[2,2,512]{2,0,1:T(2,128)S(1)} %get-tuple-element.149), channel_id=1, source_target_pairs={{0,16},{16,0},{1,17},{17,1},{2,18},{18,2},{3,19},{19,3},{4,20},{20... | collective-permute-start | bytes 24584 | tf_op jit(solution)/shard_map/ppermute | solution.py:33
  60.8 6.1 %copy-start.3 = (s32[2,1,2,512]{3,1,2,0:T(1,128)}, s32[2,1,2,512]{3,1,2,0:T(1,128)S(1)}, u32[]{:S(2)}) copy-start(s32[2,1,2,512]{3,1,2,0:T(1,128)S(1)} %get-tuple-element.119) | copy-start | bytes 24580
  137.2 19.7 %collective-permute-start.2 = (bf16[2,512,384]{2,1,0:T(8,128)(2,1)S(1)}, bf16[2,512,384]{2,1,0:T(8,128)(2,1)S(1)}, u32[]{:S(2)}, u32[]{:S(2)}) collective-permute-start(bf16[2,512,384]{2,1,0:T(8,128)(2,1)S(1)} %get-tuple-element.120), channel_id=1, source_target_pairs={{0,16},{16,0},{1,17},{17,1},{2,18},{18,2},{3,19},{19,3},{4,20},{20... | collective-permute-start | bytes 2359304 | tf_op jit(solution)/shard_map/ppermute | solution.py:33
  156.9 1.0 copy-start.4
  208.4 20.0 %collective-permute-start.3 = (bf16[1024,384]{1,0:T(8,128)(2,1)}, bf16[1024,384]{1,0:T(8,128)(2,1)S(1)}, u32[]{:S(2)}, u32[]{:S(2)}) collective-permute-start(bf16[1024,384]{1,0:T(8,128)(2,1)} %get-tuple-element.44), channel_id=1, source_target_pairs={{0,16},{16,0},{1,17},{17,1},{2,18},{18,2},{3,19},{19,3},{4,20},{20... | collective-permute-start | bytes 2359304 | tf_op jit(solution)/shard_map/ppermute | solution.py:33
  306.7 192.4 %reduce-scatter.5.cloned.1.call-start = ((), (), s32[]{:S(2)}) async-start(), calls=%async_computation.3 | async-start | bytes 11280384 | tf_op jit(solution)/shard_map/reduce_scatter | solution.py:826
  335.4 36.0 %copy-start = (f32[1024,768]{1,0:T(8,128)S(1)}, f32[1024,768]{1,0:T(8,128)}, u32[]{:S(2)}) copy-start(f32[1024,768]{1,0:T(8,128)} %get-tuple-element.40) | copy-start | bytes 9437188
  335.4 36.0 %collective-permute-start.4 = (bf16[2,512,768]{2,1,0:T(8,128)(2,1)}, bf16[2,512,768]{2,1,0:T(8,128)(2,1)}, u32[]{:S(2)}, u32[]{:S(2)}) collective-permute-start(bf16[2,512,768]{2,1,0:T(8,128)(2,1)} %input_grad.3), channel_id=1, source_target_pairs={{0,16},{16,0},{1,17},{17,1},{2,18},{18,2},{3,19},{19,3},{4,20},{20... | collective-permute-start | bytes 4718600 | tf_op jit(solution)/shard_map/ppermute | solution.py:33
  375.9 6.6 %collective-permute-start.5 = (bf16[160,768]{1,0:T(8,128)(2,1)}, bf16[160,768]{1,0:T(8,128)(2,1)S(1)}, u32[]{:S(2)}, u32[]{:S(2)}) collective-permute-start(bf16[160,768]{1,0:T(8,128)(2,1)} %bitcast.96), channel_id=1, source_target_pairs={{0,16},{16,0},{1,17},{17,1},{2,18},{18,2},{3,19},{19,3},{4,20},{20... | collective-permute-start | bytes 737288 | tf_op jit(solution)/shard_map/ppermute | solution.py:33
  499.0 16.5 %collective-permute-start.6 = (bf16[432,768]{1,0:T(8,128)(2,1)}, bf16[432,768]{1,0:T(8,128)(2,1)S(1)}, u32[]{:S(2)}, u32[]{:S(2)}) collective-permute-start(bf16[432,768]{1,0:T(8,128)(2,1)} %bitcast.95), channel_id=1, source_target_pairs={{0,16},{16,0},{1,17},{17,1},{2,18},{18,2},{3,19},{19,3},{4,20},{20... | collective-permute-start | bytes 1990664 | tf_op jit(solution)/shard_map/ppermute | solution.py:33
Sparse Core Ops, SparseCore 0:
  16.7 51.7 all-gather.4
  70.8 87.0 all-gather.6
  306.8 68.5 reduce-scatter.2
  379.3 119.7 reduce-scatter.4

commit v2 on v1

--- a/solution.py
+++ b/solution.py
@@ -1,11 +1,10 @@
-import functools
-
 import jax
 import jax.numpy as jnp
 from jax import lax
 from jax.experimental import pallas as pl
 from jax.experimental.pallas import tpu as pltpu
 from jax.sharding import PartitionSpec as P
+
 
 HEADS = 12
 GROUPS = 16
@@ -108,7 +107,7 @@
 
 
 def regroup(gathered, sizes):
-    devices, _, width = gathered.shape
+    _, _, width = gathered.shape
     pieces = []
     start = 0
     for size in sizes:
@@ -753,6 +752,9 @@
     attn_sizes = (rows, rows, rows)
     feed_sizes = (4 * rows,) + (rows,) * 5
     packed = pack_attention(query_weight, key_weight, value_weight, vector_row, side, head_dim)
+    packed, down_weight, output_weight, up_weight = lax.optimization_barrier(
+        (packed, down_weight, output_weight, up_weight)
+    )
     attn_gathered = lax.all_gather(packed[None], "shard", axis=0, tiled=True)
     feed_local = jnp.concatenate(
         [down_weight, output_weight] + [up_weight[:, j * width : j * width + width] for j in range(4)],
@@ -819,8 +821,10 @@
         chain_vectors,
     )
 
-    dc = jnp.stack([dc_own, swap(dc_other)]).reshape(2, micro, local, half)
+    dc_swapped = swap(dc_other)
     feed_part = feed_grad(left, right)
+    dc_swapped, feed_part = lax.optimization_barrier((dc_swapped, feed_part))
+    dc = jnp.stack([dc_own, dc_swapped]).reshape(2, micro, local, half)
     if devices != GROUPS:
         feed_part = ungroup(feed_part, feed_sizes, devices)
     feed_sum = lax.psum_scatter(feed_part, "shard", scatter_dimension=0, tiled=True)[0]

time: 527 us -> 528 us (level)
  waiting for transfers between devices: 226 us -> 243 us
  Pallas kernels: 226 us -> 212 us
    reduce_scatter x1, waiting for transfers between devices: 0.01 us -> 25.2 us  [on_device(): lax.psum_scatter(attn_part, 'shard', scatter_dimension=0, tiled=True)[0]]
    ppermute x7, waiting for transfers between devices: 111 us -> 94.8 us  [swap(): return lax.ppermute(value, 'seq', [(0, 1), (1, 0)])]
    pallas_call x1, Pallas kernels: 49.7 us -> 42.4 us  [attend(): pl.pallas_call(attend_kernel, grid_spec=pltpu.PrefetchScalarGridSpec(num_...]
    pallas_call x1, Pallas kernels: 59.4 us -> 52.2 us  [attend_back(): pl.pallas_call(attend_back_kernel, grid_spec=pltpu.PrefetchScalarGridSpec...]
    all_gather x1, waiting for transfers between devices: 0.97 us -> 8.2 us  [on_device(): lax.all_gather(feed_local[None], 'shard', axis=0, tiled=True)]
  transfers between devices with their start and end apart: 11 -> 11, of which waited for: 9 -> 9; matrix products, arithmetic and copies ran while one was open for 6% -> 6% of each run, Pallas kernels for 19% -> 18%
where the time goes in v2:
time: 528 us; the launch traced here: 527 us
  waiting for transfers between devices  243 us (46%)
  Pallas kernels  212 us (40%)
  local copies, waits for them, and re-layouts  32.4 us (6%)
  other arithmetic  15.6 us (3%)
  between operations  14.1 us (3%)
  starting transfers between devices  9.72 us (2%)
    reduce_scatter x1, waiting for transfers between devices, on_device(): lax.psum_scatter(feed_part, 'shard', scatter_dimension=0, tiled=True)[0]  113 us
    ppermute x7, waiting for transfers between devices, swap(): return lax.ppermute(value, 'seq', [(0, 1), (1, 0)])  94.8 us
    pallas_call x1, Pallas kernels, attend_back(): pl.pallas_call(attend_back_kernel, grid_spec=pltpu.PrefetchScalarGridSpec...  52.2 us
    pallas_call x1, Pallas kernels, chain(): pl.pallas_call(chain_kernel, grid_spec=pltpu.PrefetchScalarGridSpec(num_s...  50.6 us
    pallas_call x1, Pallas kernels, attend(): pl.pallas_call(attend_kernel, grid_spec=pltpu.PrefetchScalarGridSpec(num_...  42.4 us
    reduce_scatter x1, waiting for transfers between devices, on_device(): lax.psum_scatter(attn_part, 'shard', scatter_dimension=0, tiled=True)[0]  25.2 us
    pallas_call x1, Pallas kernels, feed_grad(): pl.pallas_call(feed_grad_kernel, grid=(9,), in_specs=[pl.BlockSpec((token...  20.4 us
    pallas_call x2, Pallas kernels, input_grad_part(): pl.pallas_call(input_grad_kernel, grid=(micro, sub), in_specs=[pl.BlockSp...  17.2 us
  transfers between devices with their start and end apart: 11, of which 9 were waited for; matrix products, arithmetic and copies ran while one was open for 6% of the time, Pallas kernels for 18%

profile of v2, /device:TPU:0, one launch (start us, length us, event | category | flops | bytes accessed | tf_op | source)
XLA Modules:
  0.0 527.0 jit_solution(8375353565997334522)
XLA Ops:
  7.3 6.9 %concatenate.121 = bf16[768]{0:T(1024)(128)(2,1)S(1)} concatenate(bf16[192]{0:T(256)(128)(2,1)} %param.24, bf16[48]{0:T(256)(128)(2,1)} %param.26, bf16[48]{0:T(256)(128)(2,1)} %param.28, bf16[48]{0:T(256)(128)(2,1)} %param.30, bf16[48]{0:T(256)(128)(2,1)} %param.31, bf16[48]{0:T(256)(128)(2,1)} %param.32, bf16[192]{0:T(256)(128)(2,1)} %param.34, bf16[48]{0:T(256)(128)(2,1)} %param.36, ...), dimensions={0} | concatenate | bytes 3072 | tf_op jit(solution)/shard_map/concatenate | solution.py:736
  14.7 1.8 pack.1
  16.6 1.0 constant_dynamic-update-slice_fusion.1
  17.6 0.9 constant_dynamic-update-slice_fusion
  18.5 0.9 slice_dynamic-update-slice_fusion.3
  19.4 0.9 slice_dynamic-update-slice_fusion.2
  20.3 0.9 slice_dynamic-update-slice_fusion.1
  21.1 0.9 slice_dynamic-update-slice_fusion
  22.0 0.8 copy-done.2
  23.0 3.0 collective-permute-start.1
  26.8 34.0 %collective-permute-done = s32[2,2,512]{2,0,1:T(2,128)S(1)} collective-permute-done((s32[2,2,512]{2,0,1:T(2,128)S(1)}, s32[2,2,512]{2,0,1:T(2,128)S(1)}, u32[]{:S(2)}, u32[]{:S(2)}) %collective-permute-start) | collective-permute-done | bytes 8224 | tf_op jit(solution)/shard_map/ppermute | solution.py:32
  62.3 1.3 broadcast_in_dim_squeeze.12.kind_ref
  63.7 1.3 copy.82.gk_ref
  65.0 1.9 pad_maximum_fusion.x_ref
  67.0 1.5 all-gather.5.cloned.1.call-done
  68.5 1.0 slice.329
  70.6 14.5 %project.1 = (bf16[2,2,512,768]{3,2,1,0:T(8,128)(2,1)}, bf16[2,2,512,768]{3,2,1,0:T(8,128)(2,1)}, bf16[2,2,768,512]{3,2,1,0:T(8,128)(2,1)}, bf16[2,2,512,384]{3,2,1,0:T(8,128)(2,1)}, bf16[2,2,384,512]{3,2,1,0:T(8,128)(2,1)}) custom-call(bf16[2,2,512,768]{3,2,1,0:T(8,128)(2,1)} %pad_maximum_fusion.x_ref, bf16[16,160,768]{2,1,0:T(8,128)(2,1)} %bitcast.83, ...), custom_call_target="tpu_custom_call" | custom-call | flops 7247757312 | bytes 15728640 | tf_op jit(solution)/shard_map/project/pallas_call | solution.py:176
  85.1 42.4 %attend.1 = (bf16[2,2,512,384]{3,2,1,0:T(8,128)(2,1)}, f32[2,384,1024]{2,1,0:T(8,128)}, f32[2,8,1024]{2,1,0:T(8,128)}) custom-call(s32[8]{0:T(128)} %reshape.369.low_ref, s32[8]{0:T(128)} %reshape.370.high_ref, bf16[2,2,512,768]{3,2,1,0:T(8,128)(2,1)} %get-tuple-element.42.qp_ref, bf16[2,2,512,768]{3,2,1,0:T(8,128)(2,1)} %get-tuple-element.43.km_ref, ...), custom_call_target="tpu_custom_call" | custom-call | flops 6442450944 | bytes 12582912 | tf_op jit(solution)/shard_map/attend/pallas_call | solution.py:261
  127.5 2.4 slice_bitcast_fusion
  129.9 1.5 collective-permute-start.2
  132.7 16.9 %collective-permute-done.2 = bf16[2,512,384]{2,1,0:T(8,128)(2,1)S(1)} collective-permute-done((bf16[2,512,384]{2,1,0:T(8,128)(2,1)S(1)}, bf16[2,512,384]{2,1,0:T(8,128)(2,1)S(1)}, u32[]{:S(2)}, u32[]{:S(2)}) %collective-permute-start.2) | collective-permute-done | bytes 786464 | tf_op jit(solution)/shard_map/ppermute | solution.py:32
  149.6 8.2 %all-gather.7.cloned.1.call-done = bf16[6912,768]{1,0:T(8,128)(2,1)} async-done(((bf16[432,768]{1,0:T(8,128)(2,1)}), bf16[6912,768]{1,0:T(8,128)(2,1)}) %all-gather.7.cloned.1.call-update) | async-done | bytes 10616848 | tf_op jit(solution)/shard_map/all_gather | solution.py:763
  157.8 50.6 %chain.1 = (bf16[1024,768]{1,0:T(8,128)(2,1)}, f32[1024,768]{1,0:T(8,128)}, bf16[1024,4608]{1,0:T(8,128)(2,1)}, bf16[1024,4608]{1,0:T(8,128)(2,1)}, bf16[1024,38...) custom-call(s32[1]{0:T(128)} %bitcast.side_ref, bf16[1024,768]{1,0:T(8,128)(2,1)} %bitcast.89, ...), custom_call_target="tpu_custom_call" | custom-call | flops 22951231488 | bytes 38928384 | tf_op jit(solution)/shard_map/chain/pallas_call | solution.py:560
  208.4 0.8 convert.64
  209.9 1.5 collective-permute-start.3
  211.4 20.4 %feed_grad.1 = bf16[16,432,768]{2,1,0:T(8,128)(2,1)} custom-call(bf16[1024,4608]{1,0:T(8,128)(2,1)} %get-tuple-element.55.l_ref, bf16[1024,4608]{1,0:T(8,128)(2,1)} %get-tuple-element.56.r_ref), custom_call_target="tpu_custom_call" | custom-call | flops 10871635968 | bytes 29491200 | tf_op jit(solution)/shard_map/feed_grad/pallas_call | solution.py:630
  231.8 1.3 pad_maximum_fusion.1.dc_ref
  233.1 52.2 %attend_back.1 = (bf16[2,2,512,2304]{3,2,1,0:T(8,128)(2,1)}, f32[8,2304]{1,0:T(8,128)}) custom-call(s32[8]{0:T(128)} %reshape.369.low_ref, s32[8]{0:T(128)} %reshape.370.high_ref, bf16[2,2,512,768]{3,2,1,0:T(8,128)(2,1)} %get-tuple-element.42.qp_ref, bf16[2,2,512,768]{3,2,1,0:T(8,128)(2,1)} %get-tuple-element.43.km_ref, ...), custom_call_target="tpu_custom_call" | custom-call | flops 16106127360 | bytes 25165824 | tf_op jit(solution)/shard_map/attend_back/pallas_call | solution.py:396
  285.3 0.7 slice_reduce_fusion.11
  286.0 0.8 slice_reduce_fusion
  288.0 0.8 pad.16.vec_ref
  288.8 12.9 %attn_grad.1 = bf16[16,160,768]{2,1,0:T(8,128)(2,1)} custom-call(bf16[2048,768]{1,0:T(8,128)(2,1)} %bitcast.86, bf16[2048,2304]{1,0:T(8,128)(2,1)} %bitcast.81, bf16[16,16,768]{2,1,0:T(8,128)(2,1)} %pad.16.vec_ref), custom_call_target="tpu_custom_call" | custom-call | flops 7247757312 | bytes 16121856 | tf_op jit(solution)/shard_map/attn_grad/pallas_call | solution.py:658
  302.3 8.1 %input_grad.3 = bf16[2,512,768]{2,1,0:T(8,128)(2,1)} custom-call(bf16[2,2,512,2304]{3,2,1,0:T(8,128)(2,1)} %get-tuple-element.60.d_ref, bf16[16,160,768]{2,1,0:T(8,128)(2,1)} %bitcast.84), custom_call_target="tpu_custom_call" | custom-call | flops 3623878656 | bytes 8650752 | tf_op jit(solution)/shard_map/input_grad/pallas_call | solution.py:691
  311.0 9.0 %input_grad.2 = f32[2,512,768]{2,1,0:T(8,128)} custom-call(bf16[2,2,512,2304]{3,2,1,0:T(8,128)(2,1)} %get-tuple-element.60.d_ref, bf16[16,160,768]{2,1,0:T(8,128)(2,1)} %bitcast.85), custom_call_target="tpu_custom_call" | custom-call | flops 3623878656 | bytes 8650752 | tf_op jit(solution)/shard_map/input_grad/pallas_call | solution.py:691
  320.0 27.0 %collective-permute-done.4 = bf16[2,512,768]{2,1,0:T(8,128)(2,1)} collective-permute-done((bf16[2,512,768]{2,1,0:T(8,128)(2,1)}, bf16[2,512,768]{2,1,0:T(8,128)(2,1)}, u32[]{:S(2)}, u32[]{:S(2)}) %collective-permute-start.4) | collective-permute-done | bytes 1572896 | tf_op jit(solution)/shard_map/ppermute | solution.py:32
  347.0 4.5 add_bitcast_fusion
  351.5 25.2 %reduce-scatter.3.cloned.1.call-done = bf16[1,160,768]{2,1,0:T(8,128)(2,1)} async-done(((bf16[16,160,768]{2,1,0:T(8,128)(2,1)}), bf16[1,160,768]{2,1,0:T(8,128)(2,1)}) %reduce-scatter.3.cloned.1.call-update) | async-done | bytes 245776 | tf_op jit(solution)/shard_map/reduce_scatter | solution.py:866
  376.7 1.5 collective-permute-start.5
  378.2 1.0 bitcast_convert_fusion
  380.1 3.2 collective-permute-done.5
  384.6 1.3 select_n.98
  387.3 113.1 %reduce-scatter.5.cloned.1.call-done = bf16[1,432,768]{2,1,0:T(8,128)(2,1)} async-done(((bf16[16,432,768]{2,1,0:T(8,128)(2,1)}), bf16[1,432,768]{2,1,0:T(8,128)(2,1)}) %reduce-scatter.5.cloned.1.call-update) | async-done | bytes 663568 | tf_op jit(solution)/shard_map/reduce_scatter | solution.py:830
  500.4 1.5 collective-permute-start.6
  503.1 13.8 %collective-permute-done.6 = bf16[432,768]{1,0:T(8,128)(2,1)S(1)} collective-permute-done((bf16[432,768]{1,0:T(8,128)(2,1)}, bf16[432,768]{1,0:T(8,128)(2,1)S(1)}, u32[]{:S(2)}, u32[]{:S(2)}) %collective-permute-start.6) | collective-permute-done | bytes 663584 | tf_op jit(solution)/shard_map/ppermute | solution.py:32
  516.9 1.2 convert_add_fusion
  518.1 0.9 slice.379
  518.9 0.7 fusion.6
  519.7 0.9 pad_maximum_fusion.2
  (106 shorter events, 13.3 us)
Async XLA Ops:
  7.2 57.8 %copy-start.1 = (bf16[2,1,512,768]{3,2,1,0:T(8,128)(2,1)S(1)}, bf16[2,1,512,768]{3,2,1,0:T(8,128)(2,1)}, u32[]{:S(2)}) copy-start(bf16[2,1,512,768]{3,2,1,0:T(8,128)(2,1)} %param.20) | copy-start | bytes 4718596
  7.2 61.3 %all-gather.5.cloned.1.call-start = ((), (), s32[]{:S(2)}) async-start(), calls=%async_computation.4 | async-start | bytes 4177920 | tf_op jit(solution)/shard_map/all_gather | solution.py:758
  16.5 141.3 %all-gather.7.cloned.1.call-start = ((), (), s32[]{:S(2)}) async-start(), calls=%async_computation.5 | async-start | bytes 11280384 | tf_op jit(solution)/shard_map/all_gather | solution.py:763
  22.0 0.8 copy-start.2
  22.9 353.8 %reduce-scatter.3.cloned.1.call-start = ((), (), s32[]{:S(2)}) async-start(), calls=%async_computation.2 | async-start | bytes 4177920 | tf_op jit(solution)/shard_map/reduce_scatter | solution.py:866
  23.0 42.1 %collective-permute-start.1 = (bf16[2,512,768]{2,1,0:T(8,128)(2,1)}, bf16[2,512,768]{2,1,0:T(8,128)(2,1)S(1)}, u32[]{:S(2)}, u32[]{:S(2)}) collective-permute-start(bf16[2,512,768]{2,1,0:T(8,128)(2,1)} %bitcast.88), channel_id=1, source_target_pairs={{0,16},{16,0},{1,17},{17,1},{2,18},{18,2},{3,19},{19,3},{4,20},{20... | collective-permute-start | bytes 4718600 | tf_op jit(solution)/shard_map/ppermute | solution.py:32
  26.7 34.1 %collective-permute-start = (s32[2,2,512]{2,0,1:T(2,128)S(1)}, s32[2,2,512]{2,0,1:T(2,128)S(1)}, u32[]{:S(2)}, u32[]{:S(2)}) collective-permute-start(s32[2,2,512]{2,0,1:T(2,128)S(1)} %get-tuple-element.161), channel_id=1, source_target_pairs={{0,16},{16,0},{1,17},{17,1},{2,18},{18,2},{3,19},{19,3},{4,20},{20... | collective-permute-start | bytes 24584 | tf_op jit(solution)/shard_map/ppermute | solution.py:32
  60.8 6.1 %copy-start.4 = (s32[2,1,2,512]{3,1,2,0:T(1,128)}, s32[2,1,2,512]{3,1,2,0:T(1,128)S(1)}, u32[]{:S(2)}) copy-start(s32[2,1,2,512]{3,1,2,0:T(1,128)S(1)} %get-tuple-element.131) | copy-start | bytes 24580
  129.9 19.7 %collective-permute-start.2 = (bf16[2,512,384]{2,1,0:T(8,128)(2,1)S(1)}, bf16[2,512,384]{2,1,0:T(8,128)(2,1)S(1)}, u32[]{:S(2)}, u32[]{:S(2)}) collective-permute-start(bf16[2,512,384]{2,1,0:T(8,128)(2,1)S(1)} %get-tuple-element.132), channel_id=1, source_target_pairs={{0,16},{16,0},{1,17},{17,1},{2,18},{18,2},{3,19},{19,3},{4,20},{20... | collective-permute-start | bytes 2359304 | tf_op jit(solution)/shard_map/ppermute | solution.py:32
  149.6 8.2 %copy-start.5 = (bf16[2,512,384]{2,1,0:T(8,128)(2,1)}, bf16[2,512,384]{2,1,0:T(8,128)(2,1)S(1)}, u32[]{:S(2)}) copy-start(bf16[2,512,384]{2,1,0:T(8,128)(2,1)S(1)} %collective-permute-done.2) | copy-start | bytes 2359300
  209.9 21.9 %collective-permute-start.3 = (bf16[1024,384]{1,0:T(8,128)(2,1)}, bf16[1024,384]{1,0:T(8,128)(2,1)S(1)}, u32[]{:S(2)}, u32[]{:S(2)}) collective-permute-start(bf16[1024,384]{1,0:T(8,128)(2,1)} %get-tuple-element.54), channel_id=1, source_target_pairs={{0,16},{16,0},{1,17},{17,1},{2,18},{18,2},{3,19},{19,3},{4,20},{20... | collective-permute-start | bytes 2359304 | tf_op jit(solution)/shard_map/ppermute | solution.py:32
  211.4 20.4 %copy-start.3 = (bf16[1024,384]{1,0:T(8,128)(2,1)S(1)}, bf16[1024,384]{1,0:T(8,128)(2,1)}, u32[]{:S(2)}) copy-start(bf16[1024,384]{1,0:T(8,128)(2,1)} %get-tuple-element.53) | copy-start | bytes 2359300
  301.7 198.7 %reduce-scatter.5.cloned.1.call-start = ((), (), s32[]{:S(2)}) async-start(), calls=%async_computation.3 | async-start | bytes 11280384 | tf_op jit(solution)/shard_map/reduce_scatter | solution.py:830
  310.4 36.6 %copy-start = (f32[1024,768]{1,0:T(8,128)S(1)}, f32[1024,768]{1,0:T(8,128)}, u32[]{:S(2)}) copy-start(f32[1024,768]{1,0:T(8,128)} %get-tuple-element.50) | copy-start | bytes 9437188
  310.4 36.6 %collective-permute-start.4 = (bf16[2,512,768]{2,1,0:T(8,128)(2,1)}, bf16[2,512,768]{2,1,0:T(8,128)(2,1)}, u32[]{:S(2)}, u32[]{:S(2)}) collective-permute-start(bf16[2,512,768]{2,1,0:T(8,128)(2,1)} %input_grad.3), channel_id=1, source_target_pairs={{0,16},{16,0},{1,17},{17,1},{2,18},{18,2},{3,19},{19,3},{4,20},{20... | collective-permute-start | bytes 4718600 | tf_op jit(solution)/shard_map/ppermute | solution.py:32
  376.7 6.5 %collective-permute-start.5 = (bf16[160,768]{1,0:T(8,128)(2,1)}, bf16[160,768]{1,0:T(8,128)(2,1)S(1)}, u32[]{:S(2)}, u32[]{:S(2)}) collective-permute-start(bf16[160,768]{1,0:T(8,128)(2,1)} %bitcast.96), channel_id=1, source_target_pairs={{0,16},{16,0},{1,17},{17,1},{2,18},{18,2},{3,19},{19,3},{4,20},{20... | collective-permute-start | bytes 737288 | tf_op jit(solution)/shard_map/ppermute | solution.py:32
  500.4 16.5 %collective-permute-start.6 = (bf16[432,768]{1,0:T(8,128)(2,1)}, bf16[432,768]{1,0:T(8,128)(2,1)S(1)}, u32[]{:S(2)}, u32[]{:S(2)}) collective-permute-start(bf16[432,768]{1,0:T(8,128)(2,1)} %bitcast.95), channel_id=1, source_target_pairs={{0,16},{16,0},{1,17},{17,1},{2,18},{18,2},{3,19},{19,3},{4,20},{20... | collective-permute-start | bytes 1990664 | tf_op jit(solution)/shard_map/ppermute | solution.py:32
Sparse Core Ops, SparseCore 0:
  16.7 51.7 all-gather.4
  70.8 87.0 all-gather.6
  301.8 74.8 reduce-scatter.2
  380.6 119.6 reduce-scatter.4

commit v3 on v2

--- a/solution.py
+++ b/solution.py
@@ -40,10 +40,9 @@
     return lax.broadcasted_iota(jnp.int32, shape, len(shape) - 1) % 128 < 64
 
 
-def pack_kernel(side_ref, q_ref, k_ref, v_ref, vec_ref, out_ref):
+def pack_into(first, q_ref, k_ref, v_ref, vec, out_ref):
     rows, width = k_ref.shape
     half = width // 2
-    first = side_ref[0] == 0
 
     def own(ref, base):
         return jnp.where(
@@ -65,7 +64,149 @@
             out_ref[e * rows : e * rows + rows, 256 * t + 128 : 256 * t + 256] = odd.astype(bf16)
     out_ref[2 * rows : 3 * rows, :half] = own(k_ref, 0).astype(bf16)
     out_ref[2 * rows : 3 * rows, half:] = own(v_ref, 0).astype(bf16)
-    out_ref[3 * rows :, :] = jnp.broadcast_to(vec_ref[...], (16, width))
+    out_ref[3 * rows :, :] = jnp.broadcast_to(vec, (16, width)).astype(bf16)
+
+
+def spots():
+    x = lax.axis_index("seq")
+    me = lax.axis_index("shard")
+    core = lax.rem(me, 2)
+    y = lax.rem(me // 2, 2)
+    z = me // 4
+    return x, me, z, y, core
+
+
+def slot_of(z, y, core):
+    return z * 4 + y * 2 + core
+
+
+def greet(peers):
+    barrier = pltpu.get_barrier_semaphore()
+    for peer in peers:
+        pl.semaphore_signal(barrier, inc=1, device_id=peer, device_id_type=pl.DeviceIdType.MESH)
+    pl.semaphore_wait(barrier, len(peers))
+
+
+def all_peers():
+    x, me, z, y, core = spots()
+    peers = [(x, slot_of(z, y, 1 - core)), (x, slot_of(z, 1 - y, core)), (1 - x, me)]
+    for step in range(1, 4):
+        peers.append((x, slot_of(lax.rem(z + step, 4), y, core)))
+    return peers
+
+
+def send(src, dst, send_sem, recv_sem, device):
+    return pltpu.make_async_remote_copy(
+        src_ref=src,
+        dst_ref=dst,
+        send_sem=send_sem,
+        recv_sem=recv_sem,
+        device_id=device,
+        device_id_type=pl.DeviceIdType.MESH,
+    )
+
+
+def gather_kernel(*refs):
+    q_ref, k_ref, v_ref = refs[:3]
+    vec_refs = refs[3:13]
+    tok_ref, kinds_ref, groups_ref = refs[13:16]
+    w_ref, tok_out, kinds_out, groups_out = refs[16:20]
+    mine, keep_sem, x_send, x_recv, z_send, z_recv, y_send, y_recv, c_send, c_recv = refs[20:]
+    x, me, z, y, core = spots()
+    across = (1 - x, me)
+    beside = (x, slot_of(z, 1 - y, core))
+    partner = (x, slot_of(z, y, 1 - core))
+    greet(all_peers())
+    over = [
+        send(src, dst, x_send.at[i], x_recv.at[i], across)
+        for i, (src, dst) in enumerate(
+            ((kinds_ref, kinds_out), (groups_ref, groups_out), (tok_ref, tok_out))
+        )
+    ]
+    for copy in over:
+        copy.start()
+    vec = jnp.concatenate([r[...].astype(f32) for r in vec_refs], axis=1)
+    pack_into(x == 0, q_ref, k_ref, v_ref, vec, mine)
+    started = []
+    for step in range(1, 4):
+        copy = send(
+            mine,
+            w_ref.at[me],
+            z_send.at[step - 1],
+            z_recv.at[z],
+            (x, slot_of(lax.rem(z + step, 4), y, core)),
+        )
+        copy.start()
+        started.append(copy)
+    copy = send(mine, w_ref.at[me], y_send.at[z], y_recv.at[z], beside)
+    copy.start()
+    started.append(copy)
+    copy = send(mine, w_ref.at[me], c_send.at[z * 2 + y], c_recv.at[z * 2 + y], partner)
+    copy.start()
+    started.append(copy)
+    keep = pltpu.make_async_copy(mine, w_ref.at[me], keep_sem)
+    keep.start()
+    for step in range(1, 4):
+        zz = lax.rem(z + step, 4)
+        at = slot_of(zz, y, core)
+        held = w_ref.at[at]
+        send(held, held, z_send.at[0], z_recv.at[zz], partner).wait_recv()
+        for copy in (
+            send(held, held, y_send.at[zz], y_recv.at[zz], beside),
+            send(held, held, c_send.at[zz * 2 + y], c_recv.at[zz * 2 + y], partner),
+        ):
+            copy.start()
+            started.append(copy)
+    for step in range(4):
+        zz = lax.rem(z + step, 4)
+        rail = zz * 2 + 1 - y
+        held = w_ref.at[slot_of(zz, 1 - y, core)]
+        send(held, held, y_send.at[0], y_recv.at[zz], partner).wait_recv()
+        copy = send(held, held, c_send.at[rail], c_recv.at[rail], partner)
+        copy.start()
+        started.append(copy)
+    for rail in range(8):
+        held = w_ref.at[2 * rail + 1 - core]
+        send(held, held, c_send.at[0], c_recv.at[rail], partner).wait_recv()
+    keep.wait()
+    for copy in started:
+        copy.wait_send()
+    for copy in over:
+        copy.wait()
+
+
+def gather_attention(query_weight, key_weight, value_weight, vectors, tokens, kinds, groups):
+    rows, width = key_weight.shape
+    vmem = pl.BlockSpec(memory_space=pltpu.VMEM)
+    anywhere = pl.BlockSpec(memory_space=pl.ANY)
+    sem = pltpu.SemaphoreType.DMA
+    return pl.pallas_call(
+        gather_kernel,
+        in_specs=[vmem] * 13 + [anywhere] * 3,
+        out_specs=[anywhere] * 4,
+        out_shape=[
+            jax.ShapeDtypeStruct((GROUPS, 3 * rows + 16, width), bf16),
+            jax.ShapeDtypeStruct(tokens.shape, tokens.dtype),
+            jax.ShapeDtypeStruct(kinds.shape, kinds.dtype),
+            jax.ShapeDtypeStruct(groups.shape, groups.dtype),
+        ],
+        scratch_shapes=[
+            pltpu.VMEM((3 * rows + 16, width), bf16),
+            sem,
+            sem((3,)),
+            sem((3,)),
+            sem((3,)),
+            sem((4,)),
+            sem((4,)),
+            sem((4,)),
+            sem((8,)),
+            sem((8,)),
+        ],
+        compiler_params=pltpu.CompilerParams(
+            collective_id=0, has_side_effects=True, vmem_limit_bytes=VMEM_LIMIT
+        ),
+        name="gather",
+    )(query_weight, key_weight, value_weight, *[v[None] for v in vectors], tokens, kinds, groups)
 
 
 def pair_columns(columns, side, head_dim):
@@ -89,21 +230,38 @@
 
 
 def pack_attention(query_weight, key_weight, value_weight, vector, side, head_dim):
-    rows, width = key_weight.shape
-    if rows % 16 == 0:
-        return pl.pallas_call(
-            pack_kernel,
-            out_shape=jax.ShapeDtypeStruct((3 * rows + 16, width), bf16),
-            in_specs=[pl.BlockSpec(memory_space=pltpu.SMEM)]
-            + [pl.BlockSpec(memory_space=pltpu.VMEM)] * 4,
-            out_specs=pl.BlockSpec(memory_space=pltpu.VMEM),
-            name="pack",
-        )(side[None], query_weight, key_weight, value_weight, vector)
+    width = key_weight.shape[1]
     pairs = pair_columns(query_weight, side, head_dim)
     key_value = jnp.concatenate([own_half(key_weight, side), own_half(value_weight, side)], axis=1)
     return jnp.concatenate(
         [pairs[:, 0], pairs[:, 1], key_value, jnp.broadcast_to(vector, (16, width))], axis=0
     )
+
+
+def pack_feed_kernel(down_ref, output_ref, up_ref, out_ref):
+    rows, width = output_ref.shape
+    out_ref[0 : 4 * rows, :] = down_ref[...]
+    out_ref[4 * rows : 5 * rows, :] = output_ref[...]
+    for j in range(4):
+        out_ref[(5 + j) * rows : (6 + j) * rows, :] = up_ref[:, j * width : j * width + width]
+
+
+def pack_feed(down_weight, output_weight, up_weight):
+    rows, width = output_weight.shape
+    if rows % 16:
+        return jnp.concatenate(
+            [down_weight, output_weight]
+            + [up_weight[:, j * width : j * width + width] for j in range(4)],
+            axis=0,
+        )
+    vmem = pl.BlockSpec(memory_space=pltpu.VMEM)
+    return pl.pallas_call(
+        pack_feed_kernel,
+        in_specs=[vmem] * 3,
+        out_specs=vmem,
+        out_shape=jax.ShapeDtypeStruct((9 * rows, width), bf16),
+        name="pack_feed",
+    )(down_weight, output_weight, up_weight)
 
 
 def regroup(gathered, sizes):
@@ -671,6 +829,197 @@
     )(x, d, vectors)
 
 
+def scatter_kernel(
+    x_ref,
+    d_ref,
+    vec_ref,
+    gq_ref,
+    gk_ref,
+    gv_ref,
+    gvec_ref,
+    part,
+    from_core,
+    from_y,
+    from_z,
+    from_x,
+    out_y,
+    out_z,
+    held,
+    total,
+    c_send,
+    c_recv,
+    y_send,
+    y_recv,
+    z_send,
+    z_recv,
+    x_send,
+    x_recv,
+):
+    width = x_ref.shape[1]
+    half = width // 2
+    rows = width // GROUPS
+    step_at = pl.program_id(0)
+    x, me, z, y, core = spots()
+    across = (1 - x, me)
+    beside = (x, slot_of(z, 1 - y, core))
+    partner = (x, slot_of(z, y, 1 - core))
+    spans = ((0, rows), (rows, rows), (2 * rows, rows + 16))
+
+    def core_copy(chunk, rail):
+        start, size = spans[chunk]
+        return send(
+            part.at[2 * rail + 1 - core, pl.ds(start, size), :],
+            from_core.at[rail, pl.ds(start, size), :],
+            c_send.at[chunk * 8 + rail],
+            c_recv.at[chunk * 8 + rail],
+            partner,
+        )
+
+    @pl.when(step_at == 0)
+    def _():
+        greet(all_peers())
+
+    grad = tn(x_ref[...], d_ref[...]).astype(bf16)
+    for chunk in range(3):
+
+        @pl.when(step_at == chunk)
+        def _(chunk=chunk):
+            start = spans[chunk][0]
+            part[:, start : start + rows, :] = grad.reshape(GROUPS, rows, width)
+            if chunk == 2:
+                part[:, 3 * rows :, :] = vec_ref[...]
+            for rail in range(8):
+                core_copy(chunk, rail).start()
+
+    @pl.when(step_at == 2)
+    def _():
+        def z_order(step):
+            return lax.rem(z + 1 + step, 4)
+
+        def y_copy(zz):
+            return send(out_y.at[zz], from_y.at[zz], y_send.at[zz], y_recv.at[zz], beside)
+
+        def z_copy(zz):
+            return send(
+                out_z.at[zz], from_z.at[z], z_send.at[zz], z_recv.at[z], (x, slot_of(zz, y, core))
+            )
+
+        def core_wait(rail):
+            for chunk in range(3):
+                start, size = spans[chunk]
+                send(
+                    part.at[0, pl.ds(start, size), :],
+                    from_core.at[rail, pl.ds(start, size), :],
+                    c_send.at[0],
+                    c_recv.at[chunk * 8 + rail],
+                    partner,
+                ).wait_recv()
+
+        for step in range(4):
+            zz = z_order(step)
+            rail = zz * 2 + 1 - y
+            core_wait(rail)
+            out_y[zz] = (part[2 * rail + core].astype(f32) + from_core[rail].astype(f32)).astype(bf16)
+            y_copy(zz).start()
+        for step in range(4):
+            zz = z_order(step)
+            rail = zz * 2 + y
+            core_wait(rail)
+            held[zz] = part[2 * rail + core].astype(f32) + from_core[rail].astype(f32)
+        for step in range(3):
+            zz = z_order(step)
+            y_copy(zz).wait_recv()
+            out_z[zz] = (held[zz] + from_y[zz].astype(f32)).astype(bf16)
+            z_copy(zz).start()
+        y_copy(z).wait_recv()
+        result = held[z] + from_y[z].astype(f32)
+        for step in range(3):
+            zz = z_order(step)
+            send(out_z.at[zz], from_z.at[zz], z_send.at[zz], z_recv.at[zz], partner).wait_recv()
+            result = result + from_z[zz].astype(f32)
+        total[...] = result.astype(bf16)
+        last = send(total, from_x, x_send, x_recv, across)
+        last.start()
+        for chunk in range(3):
+            for rail in range(8):
+                core_copy(chunk, rail).wait_send()
+        for step in range(4):
+            y_copy(z_order(step)).wait_send()
+        for step in range(3):
+            z_copy(z_order(step)).wait_send()
+        last.wait()
+        first = x == 0
+        lo = low_lanes((rows, 128))
+
+        def ordered(start, size, at):
+            own = total[start : start + size, at].astype(f32)
+            other = from_x[start : start + size, at].astype(f32)
+            return jnp.where(first, own, other), jnp.where(first, other, own)
+
+        for e in range(2):
+            for t in range(half // 128):
+                evens = ordered(e * rows, rows, slice(256 * t, 256 * t + 128))
+                odds = ordered(e * rows, rows, slice(256 * t + 128, 256 * t + 256))
+                for s in range(2):
+                    word = jnp.where(lo, evens[s], pltpu.roll(odds[s], 64, 1))
+                    entity = jnp.where(lo, pltpu.roll(evens[s], 64, 1), odds[s])
+                    base = 2 * e * width + s * half + 128 * t
+                    gq_ref[:, base : base + 128] = word
+                    gq_ref[:, base + width : base + width + 128] = entity
+        for ref, base in ((gk_ref, 0), (gv_ref, half)):
+            a, b = ordered(2 * rows, rows, slice(base, base + half))
+            ref[:, :half] = a
+            ref[:, half:] = b
+        gvec_ref[...] = total[3 * rows :, :].astype(f32) + from_x[3 * rows :, :].astype(f32)
+
+
+def scatter_attention(x, d, vectors):
+    tokens, width = x.shape
+    rows = width // GROUPS
+    tall = 3 * rows + 16
+    sem = pltpu.SemaphoreType.DMA
+
+    def whole(*dims):
+        return pl.BlockSpec(dims, lambda i: (0,) * len(dims))
+
+    outs = ((rows, 4 * width), (rows, width), (rows, width), (16, width))
+    return pl.pallas_call(
+        scatter_kernel,
+        grid=(3,),
+        in_specs=[
+            whole(tokens, width),
+            pl.BlockSpec((tokens, width), lambda i: (0, i)),
+            whole(GROUPS, 16, width),
+        ],
+        out_specs=[whole(*dims) for dims in outs],
+        out_shape=[jax.ShapeDtypeStruct(dims, f32) for dims in outs],
+        scratch_shapes=[
+            pltpu.VMEM((GROUPS, tall, width), bf16),
+            pltpu.VMEM((8, tall, width), bf16),
+            pltpu.VMEM((4, tall, width), bf16),
+            pltpu.VMEM((4, tall, width), bf16),
+            pltpu.VMEM((tall, width), bf16),
+            pltpu.VMEM((4, tall, width), bf16),
+            pltpu.VMEM((4, tall, width), bf16),
+            pltpu.VMEM((4, tall, width), f32),
+            pltpu.VMEM((tall, width), bf16),
+            sem((24,)),
+            sem((24,)),
+            sem((4,)),
+            sem((4,)),
+            sem((4,)),
+            sem((4,)),
+            sem,
+            sem,
+        ],
+        compiler_params=pltpu.CompilerParams(
+            collective_id=1, has_side_effects=True, vmem_limit_bytes=VMEM_LIMIT
+        ),
+        cost_estimate=cost(2 * tokens * width * width * 3, tokens * width * 8 + width * width * 6),
+        name="scatter",
+    )(x, d, vectors)
+
+
 def input_grad_kernel(d_ref, w_ref, out_ref):
     width = out_ref.shape[1]
     rows = width // GROUPS
@@ -701,6 +1050,30 @@
         cost_estimate=cost(2 * micro * local * wide * width, micro * local * wide * 2 + weights.size * 2),
         name="input_grad",
     )(d, weights)
+
+
+def assemble(attn_own, attn_other, side, head_dim, rows, piece):
+    attn_own, attn_other = attn_own.astype(f32), attn_other.astype(f32)
+    width = attn_own.shape[1]
+    half = width // 2
+    vec_total = attn_own[3 * rows, :piece] + attn_other[3 * rows, :piece]
+
+    def by_side(own, other, axis):
+        return jnp.where(
+            side == 0,
+            jnp.concatenate([own, other], axis=axis),
+            jnp.concatenate([other, own], axis=axis),
+        )
+
+    def query_parts(block):
+        pairs = jnp.stack([block[:rows], block[rows : 2 * rows]], axis=1)
+        return unpair_columns(pairs, head_dim)
+
+    grad_query = by_side(query_parts(attn_own), query_parts(attn_other), 3).reshape(rows, 4 * width)
+    kv_own, kv_other = attn_own[2 * rows : 3 * rows], attn_other[2 * rows : 3 * rows]
+    grad_key = by_side(kv_own[:, :half], kv_other[:, :half], 1)
+    grad_value = by_side(kv_own[:, half:], kv_other[:, half:], 1)
+    return grad_query, grad_key, grad_value, vec_total
 
 
 def on_device(
@@ -733,36 +1106,35 @@
     side = lax.axis_index("seq").astype(jnp.int32)
     per = local // BLOCK
 
-    vector = jnp.concatenate(
-        [
-            query_bias,
-            key_bias,
-            value_bias,
-            output_bias,
-            norm1_gain,
-            norm1_shift,
-            up_bias,
-            down_bias,
-            norm2_gain,
-            norm2_shift,
-        ]
+    vectors = (
+        query_bias,
+        key_bias,
+        value_bias,
+        output_bias,
+        norm1_gain,
+        norm1_shift,
+        up_bias,
+        down_bias,
+        norm2_gain,
+        norm2_shift,
     )
-    piece = vector.shape[0]
-    vector_row = jnp.pad(vector, (0, width - piece))[None]
+    piece = 16 * rows
+    direct = devices == GROUPS
     attn_sizes = (rows, rows, rows)
     feed_sizes = (4 * rows,) + (rows,) * 5
-    packed = pack_attention(query_weight, key_weight, value_weight, vector_row, side, head_dim)
-    packed, down_weight, output_weight, up_weight = lax.optimization_barrier(
-        (packed, down_weight, output_weight, up_weight)
-    )
-    attn_gathered = lax.all_gather(packed[None], "shard", axis=0, tiled=True)
-    feed_local = jnp.concatenate(
-        [down_weight, output_weight] + [up_weight[:, j * width : j * width + width] for j in range(4)],
-        axis=0,
-    )
+    if not direct:
+        vector_row = jnp.pad(jnp.concatenate(vectors), (0, width - piece))[None]
+        packed = pack_attention(query_weight, key_weight, value_weight, vector_row, side, head_dim)
+        attn_gathered = lax.all_gather(packed[None], "shard", axis=0, tiled=True)
+        other_tokens, other_kinds, other_groups = swap(tokens), swap(kinds), swap(groups)
+    feed_local = pack_feed(down_weight, output_weight, up_weight)
     feed_gathered = lax.all_gather(feed_local[None], "shard", axis=0, tiled=True)
+    if direct:
+        attn_gathered, other_tokens, other_kinds, other_groups = gather_attention(
+            query_weight, key_weight, value_weight, vectors, tokens, kinds, groups
+        )
     vectors = attn_gathered[:, 3 * rows, :piece]
-    if devices == GROUPS:
+    if direct:
         attn_w, feed_w = attn_gathered, feed_gathered
     else:
         attn_w = regroup(attn_gathered, attn_sizes)
@@ -796,10 +1168,9 @@
     )
 
     own_tokens = tokens[:, 0]
-    marks = jnp.stack([kinds[:, 0], groups[:, 0]])
-    xs = jnp.stack([own_tokens, swap(own_tokens)])
-    both_marks = jnp.stack([marks, swap(marks)])
-    kind_all, group_all = both_marks[:, 0], both_marks[:, 1]
+    xs = jnp.stack([own_tokens, other_tokens[:, 0]])
+    kind_all = jnp.stack([kinds[:, 0], other_kinds[:, 0]])
+    group_all = jnp.stack([groups[:, 0], other_groups[:, 0]])
     kind_col = kind_all[..., None]
     gk = group_all[..., None]
     gq = group_all[:, :, None, :]
@@ -855,17 +1226,23 @@
         axis=1,
     ).astype(bf16)
     grad_vectors = jnp.pad(grad_vectors[:, None, :], ((0, 0), (0, 15), (0, width - piece)))
-    if devices == GROUPS:
-        attn_part = attn_grad(xs.reshape(2 * flat, width), d.reshape(2 * flat, 3 * width), grad_vectors)
+    dx_other = input_grad_part(d, attn_w, 1, bf16)
+    flat_x = xs.reshape(2 * flat, width)
+    flat_d = d.reshape(2 * flat, 3 * width)
+    if direct:
+        grad_query, grad_key, grad_value, vec_rows = scatter_attention(flat_x, flat_d, grad_vectors)
+        vec_total = vec_rows[0, :piece]
     else:
         zeros = jnp.zeros((GROUPS, 16, width), bf16)
-        attn_part = attn_grad(xs.reshape(2 * flat, width), d.reshape(2 * flat, 3 * width), zeros)
+        attn_part = attn_grad(flat_x, flat_d, zeros)
         attn_part = jnp.concatenate(
             [ungroup(attn_part[:, : 3 * (width // GROUPS)], attn_sizes, devices), grad_vectors], axis=1
         )
-    attn_sum = lax.psum_scatter(attn_part, "shard", scatter_dimension=0, tiled=True)[0]
-
-    dx_other = input_grad_part(d, attn_w, 1, bf16)
+        attn_sum = lax.psum_scatter(attn_part, "shard", scatter_dimension=0, tiled=True)[0]
+        attn_other = swap(attn_sum)
+        grad_query, grad_key, grad_value, vec_total = assemble(
+            attn_sum, attn_other, side, head_dim, rows, piece
+        )
     dx_own = input_grad_part(d, attn_w, 0, f32)
     input_grad = dh1.reshape(micro, local, width) + dx_own + swap(dx_other).astype(f32)
 
@@ -875,25 +1252,6 @@
     grad_up = jnp.concatenate(
         [feed_total[(5 + j) * rows : (6 + j) * rows] for j in range(4)], axis=1
     )
-    attn_own = attn_sum.astype(f32)
-    attn_other = swap(attn_sum).astype(f32)
-    vec_total = attn_own[3 * rows, :piece] + attn_other[3 * rows, :piece]
-
-    def by_side(own, other, axis):
-        return jnp.where(
-            side == 0,
-            jnp.concatenate([own, other], axis=axis),
-            jnp.concatenate([other, own], axis=axis),
-        )
-
-    def query_parts(block):
-        pairs = jnp.stack([block[:rows], block[rows : 2 * rows]], axis=1)
-        return unpair_columns(pairs, head_dim)
-
-    grad_query = by_side(query_parts(attn_own), query_parts(attn_other), 3).reshape(rows, 4 * width)
-    kv_own, kv_other = attn_own[2 * rows : 3 * rows], attn_other[2 * rows : 3 * rows]
-    grad_key = by_side(kv_own[:, :half], kv_other[:, :half], 1)
-    grad_value = by_side(kv_own[:, half:], kv_other[:, half:], 1)
 
     def piece_of(start, size):
         return vec_total[start : start + size]

time: 528 us -> 437 us (0.83); the launches traced: 527 us -> 430 us
  waiting for transfers between devices: 243 us -> 26.7 us
  Pallas kernels: 212 us -> 348 us
  local copies, waits for them, and re-layouts: 32.4 us -> 24.7 us
  starting transfers between devices: 9.72 us -> 3.89 us
    pallas_call x2 -> x3, Pallas kernels: 14.7 us -> 151 us  [the longest x1 96.5 us: scatter_attention(): pl.pallas_call(scatter_kernel, grid=(3,), in_specs=[whole(tokens, width),...]
    reduce_scatter x1, waiting for transfers between devices: 113 us -> 0.01 us  [on_device(): lax.psum_scatter(feed_part, 'shard', scatter_dimension=0, tiled=True)[0]]
    ppermute x7 -> x4, waiting for transfers between devices: 94.8 us -> 26.7 us  [swap(): return lax.ppermute(value, 'seq', [(0, 1), (1, 0)])]
    reduce_scatter x1 -> x0, waiting for transfers between devices: 25.2 us -> none  [on_device(): lax.psum_scatter(attn_part, 'shard', scatter_dimension=0, tiled=True)[0]]
    all_gather x1, waiting for transfers between devices: 8.2 us -> 0.01 us  [on_device(): lax.all_gather(feed_local[None], 'shard', axis=0, tiled=True)]
    concatenate x2 -> x0, local copies, waits for them, and re-layouts: 7.75 us -> none  [the longest x1 6.86 us: on_device(): jnp.concatenate([query_bias, key_bias, value_bias, output_bias, norm1_gai...]
    ppermute x7 -> x4, starting transfers between devices: 9.56 us -> 3.81 us  [swap(): return lax.ppermute(value, 'seq', [(0, 1), (1, 0)])]
  transfers between devices with their start and end apart: 11 -> 6, of which waited for: 9 -> 2; matrix products, arithmetic and copies ran while one was open for 6% -> 7% of each run, Pallas kernels for 18% -> 69%
where the time goes in v3:
time: 437 us; the launch traced here: 430 us
  Pallas kernels  348 us (80%)
  waiting for transfers between devices  26.7 us (6%)
  local copies, waits for them, and re-layouts  24.7 us (6%)
  between operations  14.3 us (3%)
  other arithmetic  12.6 us (3%)
    pallas_call x1, Pallas kernels, scatter_attention(): pl.pallas_call(scatter_kernel, grid=(3,), in_specs=[whole(tokens, width),...  96.5 us
    pallas_call x1, Pallas kernels, attend_back(): pl.pallas_call(attend_back_kernel, grid_spec=pltpu.PrefetchScalarGridSpec...  52.5 us
    pallas_call x1, Pallas kernels, gather_attention(): pl.pallas_call(gather_kernel, in_specs=[vmem] * 13 + [anywhere] * 3, out_...  52 us
    pallas_call x1, Pallas kernels, chain(): pl.pallas_call(chain_kernel, grid_spec=pltpu.PrefetchScalarGridSpec(num_s...  50.6 us
    pallas_call x1, Pallas kernels, attend(): pl.pallas_call(attend_kernel, grid_spec=pltpu.PrefetchScalarGridSpec(num_...  42.5 us
    ppermute x4, waiting for transfers between devices, swap(): return lax.ppermute(value, 'seq', [(0, 1), (1, 0)])  26.7 us
    pallas_call x1, Pallas kernels, feed_grad(): pl.pallas_call(feed_grad_kernel, grid=(9,), in_specs=[pl.BlockSpec((token...  20.3 us
    pallas_call x2, Pallas kernels, input_grad_part(): pl.pallas_call(input_grad_kernel, grid=(micro, sub), in_specs=[pl.BlockSp...  16.7 us
  transfers between devices with their start and end apart: 6, of which 2 were waited for; matrix products, arithmetic and copies ran while one was open for 7% of the time, Pallas kernels for 69%

profile of v3, /device:TPU:0, one launch (start us, length us, event | category | flops | bytes accessed | tf_op | source)
XLA Modules:
  0.0 430.0 jit_solution(15613124140425821860)
XLA Ops:
  7.3 2.1 pack_feed.1
  9.5 1.2 broadcast_in_dim.60.refs_3_
  10.7 1.2 broadcast_in_dim.66.refs_9_
  11.9 0.7 reduce
  12.6 52.0 %gather.1 = (bf16[16,160,768]{2,1,0:T(8,128)(2,1)}, bf16[2,1,512,768]{3,2,1,0:T(8,128)(2,1)}, s32[2,1,512]{2,1,0:T(1,128)}, s32[2,1,512]{2,1,0:T(1,128)}) custom-call(bf16[48,3072]{1,0:T(8,128)(2,1)} %refs_0_.1, bf16[48,768]{1,0:T(8,128)(2,1)} %refs_1_.1, bf16[48,768]{1,0:T(8,128)(2,1)} %refs_2_.1, bf16[1,192]{1,0:T(2,128)(2,1)} %broadcast_in_dim.60.refs_3_, ...), custom_call_target="tpu_custom_call" | custom-call | tf_op jit(solution)/shard_map/gather/pallas_call | solution.py:183
  64.6 0.8 reduce.1
  65.5 0.3 slice_reduce_fusion.1
  65.8 0.6 reshape.353.high_ref
  66.4 0.6 reshape.352.low_ref
  67.0 0.7 copy_bitcast_fusion.2
  67.7 0.6 broadcast_in_dim.73.gq_ref
  68.3 1.0 slice.207
  69.9 0.7 add_bitcast_fusion.1
  70.6 1.4 copy.96.kind_ref
  72.0 1.3 copy.97.gk_ref
  73.3 0.6 pad_maximum_fusion.3.bias_ref
  73.9 1.9 pad_maximum_fusion.x_ref
  75.9 14.5 %project.1 = (bf16[2,2,512,768]{3,2,1,0:T(8,128)(2,1)}, bf16[2,2,512,768]{3,2,1,0:T(8,128)(2,1)}, bf16[2,2,768,512]{3,2,1,0:T(8,128)(2,1)}, bf16[2,2,512,384]{3,2,1,0:T(8,128)(2,1)}, bf16[2,2,384,512]{3,2,1,0:T(8,128)(2,1)}) custom-call(bf16[2,2,512,768]{3,2,1,0:T(8,128)(2,1)} %pad_maximum_fusion.x_ref, bf16[16,160,768]{2,1,0:T(8,128)(2,1)} %get-tuple-element.47.w_ref, ...), custom_call_target="tpu_custom_call" | custom-call | flops 7247757312 | bytes 15728640 | tf_op jit(solution)/shard_map/project/pallas_call | solution.py:334
  90.4 42.5 %attend.1 = (bf16[2,2,512,384]{3,2,1,0:T(8,128)(2,1)}, f32[2,384,1024]{2,1,0:T(8,128)}, f32[2,8,1024]{2,1,0:T(8,128)}) custom-call(s32[8]{0:T(128)} %reshape.352.low_ref, s32[8]{0:T(128)} %reshape.353.high_ref, bf16[2,2,512,768]{3,2,1,0:T(8,128)(2,1)} %get-tuple-element.49.qp_ref, bf16[2,2,512,768]{3,2,1,0:T(8,128)(2,1)} %get-tuple-element.50.km_ref, ...), custom_call_target="tpu_custom_call" | custom-call | flops 6442450944 | bytes 12582912 | tf_op jit(solution)/shard_map/attend/pallas_call | solution.py:419
  132.9 2.4 slice_bitcast_fusion
  135.3 2.1 collective-permute-start
  138.1 0.6 concatenate.99.vec_ref
  138.7 16.7 %collective-permute-done = bf16[2,512,384]{2,1,0:T(8,128)(2,1)S(1)} collective-permute-done((bf16[2,512,384]{2,1,0:T(8,128)(2,1)S(1)}, bf16[2,512,384]{2,1,0:T(8,128)(2,1)S(1)}, u32[]{:S(2)}, u32[]{:S(2)}) %collective-permute-start) | collective-permute-done | bytes 786464 | tf_op jit(solution)/shard_map/ppermute | solution.py:32
  155.4 0.9 copy-done.11
  156.3 50.6 %chain.1 = (bf16[1024,768]{1,0:T(8,128)(2,1)}, f32[1024,768]{1,0:T(8,128)}, bf16[1024,4608]{1,0:T(8,128)(2,1)}, bf16[1024,4608]{1,0:T(8,128)(2,1)}, bf16[1024,38...) custom-call(s32[1]{0:T(128)} %bitcast.side_ref, bf16[1024,768]{1,0:T(8,128)(2,1)} %bitcast.75, ...), custom_call_target="tpu_custom_call" | custom-call | flops 22951231488 | bytes 38928384 | tf_op jit(solution)/shard_map/chain/pallas_call | solution.py:718
  206.9 1.8 collective-permute-start.1
  208.6 20.3 %feed_grad.1 = bf16[16,432,768]{2,1,0:T(8,128)(2,1)} custom-call(bf16[1024,4608]{1,0:T(8,128)(2,1)} %get-tuple-element.59.l_ref, bf16[1024,4608]{1,0:T(8,128)(2,1)} %get-tuple-element.60.r_ref), custom_call_target="tpu_custom_call" | custom-call | flops 10871635968 | bytes 29491200 | tf_op jit(solution)/shard_map/feed_grad/pallas_call | solution.py:788
  229.0 0.8 copy-done.8
  230.5 1.3 pad_maximum_fusion.1.dc_ref
  231.8 52.5 %attend_back.1 = (bf16[2,2,512,2304]{3,2,1,0:T(8,128)(2,1)}, f32[8,2304]{1,0:T(8,128)}) custom-call(s32[8]{0:T(128)} %reshape.352.low_ref, s32[8]{0:T(128)} %reshape.353.high_ref, bf16[2,2,512,768]{3,2,1,0:T(8,128)(2,1)} %get-tuple-element.49.qp_ref, bf16[2,2,512,768]{3,2,1,0:T(8,128)(2,1)} %get-tuple-element.50.km_ref, ...), custom_call_target="tpu_custom_call" | custom-call | flops 16106127360 | bytes 25165824 | tf_op jit(solution)/shard_map/attend_back/pallas_call | solution.py:554
  284.3 0.8 slice_reduce_fusion
  285.8 0.7 slice_reduce_fusion.13
  286.7 8.1 %input_grad.3 = bf16[2,512,768]{2,1,0:T(8,128)(2,1)} custom-call(bf16[2,2,512,2304]{3,2,1,0:T(8,128)(2,1)} %get-tuple-element.64.d_ref, bf16[16,160,768]{2,1,0:T(8,128)(2,1)} %get-tuple-element.47.w_ref), custom_call_target="tpu_custom_call" | custom-call | flops 3623878656 | bytes 8650752 | tf_op jit(solution)/shard_map/input_grad/pallas_call | solution.py:1040
  294.9 0.3 concatenate.127
  295.2 0.8 pad.16.vec_ref
  296.0 96.5 %scatter.1 = (f32[48,3072]{1,0:T(8,128)}, f32[48,768]{1,0:T(8,128)}, f32[48,768]{1,0:T(8,128)}, f32[16,768]{1,0:T(8,128)}) custom-call(bf16[2048,768]{1,0:T(8,128)(2,1)} %bitcast.77, bf16[2048,2304]{1,0:T(8,128)(2,1)} %bitcast.74, bf16[16,16,768]{2,1,0:T(8,128)(2,1)} %pad.16.vec_ref), custom_call_target="tpu_custom_call" | custom-call | flops 7247757312 | bytes 16121856 | tf_op jit(solution)/shard_map/scatter/pallas_call | solution.py:986
  392.5 1.4 fusion.3
  393.9 8.5 %input_grad.2 = f32[2,512,768]{2,1,0:T(8,128)} custom-call(bf16[2,2,512,2304]{3,2,1,0:T(8,128)(2,1)} %get-tuple-element.64.d_ref, bf16[16,160,768]{2,1,0:T(8,128)(2,1)} %get-tuple-element.47.w_ref), custom_call_target="tpu_custom_call" | custom-call | flops 3623878656 | bytes 8650752 | tf_op jit(solution)/shard_map/input_grad/pallas_call | solution.py:1040
  402.4 1.4 slice_bitcast_fusion.1
  403.8 4.6 %add_bitcast_fusion = f32[2,1,512,768]{3,2,1,0:T(8,128)} fusion(bf16[2,512,768]{2,1,0:T(8,128)(2,1)} %collective-permute-done.2, f32[2,512,768]{2,1,0:T(8,128)S(1)} %bitcast.78, f32[2,512,768]{2,1,0:T(8,128)} %input_grad.2), kind=kLoop, calls=%fused_computation.1 | loop fusion | flops 2359296 | bytes 11010048
  408.4 10.0 %collective-permute-done.3 = bf16[432,768]{1,0:T(8,128)(2,1)S(1)} collective-permute-done((bf16[432,768]{1,0:T(8,128)(2,1)}, bf16[432,768]{1,0:T(8,128)(2,1)S(1)}, u32[]{:S(2)}, u32[]{:S(2)}) %collective-permute-start.3) | collective-permute-done | bytes 663584 | tf_op jit(solution)/shard_map/ppermute | solution.py:32
  418.4 0.2 convert_add_fusion
  418.6 0.9 slice.300
  419.4 0.7 fusion.2
  420.2 0.9 pad_maximum_fusion.2
  421.0 0.8 copy.128
  421.8 0.7 copy.129
  422.5 0.7 copy.130
  (87 shorter events, 2.9 us)
Async XLA Ops:
  7.2 59.8 %copy-start.9 = (s32[2,1,512]{2,1,0:T(1,128)S(1)}, s32[2,1,512]{2,1,0:T(1,128)}, u32[]{:S(2)}) copy-start(s32[2,1,512]{2,1,0:T(1,128)} %refs_15_.1) | copy-start | bytes 12292
  7.2 66.7 %copy-start = (bf16[2,1,512,768]{3,2,1,0:T(8,128)(2,1)S(1)}, bf16[2,1,512,768]{3,2,1,0:T(8,128)(2,1)}, u32[]{:S(2)}) copy-start(bf16[2,1,512,768]{3,2,1,0:T(8,128)(2,1)} %refs_13_.1) | copy-start | bytes 4718596
  7.2 62.7 %copy-start.10 = (s32[2,1,512]{2,1,0:T(1,128)S(1)}, s32[2,1,512]{2,1,0:T(1,128)}, u32[]{:S(2)}) copy-start(s32[2,1,512]{2,1,0:T(1,128)} %refs_14_.1) | copy-start | bytes 12292
  7.2 148.2 %all-gather.3.cloned.1.call-start = ((), (), s32[]{:S(2)}) async-start(), calls=%async_computation.2 | async-start | bytes 11280384 | tf_op jit(solution)/shard_map/all_gather | solution.py:1131
  9.4 393.0 %reduce-scatter.2.cloned.1.call-start = ((), (), s32[]{:S(2)}) async-start(), calls=%async_computation.1 | async-start | bytes 11280384 | tf_op jit(solution)/shard_map/reduce_scatter | solution.py:1201
  64.6 9.3 %copy-start.2 = (bf16[2,1,512,768]{3,2,1,0:T(8,128)(2,1)S(1)}, bf16[2,1,512,768]{3,2,1,0:T(8,128)(2,1)}, u32[]{:S(2)}) copy-start(bf16[2,1,512,768]{3,2,1,0:T(8,128)(2,1)} %get-tuple-element.46) | copy-start | bytes 4718596
  135.3 20.1 %collective-permute-start = (bf16[2,512,384]{2,1,0:T(8,128)(2,1)S(1)}, bf16[2,512,384]{2,1,0:T(8,128)(2,1)S(1)}, u32[]{:S(2)}, u32[]{:S(2)}) collective-permute-start(bf16[2,512,384]{2,1,0:T(8,128)(2,1)S(1)} %get-tuple-element.158), channel_id=1, source_target_pairs={{0,16},{16,0},{1,17},{17,1},{2,18},{18,2},{3,19},{19,3},{4,20},{20... | collective-permute-start | bytes 2359304 | tf_op jit(solution)/shard_map/ppermute | solution.py:32
  155.4 0.9 copy-start.11
  206.9 22.1 %collective-permute-start.1 = (bf16[1024,384]{1,0:T(8,128)(2,1)}, bf16[1024,384]{1,0:T(8,128)(2,1)S(1)}, u32[]{:S(2)}, u32[]{:S(2)}) collective-permute-start(bf16[1024,384]{1,0:T(8,128)(2,1)} %get-tuple-element.58), channel_id=1, source_target_pairs={{0,16},{16,0},{1,17},{17,1},{2,18},{18,2},{3,19},{19,3},{4,20},{20... | collective-permute-start | bytes 2359304 | tf_op jit(solution)/shard_map/ppermute | solution.py:32
  229.0 0.8 copy-start.8
  229.0 1.5 copy-start.3
  294.8 109.0 %collective-permute-start.2 = (bf16[2,512,768]{2,1,0:T(8,128)(2,1)}, bf16[2,512,768]{2,1,0:T(8,128)(2,1)}, u32[]{:S(2)}, u32[]{:S(2)}) collective-permute-start(bf16[2,512,768]{2,1,0:T(8,128)(2,1)} %input_grad.3), channel_id=1, source_target_pairs={{0,16},{16,0},{1,17},{17,1},{2,18},{18,2},{3,19},{19,3},{4,20},{20... | collective-permute-start | bytes 4718600 | tf_op jit(solution)/shard_map/ppermute | solution.py:32
  393.9 10.0 %copy-start.1 = (f32[1024,768]{1,0:T(8,128)S(1)}, f32[1024,768]{1,0:T(8,128)}, u32[]{:S(2)}) copy-start(f32[1024,768]{1,0:T(8,128)} %get-tuple-element.54) | copy-start | bytes 9437188
  402.4 16.0 %collective-permute-start.3 = (bf16[432,768]{1,0:T(8,128)(2,1)}, bf16[432,768]{1,0:T(8,128)(2,1)S(1)}, u32[]{:S(2)}, u32[]{:S(2)}) collective-permute-start(bf16[432,768]{1,0:T(8,128)(2,1)} %bitcast.83), channel_id=1, source_target_pairs={{0,16},{16,0},{1,17},{17,1},{2,18},{18,2},{3,19},{19,3},{4,20},{20... | collective-permute-start | bytes 1990664 | tf_op jit(solution)/shard_map/ppermute | solution.py:32
  403.8 14.6 %copy-start.4 = (bf16[1,432,768]{2,1,0:T(8,128)(2,1)S(1)}, bf16[1,432,768]{2,1,0:T(8,128)(2,1)}, u32[]{:S(2)}) copy-start(bf16[1,432,768]{2,1,0:T(8,128)(2,1)} %reduce-scatter.2.cloned.1.call-done) | copy-start | bytes 1990660
  408.4 12.6 %copy-start.5 = (f32[48,3072]{1,0:T(8,128)S(1)}, f32[48,3072]{1,0:T(8,128)}, u32[]{:S(2)}) copy-start(f32[48,3072]{1,0:T(8,128)} %get-tuple-element.211) | copy-start | bytes 1769476
  418.6 3.3 copy-start.7
  418.6 3.9 copy-start.6
Sparse Core Ops, SparseCore 0:
  10.3 110.1 all-gather.2
  229.2 162.4 reduce-scatter.1

commit v4 on v3

--- a/solution.py
+++ b/solution.py
@@ -286,12 +286,41 @@
     return jnp.concatenate(pieces, axis=1)
 
 
-def project_kernel(x_ref, w_ref, bias_ref, kind_ref, qp_ref, km_ref, kmt_ref, v_ref, vt_ref):
-    width = x_ref.shape[1]
+def project_kernel(
+    own_ref,
+    other_ref,
+    own_kind_ref,
+    other_kind_ref,
+    own_group_ref,
+    other_group_ref,
+    w_ref,
+    bias_ref,
+    qp_ref,
+    km_ref,
+    kmt_ref,
+    v_ref,
+    vt_ref,
+    xs_ref,
+    kind_ref,
+    gk_ref,
+    gq_ref,
+):
+    width = own_ref.shape[1]
     half = width // 2
     rows = width // GROUPS
-    x = x_ref[...]
-    kind = kind_ref[...]
+    mine = pl.program_id(0) == 0
+
+    def column(row):
+        return jnp.broadcast_to(row.astype(f32), (128, BLOCK)).T.astype(jnp.int32)
+
+    x = jnp.where(mine, own_ref[...].astype(f32), other_ref[...].astype(f32)).astype(bf16)
+    group = jnp.where(mine, own_group_ref[...], other_group_ref[...])
+    kinds = column(jnp.where(mine, own_kind_ref[...], other_kind_ref[...]))
+    kind = kinds[:, 0:1]
+    xs_ref[...] = x
+    kind_ref[...] = kind
+    gk_ref[...] = column(group)[:, 0:1]
+    gq_ref[...] = group
     wa = w_ref[:, 0:rows, :].reshape(width, width)
     wb = w_ref[:, rows : 2 * rows, :].reshape(width, width)
     wkv = w_ref[:, 2 * rows : 3 * rows, :].reshape(width, width)
@@ -300,7 +329,7 @@
     qp_ref[...] = (jnp.where(kind == 1, qb, qa) * 0.125).astype(bf16)
     kv = nn(x, wkv) + bias_ref[2:3, :]
     lane_high = (lax.broadcasted_iota(jnp.int32, (BLOCK, 128), 1) >= 64).astype(jnp.int32)
-    keep = lane_high == kind
+    keep = lane_high == kinds
     lo = lane_high == 0
     for t in range(half // 128):
         k = kv[:, 128 * t : 128 * t + 128]
@@ -316,8 +345,9 @@
     vt_ref[...] = v.T.astype(bf16)
 
 
-def project(xs, weights, bias_rows, kind_col):
-    halves, micro, local, width = xs.shape
+def project(tokens, other_tokens, kinds, other_kinds, groups, other_groups, weights, bias_rows):
+    micro, _, local, width = tokens.shape
+    halves = 2
     half = width // 2
     sub = local // BLOCK
 
@@ -327,46 +357,86 @@
     def cols_spec(count):
         return pl.BlockSpec((None, None, count, BLOCK), lambda a, m, i: (a, m, 0, i))
 
-    def shape(*dims):
-        return jax.ShapeDtypeStruct((halves, micro) + dims, bf16)
-
-    tokens = halves * micro * local
+    def shape(*dims, kind=bf16):
+        return jax.ShapeDtypeStruct((halves, micro) + dims, kind)
+
+    def pick(own, a, index, stop):
+        return jnp.where(a == 0, index, stop) if own else jnp.where(a == 0, 0, index)
+
+    def token_spec(own):
+        return pl.BlockSpec(
+            (None, None, BLOCK, width),
+            lambda a, m, i: (pick(own, a, m, micro - 1), 0, pick(own, a, i, sub - 1), 0),
+        )
+
+    def mark_spec(own):
+        return pl.BlockSpec(
+            (None, 1, BLOCK),
+            lambda a, m, i: (pick(own, a, m, micro - 1), 0, pick(own, a, i, sub - 1)),
+        )
+
+    count = halves * micro * local
     return pl.pallas_call(
         project_kernel,
         grid=(halves, micro, sub),
         in_specs=[
-            rows_spec(width),
+            token_spec(True),
+            token_spec(False),
+            mark_spec(True),
+            mark_spec(False),
+            mark_spec(True),
+            mark_spec(False),
             pl.BlockSpec(weights.shape, lambda a, m, i: (0, 0, 0)),
             pl.BlockSpec(bias_rows.shape, lambda a, m, i: (0, 0)),
+        ],
+        out_specs=[
+            rows_spec(width),
+            rows_spec(width),
+            cols_spec(width),
+            rows_spec(half),
+            cols_spec(half),
+            rows_spec(width),
             rows_spec(1),
-        ],
-        out_specs=[rows_spec(width), rows_spec(width), cols_spec(width), rows_spec(half), cols_spec(half)],
+            rows_spec(1),
+            cols_spec(1),
+        ],
         out_shape=[
             shape(local, width),
             shape(local, width),
             shape(width, local),
             shape(local, half),
             shape(half, local),
+            shape(local, width),
+            shape(local, 1, kind=jnp.int32),
+            shape(local, 1, kind=jnp.int32),
+            shape(1, local, kind=jnp.int32),
         ],
         compiler_params=pltpu.CompilerParams(vmem_limit_bytes=VMEM_LIMIT),
-        cost_estimate=cost(2 * tokens * width * 3 * width, tokens * width * 10),
+        cost_estimate=cost(2 * count * width * 3 * width, count * width * 10),
         name="project",
-    )(xs, weights, bias_rows, kind_col)
+    )(tokens, other_tokens, kinds, other_kinds, groups, other_groups, weights, bias_rows)
 
 
 def place(block, per):
     return block // per, pl.multiple_of(lax.rem(block, per) * BLOCK, BLOCK)
 
 
+def ends_of(own_ref, other_ref, micro_at, block, per):
+    at = lax.rem(block, per) * BLOCK
+    mine = block < per
+    first = jnp.where(mine, own_ref[micro_at, at], other_ref[micro_at, at])
+    last_at = at + BLOCK - 1
+    return first, jnp.where(mine, own_ref[micro_at, last_at], other_ref[micro_at, last_at])
+
+
 def attend_kernel(
-    low_ref, high_ref, qp_ref, km_ref, vt_ref, gk_ref, gq_ref, c_ref, ct_ref, lse_ref, m_sc, l_sc, acc_sc
+    own_ref, other_ref, qp_ref, km_ref, vt_ref, gk_ref, gq_ref, c_ref, ct_ref, lse_ref, m_sc, l_sc, acc_sc
 ):
     micro_at = pl.program_id(0)
     local = qp_ref.shape[1]
     per = local // BLOCK
     blocks = 2 * per
     heads = qp_ref.shape[2] // 128
-    base = micro_at * blocks
 
     @pl.loop(0, blocks)
     def _(qb):
@@ -374,11 +444,13 @@
         m_sc[...] = jnp.full_like(m_sc, masked_score)
         l_sc[...] = jnp.zeros_like(l_sc)
         acc_sc[...] = jnp.zeros_like(acc_sc)
-        q_low, q_high = low_ref[base + qb], high_ref[base + qb]
+        q_low, q_high = ends_of(own_ref, other_ref, micro_at, qb, per)
 
         @pl.loop(0, blocks)
         def _(kb):
-            @pl.when((q_low <= high_ref[base + kb]) & (low_ref[base + kb] <= q_high))
+            k_low, k_high = ends_of(own_ref, other_ref, micro_at, kb, per)
+
+            @pl.when((q_low <= k_high) & (k_low <= q_high))
             def _():
                 kh, ko = place(kb, per)
                 same = gk_ref[kh, pl.ds(ko, BLOCK), :] == gq_ref[qh, :, pl.ds(qo, BLOCK)]
@@ -411,7 +483,7 @@
     return pl.BlockSpec((array.shape[0], None) + rest, lambda m, *_: (0, m) + (0,) * len(rest))
 
 
-def attend(low, high, qp, km, vt, gk, gq):
+def attend(own_groups, other_groups, qp, km, vt, gk, gq):
     halves, micro, local, width = qp.shape
     half = width // 2
     heads = width // 128
@@ -443,12 +515,12 @@
             micro * heads * length * length * 512, micro * length * width * 8, micro * heads * length * length
         ),
         name="attend",
-    )(low, high, qp, km, vt, gk, gq)
+    )(own_groups, other_groups, qp, km, vt, gk, gq)
 
 
 def attend_back_kernel(
-    low_ref,
-    high_ref,
+    own_ref,
+    other_ref,
     qp_ref,
     km_ref,
     kmt_ref,
@@ -472,7 +544,6 @@
     per = local // BLOCK
     blocks = 2 * per
     tiles = half // 128
-    base = micro_at * blocks
     dk_sc[...] = jnp.zeros_like(dk_sc)
     dv_sc[...] = jnp.zeros_like(dv_sc)
 
@@ -492,11 +563,13 @@
         for h in range(2 * tiles):
             delta_sc[h : h + 1, :] = jnp.sum(inner[64 * h : 64 * h + 64, :], axis=0, keepdims=True)
         dqt_sc[...] = jnp.zeros_like(dqt_sc)
-        q_low, q_high = low_ref[base + qb], high_ref[base + qb]
+        q_low, q_high = ends_of(own_ref, other_ref, micro_at, qb, per)
 
         @pl.loop(0, blocks)
         def _(kb):
-            @pl.when((q_low <= high_ref[base + kb]) & (low_ref[base + kb] <= q_high))
+            k_low, k_high = ends_of(own_ref, other_ref, micro_at, kb, per)
+
+            @pl.when((q_low <= k_high) & (k_low <= q_high))
             def _():
                 kh, ko = place(kb, per)
                 krows = pl.ds(ko, BLOCK)
@@ -546,7 +619,7 @@
         db_ref[0:1, :] += jnp.sum(d_ref[kh, krows, :].astype(f32), axis=0, keepdims=True)
 
 
-def attend_back(low, high, qp, km, kmt, v, dc, ct, lse, gk, gq, kind_col):
+def attend_back(own_groups, other_groups, qp, km, kmt, v, dc, ct, lse, gk, gq, kind_col):
     halves, micro, local, width = qp.shape
     half = width // 2
     heads = width // 128
@@ -582,7 +655,7 @@
             micro * heads * length * length * 1280, micro * length * width * 16, micro * heads * length * length
         ),
         name="attend_back",
-    )(low, high, qp, km, kmt, v, dc, ct, lse, gk, gq, kind_col)
+    )(own_groups, other_groups, qp, km, kmt, v, dc, ct, lse, gk, gq, kind_col)
 
 
 def norm_forward(hidden):
@@ -774,7 +847,56 @@
         out_ref[pl.ds((at - 5) * 4, 4), 0 : 4 * rows, :] = grad.reshape(4, 4 * rows, width)
 
 
-def feed_grad(left, right):
+def chip_grad_kernel(l_ref, r_ref, out_ref, part, from_core, c_send, c_recv):
+    width = l_ref.shape[1]
+    rows = width // GROUPS
+    at = pl.program_id(0)
+    x, _, z, y, core = spots()
+    partner = (x, slot_of(z, y, 1 - core))
+    spans = [(slice(0, 8), 4 * rows + i * rows, rows) for i in range(5)]
+    spans += [(slice(2 * j, 2 * j + 2), 0, 4 * rows) for j in range(4)]
+
+    def copy_of(i):
+        rails, start, size = spans[i]
+        return send(
+            part.at[rails, 1 - core, slice(start, start + size), :],
+            from_core.at[rails, slice(start, start + size), :],
+            c_send.at[i],
+            c_recv.at[i],
+            partner,
+        )
+
+    def add(i):
+        rails, start, size = spans[i]
+        copy_of(i).wait_recv()
+        for rail in range(rails.start, rails.stop):
+            mine = part[rail, core, start : start + size, :].astype(f32)
+            theirs = from_core[rail, start : start + size, :].astype(f32)
+            out_ref[rail, start : start + size, :] = (mine + theirs).astype(bf16)
+
+    @pl.when(at == 0)
+    def _():
+        greet([partner])
+
+    grad = tn(l_ref[...], r_ref[...]).astype(bf16)
+    for i in range(9):
+
+        @pl.when(at == i)
+        def _(i=i):
+            rails, start, size = spans[i]
+            count = rails.stop - rails.start
+            part[rails, :, start : start + size, :] = grad.reshape(count, 2, size, width)
+            copy_of(i).start()
+            if i >= 2:
+                add(i - 2)
+            if i == 8:
+                add(7)
+                add(8)
+                for k in range(9):
+                    copy_of(k).wait_send()
+
+
+def feed_grad(left, right, direct):
     tokens = left.shape[0]
     width = left.shape[1] // 6
     rows = width // GROUPS
@@ -785,16 +907,25 @@
     def right_at(i):
         return (0, jnp.minimum(i, 5))
 
+    slots = 8 if direct else GROUPS
+    scratch = [
+        pltpu.VMEM((8, 2, 9 * rows, width), bf16),
+        pltpu.VMEM((8, 9 * rows, width), bf16),
+        pltpu.SemaphoreType.DMA((9,)),
+        pltpu.SemaphoreType.DMA((9,)),
+    ]
+    extra = dict(collective_id=2, has_side_effects=True) if direct else {}
     return pl.pallas_call(
-        feed_grad_kernel,
+        chip_grad_kernel if direct else feed_grad_kernel,
         grid=(9,),
         in_specs=[
             pl.BlockSpec((tokens, width), left_at),
             pl.BlockSpec((tokens, width), right_at),
         ],
-        out_specs=pl.BlockSpec((GROUPS, 9 * rows, width), lambda i: (0, 0, 0)),
-        out_shape=jax.ShapeDtypeStruct((GROUPS, 9 * rows, width), bf16),
-        compiler_params=pltpu.CompilerParams(vmem_limit_bytes=VMEM_LIMIT),
+        out_specs=pl.BlockSpec((slots, 9 * rows, width), lambda i: (0, 0, 0)),
+        out_shape=jax.ShapeDtypeStruct((slots, 9 * rows, width), bf16),
+        scratch_shapes=scratch if direct else (),
+        compiler_params=pltpu.CompilerParams(vmem_limit_bytes=VMEM_LIMIT, **extra),
         cost_estimate=cost(2 * tokens * width * width * 9, tokens * width * 24 + width * width * 18),
         name="feed_grad",
     )(left, right)
@@ -833,6 +964,9 @@
     x_ref,
     d_ref,
     vec_ref,
+    w_ref,
+    dh_ref,
+    dx_ref,
     gq_ref,
     gk_ref,
     gv_ref,
@@ -846,6 +980,10 @@
     out_z,
     held,
     total,
+    dx_out,
+    from_dx,
+    d_send,
+    d_recv,
     c_send,
     c_recv,
     y_send,
@@ -879,7 +1017,8 @@
     def _():
         greet(all_peers())
 
-    grad = tn(x_ref[...], d_ref[...]).astype(bf16)
+    columns = pl.ds(pl.multiple_of(step_at * width, 128), width)
+    grad = tn(x_ref[...], d_ref[:, columns]).astype(bf16)
     for chunk in range(3):
 
         @pl.when(step_at == chunk)
@@ -890,6 +1029,18 @@
                 part[:, 3 * rows :, :] = vec_ref[...]
             for rail in range(8):
                 core_copy(chunk, rail).start()
+
+    flat = dh_ref.shape[0]
+
+    def input_part(start):
+        found = None
+        for i in range(3):
+            piece = nt(
+                d_ref[pl.ds(pl.multiple_of(start, BLOCK), BLOCK), i * width : i * width + width],
+                w_ref[:, i * rows : i * rows + rows, :].reshape(width, width),
+            )
+            found = piece if found is None else found + piece
+        return found
 
     @pl.when(step_at == 2)
     def _():
@@ -921,6 +1072,14 @@
             core_wait(rail)
             out_y[zz] = (part[2 * rail + core].astype(f32) + from_core[rail].astype(f32)).astype(bf16)
             y_copy(zz).start()
+
+        @pl.loop(0, flat // BLOCK)
+        def _(i):
+            at = pl.ds(pl.multiple_of(i * BLOCK, BLOCK), BLOCK)
+            dx_out[at, :] = input_part(flat + i * BLOCK).astype(bf16)
+
+        exchange = send(dx_out, from_dx, d_send, d_recv, across)
+        exchange.start()
         for step in range(4):
             zz = z_order(step)
             rail = zz * 2 + y
@@ -931,6 +1090,12 @@
             y_copy(zz).wait_recv()
             out_z[zz] = (held[zz] + from_y[zz].astype(f32)).astype(bf16)
             z_copy(zz).start()
+
+        @pl.loop(0, flat // BLOCK)
+        def _(i):
+            at = pl.ds(pl.multiple_of(i * BLOCK, BLOCK), BLOCK)
+            dx_ref[at, :] = dh_ref[at, :] + input_part(i * BLOCK)
+
         y_copy(z).wait_recv()
         result = held[z] + from_y[z].astype(f32)
         for step in range(3):
@@ -940,6 +1105,13 @@
         total[...] = result.astype(bf16)
         last = send(total, from_x, x_send, x_recv, across)
         last.start()
+        exchange.wait()
+
+        @pl.loop(0, flat // BLOCK)
+        def _(i):
+            at = pl.ds(pl.multiple_of(i * BLOCK, BLOCK), BLOCK)
+            dx_ref[at, :] += from_dx[at, :].astype(f32)
+
         for chunk in range(3):
             for rail in range(8):
                 core_copy(chunk, rail).wait_send()
@@ -973,23 +1145,25 @@
         gvec_ref[...] = total[3 * rows :, :].astype(f32) + from_x[3 * rows :, :].astype(f32)
 
 
-def scatter_attention(x, d, vectors):
+def scatter_attention(x, d, vectors, weights, dh):
     tokens, width = x.shape
     rows = width // GROUPS
     tall = 3 * rows + 16
     sem = pltpu.SemaphoreType.DMA
 
     def whole(*dims):
-        return pl.BlockSpec(dims, lambda i: (0,) * len(dims))
-
-    outs = ((rows, 4 * width), (rows, width), (rows, width), (16, width))
+        return pl.BlockSpec(dims, lambda i: (0,) * len(dims), pipeline_mode=pl.Buffered(1))
+
+    outs = (dh.shape, (rows, 4 * width), (rows, width), (rows, width), (16, width))
     return pl.pallas_call(
         scatter_kernel,
         grid=(3,),
         in_specs=[
             whole(tokens, width),
-            pl.BlockSpec((tokens, width), lambda i: (0, i)),
+            whole(*d.shape),
             whole(GROUPS, 16, width),
+            whole(*weights.shape),
+            whole(*dh.shape),
         ],
         out_specs=[whole(*dims) for dims in outs],
         out_shape=[jax.ShapeDtypeStruct(dims, f32) for dims in outs],
@@ -1003,6 +1177,10 @@
             pltpu.VMEM((4, tall, width), bf16),
             pltpu.VMEM((4, tall, width), f32),
             pltpu.VMEM((tall, width), bf16),
+            pltpu.VMEM(dh.shape, bf16),
+            pltpu.VMEM(dh.shape, bf16),
+            sem,
+            sem,
             sem((24,)),
             sem((24,)),
             sem((4,)),
@@ -1017,7 +1195,7 @@
         ),
         cost_estimate=cost(2 * tokens * width * width * 3, tokens * width * 8 + width * width * 6),
         name="scatter",
-    )(x, d, vectors)
+    )(x, d, vectors, weights, dh)
 
 
 def input_grad_kernel(d_ref, w_ref, out_ref):
@@ -1104,7 +1282,6 @@
     devices = lax.axis_size("shard")
     rows = width // devices
     side = lax.axis_index("seq").astype(jnp.int32)
-    per = local // BLOCK
 
     vectors = (
         query_bias,
@@ -1168,18 +1345,11 @@
     )
 
     own_tokens = tokens[:, 0]
-    xs = jnp.stack([own_tokens, other_tokens[:, 0]])
-    kind_all = jnp.stack([kinds[:, 0], other_kinds[:, 0]])
-    group_all = jnp.stack([groups[:, 0], other_groups[:, 0]])
-    kind_col = kind_all[..., None]
-    gk = group_all[..., None]
-    gq = group_all[:, :, None, :]
-    by_block = group_all.reshape(2, micro, per, BLOCK)
-    low = jnp.swapaxes(by_block[..., 0], 0, 1).reshape(-1)
-    high = jnp.swapaxes(by_block[..., BLOCK - 1], 0, 1).reshape(-1)
-
-    qp, km, kmt, v, vt = project(xs, attn_w, bias_rows, kind_col)
-    c, ct, lse = attend(low, high, qp, km, vt, gk, gq)
+    own_groups, far_groups = groups.reshape(micro, local), other_groups.reshape(micro, local)
+    qp, km, kmt, v, vt, xs, kind_col, gk, gq = project(
+        tokens, other_tokens, kinds, other_kinds, groups, other_groups, attn_w, bias_rows
+    )
+    c, ct, lse = attend(own_groups, far_groups, qp, km, vt, gk, gq)
     c_other = swap(c[1])
     flat = micro * local
     mixed, dh1, left, right, dc_own, dc_other, sums = chain(
@@ -1193,13 +1363,18 @@
     )
 
     dc_swapped = swap(dc_other)
-    feed_part = feed_grad(left, right)
+    feed_part = feed_grad(left, right, direct)
     dc_swapped, feed_part = lax.optimization_barrier((dc_swapped, feed_part))
     dc = jnp.stack([dc_own, dc_swapped]).reshape(2, micro, local, half)
-    if devices != GROUPS:
+    rails = None
+    if direct:
+        rails = [[2 * rail + core for rail in range(8)] for core in range(2)]
+    else:
         feed_part = ungroup(feed_part, feed_sizes, devices)
-    feed_sum = lax.psum_scatter(feed_part, "shard", scatter_dimension=0, tiled=True)[0]
-    d, db = attend_back(low, high, qp, km, kmt, v, dc, ct, lse, gk, gq, kind_col)
+    feed_sum = lax.psum_scatter(
+        feed_part, "shard", scatter_dimension=0, axis_index_groups=rails, tiled=True
+    )[0]
+    d, db = attend_back(own_groups, far_groups, qp, km, kmt, v, dc, ct, lse, gk, gq, kind_col)
 
     query_own = unpair_columns(db[0, : 2 * width].reshape(2, width), head_dim)
     zero = jnp.zeros((half,), f32)
@@ -1226,11 +1401,13 @@
         axis=1,
     ).astype(bf16)
     grad_vectors = jnp.pad(grad_vectors[:, None, :], ((0, 0), (0, 15), (0, width - piece)))
-    dx_other = input_grad_part(d, attn_w, 1, bf16)
     flat_x = xs.reshape(2 * flat, width)
     flat_d = d.reshape(2 * flat, 3 * width)
     if direct:
-        grad_query, grad_key, grad_value, vec_rows = scatter_attention(flat_x, flat_d, grad_vectors)
+        input_grad, grad_query, grad_key, grad_value, vec_rows = scatter_attention(
+            flat_x, flat_d, grad_vectors, attn_w, dh1
+        )
+        input_grad = input_grad.reshape(micro, local, width)
         vec_total = vec_rows[0, :piece]
     else:
         zeros = jnp.zeros((GROUPS, 16, width), bf16)
@@ -1243,8 +1420,9 @@
         grad_query, grad_key, grad_value, vec_total = assemble(
             attn_sum, attn_other, side, head_dim, rows, piece
         )
-    dx_own = input_grad_part(d, attn_w, 0, f32)
-    input_grad = dh1.reshape(micro, local, width) + dx_own + swap(dx_other).astype(f32)
+        dx_other = input_grad_part(d, attn_w, 1, bf16)
+        dx_own = input_grad_part(d, attn_w, 0, f32)
+        input_grad = dh1.reshape(micro, local, width) + dx_own + swap(dx_other).astype(f32)
 
     feed_total = feed_sum.astype(f32) + swap(feed_sum).astype(f32)
     grad_down = feed_total[: 4 * rows]

time: 437 us -> 431 us (0.986); the launches traced: 430 us -> 430 us
  waiting for transfers between devices: 26.7 us -> 82.5 us
  Pallas kernels: 348 us -> 304 us
  other arithmetic: 12.6 us -> 3.83 us
    reduce_scatter x1, waiting for transfers between devices: 0.01 us -> 65.9 us  [on_device(): lax.psum_scatter(feed_part, 'shard', scatter_dimension=0, axis_index_grou...]
    pallas_call x1, Pallas kernels: 96.5 us -> 66.2 us  [scatter_attention(): pl.pallas_call(scatter_kernel, grid=(3,), in_specs=[whole(tokens, width),...]
    pallas_call x4 -> x2, Pallas kernels: 51.5 us -> 38.4 us  [the longest x1 22.1 us: feed_grad(): pl.pallas_call(chip_grad_kernel if direct else feed_grad_kernel, grid=(9,...]
    ppermute x4 -> x3, waiting for transfers between devices: 26.7 us -> 16.6 us  [swap(): return lax.ppermute(value, 'seq', [(0, 1), (1, 0)])]
    unnamed x2 -> x0, other arithmetic: 5.3 us -> none
  transfers between devices with their start and end apart: 6 -> 5, of which waited for: 2 -> 2; matrix products, arithmetic and copies ran while one was open for 7% -> 4% of each run, Pallas kernels for 69% -> 58%
where the time goes in v4:
time: 431 us; the launch traced here: 430 us
  Pallas kernels  304 us (71%)
  waiting for transfers between devices  82.5 us (19%)
  local copies, waits for them, and re-layouts  20.7 us (5%)
  between operations  14.3 us (3%)
  starting transfers between devices  5.13 us (1%)
    pallas_call x1, Pallas kernels, scatter_attention(): pl.pallas_call(scatter_kernel, grid=(3,), in_specs=[whole(tokens, width),...  66.2 us
    reduce_scatter x1, waiting for transfers between devices, on_device(): lax.psum_scatter(feed_part, 'shard', scatter_dimension=0, axis_index_grou...  65.9 us
    pallas_call x1, Pallas kernels, attend_back(): pl.pallas_call(attend_back_kernel, grid_spec=pltpu.PrefetchScalarGridSpec...  52.6 us
    pallas_call x1, Pallas kernels, gather_attention(): pl.pallas_call(gather_kernel, in_specs=[vmem] * 13 + [anywhere] * 3, out_...  51.3 us
    pallas_call x1, Pallas kernels, chain(): pl.pallas_call(chain_kernel, grid_spec=pltpu.PrefetchScalarGridSpec(num_s...  50.6 us
    pallas_call x1, Pallas kernels, attend(): pl.pallas_call(attend_kernel, grid_spec=pltpu.PrefetchScalarGridSpec(num_...  42.9 us
    pallas_call x1, Pallas kernels, feed_grad(): pl.pallas_call(chip_grad_kernel if direct else feed_grad_kernel, grid=(9,...  22.1 us
    ppermute x3, waiting for transfers between devices, swap(): return lax.ppermute(value, 'seq', [(0, 1), (1, 0)])  16.6 us
  transfers between devices with their start and end apart: 5, of which 2 were waited for; matrix products, arithmetic and copies ran while one was open for 4% of the time, Pallas kernels for 58%

profile of v4, /device:TPU:0, one launch (start us, length us, event | category | flops | bytes accessed | tf_op | source)
XLA Modules:
  0.0 430.5 jit_solution(15135951072042596154)
XLA Ops:
  7.3 2.0 pack_feed.1
  9.3 0.6 broadcast_in_dim.48.refs_3_
  9.9 0.6 broadcast_in_dim.54.refs_9_
  10.5 51.3 %gather.1 = (bf16[16,160,768]{2,1,0:T(8,128)(2,1)}, bf16[2,1,512,768]{3,2,1,0:T(8,128)(2,1)}, s32[2,1,512]{2,1,0:T(1,128)}, s32[2,1,512]{2,1,0:T(1,128)}) custom-call(bf16[48,3072]{1,0:T(8,128)(2,1)} %refs_0_.1, bf16[48,768]{1,0:T(8,128)(2,1)} %refs_1_.1, bf16[48,768]{1,0:T(8,128)(2,1)} %refs_2_.1, bf16[1,192]{1,0:T(2,128)(2,1)} %broadcast_in_dim.48.refs_3_, ...), custom_call_target="tpu_custom_call" | custom-call | tf_op jit(solution)/shard_map/gather/pallas_call | solution.py:183
  61.7 1.0 slice.199
  63.2 0.1 reshape.346
  63.2 0.6 pad_maximum_fusion.2.bias_ref
  63.9 1.3 copy_bitcast_fusion.2
  65.1 16.3 %project.1 = (bf16[2,2,512,768]{3,2,1,0:T(8,128)(2,1)}, bf16[2,2,512,768]{3,2,1,0:T(8,128)(2,1)}, bf16[2,2,768,512]{3,2,1,0:T(8,128)(2,1)}, bf16[2,2,512,384]{3,...) custom-call(bf16[2,1,512,768]{3,2,1,0:T(8,128)(2,1)} %own_ref.1, ...), custom_call_target="tpu_custom_call" | custom-call | flops 7247757312 | bytes 15728640 | tf_op jit(solution)/shard_map/project/pallas_call | solution.py:379
  81.4 42.9 %attend.1 = (bf16[2,2,512,384]{3,2,1,0:T(8,128)(2,1)}, f32[2,384,1024]{2,1,0:T(8,128)}, f32[2,8,1024]{2,1,0:T(8,128)}) custom-call(s32[2,512]{1,0:T(2,128)} %get-tuple-element.160.own_ref, s32[2,512]{1,0:T(2,128)} %get-tuple-element.159.other_ref, bf16[2,2,512,768]{3,2,1,0:T(8,128)(2,1)} %get-tuple-element.54.qp_ref, ...), custom_call_target="tpu_custom_call" | custom-call | flops 6442450944 | bytes 12582912 | tf_op jit(solution)/shard_map/attend/pallas_call | solution.py:491
  124.3 2.4 slice_bitcast_fusion
  126.7 1.8 collective-permute-start
  128.6 0.1 convert_element_type.109
  129.3 0.6 concatenate.98.vec_ref
  129.9 16.6 %collective-permute-done = bf16[2,512,384]{2,1,0:T(8,128)(2,1)S(1)} collective-permute-done((bf16[2,512,384]{2,1,0:T(8,128)(2,1)S(1)}, bf16[2,512,384]{2,1,0:T(8,128)(2,1)S(1)}, u32[]{:S(2)}, u32[]{:S(2)}) %collective-permute-start) | collective-permute-done | bytes 786464 | tf_op jit(solution)/shard_map/ppermute | solution.py:32
  146.5 0.9 copy-done.8
  147.4 50.6 %chain.1 = (bf16[1024,768]{1,0:T(8,128)(2,1)}, f32[1024,768]{1,0:T(8,128)}, bf16[1024,4608]{1,0:T(8,128)(2,1)}, bf16[1024,4608]{1,0:T(8,128)(2,1)}, bf16[1024,38...) custom-call(s32[1]{0:T(128)} %bitcast.side_ref, bf16[1024,768]{1,0:T(8,128)(2,1)} %bitcast.63, ...), custom_call_target="tpu_custom_call" | custom-call | flops 22951231488 | bytes 38928384 | tf_op jit(solution)/shard_map/chain/pallas_call | solution.py:791
  197.9 1.7 collective-permute-start.1
  199.7 22.1 %feed_grad.1 = bf16[8,432,768]{2,1,0:T(8,128)(2,1)} custom-call(bf16[1024,4608]{1,0:T(8,128)(2,1)} %get-tuple-element.66.l_ref, bf16[1024,4608]{1,0:T(8,128)(2,1)} %get-tuple-element.67.r_ref), custom_call_target="tpu_custom_call" | custom-call | flops 10871635968 | bytes 29491200 | tf_op jit(solution)/shard_map/feed_grad/pallas_call | solution.py:918
  221.9 0.7 copy-done.6
  222.9 0.1 concatenate.134
  222.9 0.1 concatenate.132
  223.0 0.1 concatenate.131
  223.1 0.1 concatenate.130
  223.2 0.1 concatenate.133
  223.3 1.3 pad_maximum_fusion.dc_ref
  224.6 52.6 %attend_back.1 = (bf16[2,2,512,2304]{3,2,1,0:T(8,128)(2,1)}, f32[8,2304]{1,0:T(8,128)}) custom-call(s32[2,512]{1,0:T(2,128)} %get-tuple-element.160.own_ref, s32[2,512]{1,0:T(2,128)} %get-tuple-element.159.other_ref, bf16[2,2,512,768]{3,2,1,0:T(8,128)(2,1)} %get-tuple-element.54.qp_ref, bf16[2,2,512,768]{3,2,1,0:T(8,128)(2,1)} %get-tuple-element.55.km_ref, ...), custom_call_target="tpu_custom_call" | custom-call | flops 16106127360 | bytes 25165824 | tf_op jit(solution)/shard_map/attend_back/pallas_call | solution.py:627
  277.2 0.8 slice_reduce_fusion
  278.4 0.1 concatenate.110
  278.5 0.1 concatenate.107
  278.6 0.1 concatenate.104
  278.7 0.7 slice_reduce_fusion.11
  279.5 0.1 concatenate.129
  279.7 0.3 concatenate.126
  280.0 0.8 pad.16.vec_ref
  280.8 65.9 %reduce-scatter.2.cloned.1.call-done = bf16[1,432,768]{2,1,0:T(8,128)(2,1)} async-done(((bf16[8,432,768]{2,1,0:T(8,128)(2,1)}), bf16[1,432,768]{2,1,0:T(8,128)(2,1)}) %reduce-scatter.2.cloned.1.call-update) | async-done | bytes 663568 | tf_op jit(solution)/shard_map/reduce_scatter | solution.py:1374
  346.7 1.5 collective-permute-start.2
  348.1 66.2 %scatter.1 = (f32[1024,768]{1,0:T(8,128)}, f32[48,3072]{1,0:T(8,128)}, f32[48,768]{1,0:T(8,128)}, f32[48,768]{1,0:T(8,128)}, f32[16,768]{1,0:T(8,128)}) custom-call(bf16[2048,768]{1,0:T(8,128)(2,1)} %bitcast.85, bf16[2048,2304]{1,0:T(8,128)(2,1)} %bitcast.84, bf16[16,16,768]{2,1,0:T(8,128)(2,1)} %pad.16.vec_ref, ...), custom_call_target="tpu_custom_call" | custom-call | flops 7247757312 | bytes 16121856 | tf_op jit(solution)/shard_map/scatter/pallas_call | solution.py:1158
  414.4 1.4 slice_bitcast_fusion.1
  415.8 1.3 fusion.2
  417.2 0.2 convert_add_fusion
  417.4 0.9 slice.290
  418.2 0.7 fusion.1
  418.9 0.9 pad_maximum_fusion.1
  419.8 1.7 copy.69
  421.5 0.8 copy.70
  422.3 0.7 copy.71
  423.0 0.7 copy.72
  (64 shorter events, 1.9 us)
Async XLA Ops:
  7.2 2.1 copy-start.9
  7.2 2.7 copy-start.10
  7.2 139.3 %all-gather.3.cloned.1.call-start = ((), (), s32[]{:S(2)}) async-start(), calls=%async_computation.2 | async-start | bytes 11280384 | tf_op jit(solution)/shard_map/all_gather | solution.py:1308
  9.2 54.6 %copy-start.7 = (s32[2,1,512]{2,1,0:T(1,128)S(1)}, s32[2,1,512]{2,1,0:T(1,128)}, u32[]{:S(2)}) copy-start(s32[2,1,512]{2,1,0:T(1,128)} %own_group_ref.1) | copy-start | bytes 12292
  9.3 337.4 %reduce-scatter.2.cloned.1.call-start = ((), (), s32[]{:S(2)}) async-start(), calls=%async_computation.1 | async-start | bytes 5971968 | tf_op jit(solution)/shard_map/reduce_scatter | solution.py:1374
  126.7 19.7 %collective-permute-start = (bf16[2,512,384]{2,1,0:T(8,128)(2,1)S(1)}, bf16[2,512,384]{2,1,0:T(8,128)(2,1)S(1)}, u32[]{:S(2)}, u32[]{:S(2)}) collective-permute-start(bf16[2,512,384]{2,1,0:T(8,128)(2,1)S(1)} %get-tuple-element.130), channel_id=1, source_target_pairs={{0,16},{16,0},{1,17},{17,1},{2,18},{18,2},{3,19},{19,3},{4,20},{20... | collective-permute-start | bytes 2359304 | tf_op jit(solution)/shard_map/ppermute | solution.py:32
  146.5 0.9 copy-start.8
  197.9 23.9 %collective-permute-start.1 = (bf16[1024,384]{1,0:T(8,128)(2,1)}, bf16[1024,384]{1,0:T(8,128)(2,1)S(1)}, u32[]{:S(2)}, u32[]{:S(2)}) collective-permute-start(bf16[1024,384]{1,0:T(8,128)(2,1)} %get-tuple-element.65), channel_id=1, source_target_pairs={{0,16},{16,0},{1,17},{17,1},{2,18},{18,2},{3,19},{19,3},{4,20},{20... | collective-permute-start | bytes 2359304 | tf_op jit(solution)/shard_map/ppermute | solution.py:32
  221.8 0.8 copy-start.6
  221.8 1.5 copy-start.1
  346.7 70.5 %collective-permute-start.2 = (bf16[432,768]{1,0:T(8,128)(2,1)}, bf16[432,768]{1,0:T(8,128)(2,1)S(1)}, u32[]{:S(2)}, u32[]{:S(2)}) collective-permute-start(bf16[432,768]{1,0:T(8,128)(2,1)} %bitcast.67), channel_id=1, source_target_pairs={{0,16},{16,0},{1,17},{17,1},{2,18},{18,2},{3,19},{19,3},{4,20},{20... | collective-permute-start | bytes 1990664 | tf_op jit(solution)/shard_map/ppermute | solution.py:32
  348.1 69.0 %copy-start.2 = (bf16[1,432,768]{2,1,0:T(8,128)(2,1)S(1)}, bf16[1,432,768]{2,1,0:T(8,128)(2,1)}, u32[]{:S(2)}) copy-start(bf16[1,432,768]{2,1,0:T(8,128)(2,1)} %reduce-scatter.2.cloned.1.call-done) | copy-start | bytes 1990660
  417.4 2.4 copy-start
  419.8 1.7 copy-start.3
  419.8 2.5 copy-start.5
  421.5 1.5 copy-start.4
Sparse Core Ops, SparseCore 0:
  10.3 107.4 all-gather.2
  222.0 124.6 reduce-scatter.1

commit v5 on v4

--- a/solution.py
+++ b/solution.py
@@ -1,3 +1,5 @@
+import functools
+
 import jax
 import jax.numpy as jnp
 from jax import lax
@@ -519,6 +521,7 @@
 
 
 def attend_back_kernel(
+    micro_at,
     own_ref,
     other_ref,
     qp_ref,
@@ -531,14 +534,9 @@
     gk_ref,
     gq_ref,
     kind_ref,
-    d_ref,
-    db_ref,
-    dqt_sc,
-    dk_sc,
-    dv_sc,
-    delta_sc,
+    *rest,
 ):
-    micro_at = pl.program_id(0)
+    d_ref, db_ref, dqt_sc, dk_sc, dv_sc, delta_sc = rest[-6:]
     local, width = qp_ref.shape[1], qp_ref.shape[2]
     half = width // 2
     per = local // BLOCK
@@ -547,9 +545,7 @@
     dk_sc[...] = jnp.zeros_like(dk_sc)
     dv_sc[...] = jnp.zeros_like(dv_sc)
 
-    @pl.when(micro_at == 0)
-    def _():
-        db_ref[...] = jnp.zeros_like(db_ref)
+    db_ref[...] = jnp.zeros_like(db_ref)
 
     lo = low_lanes((BLOCK, 128))
 
@@ -619,24 +615,33 @@
         db_ref[0:1, :] += jnp.sum(d_ref[kh, krows, :].astype(f32), axis=0, keepdims=True)
 
 
-def attend_back(own_groups, other_groups, qp, km, kmt, v, dc, ct, lse, gk, gq, kind_col):
+def attend_back(own_groups, other_groups, qp, km, kmt, v, dc, ct, lse, gk, gq, kind_col, micro_at, d_before):
     halves, micro, local, width = qp.shape
     half = width // 2
     heads = width // 128
     length = halves * local
+
+    def one(array):
+        rest = array.shape[2:]
+        return pl.BlockSpec(
+            (array.shape[0], None) + rest, lambda m, *_: (0, micro_at) + (0,) * len(rest)
+        )
+
+    before = () if d_before is None else (d_before,)
     return pl.pallas_call(
-        attend_back_kernel,
+        functools.partial(attend_back_kernel, micro_at),
         grid_spec=pltpu.PrefetchScalarGridSpec(
             num_scalar_prefetch=2,
-            grid=(micro,),
-            in_specs=[whole_micro(a) for a in (qp, km, kmt, v, dc)]
+            grid=(1,),
+            in_specs=[one(a) for a in (qp, km, kmt, v, dc)]
             + [
-                pl.BlockSpec((None, half, length), lambda m, *_: (m, 0, 0)),
-                pl.BlockSpec((None, 8, length), lambda m, *_: (m, 0, 0)),
+                pl.BlockSpec((None, half, length), lambda m, *_: (micro_at, 0, 0)),
+                pl.BlockSpec((None, 8, length), lambda m, *_: (micro_at, 0, 0)),
             ]
-            + [whole_micro(a) for a in (gk, gq, kind_col)],
+            + [one(a) for a in (gk, gq, kind_col)]
+            + [pl.BlockSpec(memory_space=pl.ANY)] * len(before),
             out_specs=[
-                pl.BlockSpec((halves, None, local, 3 * width), lambda m, *_: (0, m, 0, 0)),
+                pl.BlockSpec((halves, None, local, 3 * width), lambda m, *_: (0, micro_at, 0, 0)),
                 pl.BlockSpec((8, 3 * width), lambda m, *_: (0, 0)),
             ],
             scratch_shapes=[
@@ -652,10 +657,11 @@
         ],
         compiler_params=pltpu.CompilerParams(vmem_limit_bytes=VMEM_LIMIT),
         cost_estimate=cost(
-            micro * heads * length * length * 1280, micro * length * width * 16, micro * heads * length * length
+            heads * length * length * 1280, length * width * 16, heads * length * length
         ),
+        input_output_aliases={12: 0} if before else {},
         name="attend_back",
-    )(own_groups, other_groups, qp, km, kmt, v, dc, ct, lse, gk, gq, kind_col)
+    )(own_groups, other_groups, qp, km, kmt, v, dc, ct, lse, gk, gq, kind_col, *before)
 
 
 def norm_forward(hidden):
@@ -681,7 +687,7 @@
     side_ref,
     x_ref,
     own_ref,
-    other_ref,
+    far_ref,
     cot_ref,
     w_ref,
     vec_ref,
@@ -694,6 +700,9 @@
     sums_ref,
     slope_sc,
     z_sc,
+    landed,
+    c_send,
+    c_recv,
 ):
     width = x_ref.shape[1]
     half = width // 2
@@ -701,9 +710,35 @@
     chunks = 4
     first = side_ref[0] == 0
 
-    @pl.when(pl.program_id(0) == 0)
+    step_at = pl.program_id(0)
+    blocks = landed.shape[0]
+    per = far_ref.shape[2] // BLOCK
+    across = (1 - lax.axis_index("seq"), lax.axis_index("shard"))
+
+    def far_copy(i):
+        return send(
+            far_ref.at[1, i // per, pl.ds((i % per) * BLOCK, BLOCK), :],
+            landed.at[i],
+            c_send.at[i],
+            c_recv.at[i],
+            across,
+        )
+
+    @pl.when(step_at == 0)
     def _():
         sums_ref[...] = jnp.zeros_like(sums_ref)
+        greet([across])
+        for i in range(blocks):
+            far_copy(i).start()
+
+    for i in range(blocks):
+
+        @pl.when(step_at == i)
+        def _(i=i):
+            far_copy(i).wait_recv()
+            if i == blocks - 1:
+                for k in range(blocks):
+                    far_copy(k).wait_send()
 
     def vector(at):
         return vec_ref[at : at + 1, :]
@@ -719,7 +754,7 @@
         return w_ref[:, 4 * rows : 5 * rows, :].reshape(width, width)
 
     own = own_ref[...].astype(f32)
-    other = other_ref[...].astype(f32)
+    other = landed[step_at].astype(f32)
     context = jnp.concatenate(
         [jnp.where(first, own, other), jnp.where(first, other, own)], axis=1
     ).astype(bf16)
@@ -778,9 +813,11 @@
     dcx_ref[...] = jnp.where(first, dc[:, half:], dc[:, :half]).astype(bf16)
 
 
-def chain(side, x, c_own, c_other, cot, weights, vectors):
+def chain(side, x, c, cot, weights, vectors):
     tokens, width = x.shape
     half = width // 2
+    per = c.shape[2] // BLOCK
+    blocks = tokens // BLOCK
 
     def rows_spec(cols):
         return pl.BlockSpec((BLOCK, cols), lambda i, *_: (i, 0))
@@ -795,8 +832,8 @@
             grid=(tokens // BLOCK,),
             in_specs=[
                 rows_spec(width),
-                rows_spec(half),
-                rows_spec(half),
+                pl.BlockSpec((None, None, BLOCK, half), lambda i, *_: (0, i // per, i % per, 0)),
+                pl.BlockSpec(memory_space=pl.ANY),
                 rows_spec(width),
                 pl.BlockSpec(weights.shape, lambda i, *_: (0, 0, 0), pipeline_mode=pl.Buffered(1)),
                 pl.BlockSpec(vectors.shape, lambda i, *_: (0, 0)),
@@ -810,7 +847,13 @@
                 rows_spec(half),
                 pl.BlockSpec((16, width), lambda i, *_: (0, 0)),
             ],
-            scratch_shapes=[pltpu.VMEM((BLOCK, 4 * width), f32), pltpu.VMEM((BLOCK, width), f32)],
+            scratch_shapes=[
+                pltpu.VMEM((BLOCK, 4 * width), f32),
+                pltpu.VMEM((BLOCK, width), f32),
+                pltpu.VMEM((blocks, BLOCK, half), bf16),
+                pltpu.SemaphoreType.DMA((blocks,)),
+                pltpu.SemaphoreType.DMA((blocks,)),
+            ],
         ),
         out_shape=[
             shape(width, bf16),
@@ -821,10 +864,12 @@
             shape(half, bf16),
             jax.ShapeDtypeStruct((16, width), f32),
         ],
-        compiler_params=pltpu.CompilerParams(vmem_limit_bytes=VMEM_LIMIT),
+        compiler_params=pltpu.CompilerParams(
+            collective_id=3, has_side_effects=True, vmem_limit_bytes=VMEM_LIMIT
+        ),
         cost_estimate=cost(2 * tokens * width * width * 19, tokens * width * 36 + weights.size * 2),
         name="chain",
-    )(side[None], x, c_own, c_other, cot, weights, vectors)
+    )(side[None], x, c, c, cot, weights, vectors)
 
 
 def feed_grad_kernel(l_ref, r_ref, out_ref):
@@ -847,7 +892,7 @@
         out_ref[pl.ds((at - 5) * 4, 4), 0 : 4 * rows, :] = grad.reshape(4, 4 * rows, width)
 
 
-def chip_grad_kernel(l_ref, r_ref, out_ref, part, from_core, c_send, c_recv):
+def chip_grad_kernel(l_ref, r_ref, keep_ref, give_ref, part, from_core, c_send, c_recv):
     width = l_ref.shape[1]
     rows = width // GROUPS
     at = pl.program_id(0)
@@ -872,7 +917,10 @@
         for rail in range(rails.start, rails.stop):
             mine = part[rail, core, start : start + size, :].astype(f32)
             theirs = from_core[rail, start : start + size, :].astype(f32)
-            out_ref[rail, start : start + size, :] = (mine + theirs).astype(bf16)
+            whole = mine + theirs
+            left, right = whole[:, : width // 2], whole[:, width // 2 :]
+            keep_ref[rail, start : start + size, :] = jnp.where(x == 0, left, right).astype(bf16)
+            give_ref[rail, start : start + size, :] = jnp.where(x == 0, right, left).astype(bf16)
 
     @pl.when(at == 0)
     def _():
@@ -907,7 +955,8 @@
     def right_at(i):
         return (0, jnp.minimum(i, 5))
 
-    slots = 8 if direct else GROUPS
+    out = (8, 9 * rows, width // 2) if direct else (GROUPS, 9 * rows, width)
+    count = 2 if direct else 1
     scratch = [
         pltpu.VMEM((8, 2, 9 * rows, width), bf16),
         pltpu.VMEM((8, 9 * rows, width), bf16),
@@ -922,8 +971,8 @@
             pl.BlockSpec((tokens, width), left_at),
             pl.BlockSpec((tokens, width), right_at),
         ],
-        out_specs=pl.BlockSpec((slots, 9 * rows, width), lambda i: (0, 0, 0)),
-        out_shape=jax.ShapeDtypeStruct((slots, 9 * rows, width), bf16),
+        out_specs=[pl.BlockSpec(out, lambda i: (0, 0, 0))] * count,
+        out_shape=[jax.ShapeDtypeStruct(out, bf16)] * count,
         scratch_shapes=scratch if direct else (),
         compiler_params=pltpu.CompilerParams(vmem_limit_bytes=VMEM_LIMIT, **extra),
         cost_estimate=cost(2 * tokens * width * width * 9, tokens * width * 24 + width * width * 18),
@@ -1350,13 +1399,11 @@
         tokens, other_tokens, kinds, other_kinds, groups, other_groups, attn_w, bias_rows
     )
     c, ct, lse = attend(own_groups, far_groups, qp, km, vt, gk, gq)
-    c_other = swap(c[1])
     flat = micro * local
     mixed, dh1, left, right, dc_own, dc_other, sums = chain(
         side,
         own_tokens.reshape(flat, width),
-        c[0].reshape(flat, half),
-        c_other.reshape(flat, half),
+        c,
         cotangent.reshape(flat, width),
         feed_w,
         chain_vectors,
@@ -1366,15 +1413,29 @@
     feed_part = feed_grad(left, right, direct)
     dc_swapped, feed_part = lax.optimization_barrier((dc_swapped, feed_part))
     dc = jnp.stack([dc_own, dc_swapped]).reshape(2, micro, local, half)
+
+    def mix_back(micro_at, before):
+        return attend_back(
+            own_groups, far_groups, qp, km, kmt, v, dc, ct, lse, gk, gq, kind_col, micro_at, before
+        )
+
+    d, db = None, 0.0
+    for m in range(micro - 1):
+        d, part = mix_back(m, d)
+        db = db + part
     rails = None
     if direct:
         rails = [[2 * rail + core for rail in range(8)] for core in range(2)]
+        keep, give = feed_part
+        taken, d = lax.optimization_barrier((swap(give), d))
+        feed_part = (keep.astype(f32) + taken.astype(f32)).astype(bf16)
     else:
-        feed_part = ungroup(feed_part, feed_sizes, devices)
+        feed_part = ungroup(feed_part[0], feed_sizes, devices)
     feed_sum = lax.psum_scatter(
         feed_part, "shard", scatter_dimension=0, axis_index_groups=rails, tiled=True
     )[0]
-    d, db = attend_back(own_groups, far_groups, qp, km, kmt, v, dc, ct, lse, gk, gq, kind_col)
+    d, part = mix_back(micro - 1, d)
+    db = db + part
 
     query_own = unpair_columns(db[0, : 2 * width].reshape(2, width), head_dim)
     zero = jnp.zeros((half,), f32)
@@ -1424,7 +1485,15 @@
         dx_own = input_grad_part(d, attn_w, 0, f32)
         input_grad = dh1.reshape(micro, local, width) + dx_own + swap(dx_other).astype(f32)
 
-    feed_total = feed_sum.astype(f32) + swap(feed_sum).astype(f32)
+    feed_other = swap(feed_sum)
+    if direct:
+        feed_total = jnp.where(
+            side == 0,
+            jnp.concatenate([feed_sum, feed_other], axis=1),
+            jnp.concatenate([feed_other, feed_sum], axis=1),
+        ).astype(f32)
+    else:
+        feed_total = feed_sum.astype(f32) + feed_other.astype(f32)
     grad_down = feed_total[: 4 * rows]
     grad_output = feed_total[4 * rows : 5 * rows]
     grad_up = jnp.concatenate(

time: 431 us -> 426 us (0.988)
  waiting for transfers between devices: 82.5 us -> 31.5 us
  Pallas kernels: 304 us -> 348 us
  other arithmetic: 3.83 us -> 9.71 us
    reduce_scatter x1, waiting for transfers between devices: 65.9 us -> 0.02 us  [on_device(): lax.psum_scatter(feed_part, 'shard', scatter_dimension=0, axis_index_grou...]
    pallas_call x1, Pallas kernels: 66.2 us -> 95.2 us  [scatter_attention(): pl.pallas_call(scatter_kernel, grid=(3,), in_specs=[whole(tokens, width),...]
    ppermute x3, waiting for transfers between devices: 16.6 us -> 31.4 us  [swap(): return lax.ppermute(value, 'seq', [(0, 1), (1, 0)])]
    pallas_call x1, Pallas kernels: 50.6 us -> 58.7 us  [chain(): pl.pallas_call(chain_kernel, grid_spec=pltpu.PrefetchScalarGridSpec(num_s...]
    pallas_call x1 -> x2, Pallas kernels: 52.6 us -> 59.3 us  [attend_back(): pl.pallas_call(functools.partial(attend_back_kernel, micro_at), grid_spec...]
    convert_element_type x0 -> x2, other arithmetic: none -> 5.15 us  [the longest x1 3.91 us: on_device(): feed_part = (keep.astype(f32) + taken.astype(f32)).astype(bf16)]
  transfers between devices with their start and end apart: 5 -> 5, of which waited for: 2 -> 2; matrix products, arithmetic and copies ran while one was open for 4% -> 3% of each run, Pallas kernels for 58% -> 68%
where the time goes in v5:
time: 426 us; the launch traced here: 425 us
  Pallas kernels  348 us (82%)
  waiting for transfers between devices  31.5 us (7%)
  local copies, waits for them, and re-layouts  18.3 us (4%)
  between operations  14.3 us (3%)
  other arithmetic  9.71 us (2%)
    pallas_call x1, Pallas kernels, scatter_attention(): pl.pallas_call(scatter_kernel, grid=(3,), in_specs=[whole(tokens, width),...  95.2 us
    pallas_call x2, Pallas kernels, attend_back(): pl.pallas_call(functools.partial(attend_back_kernel, micro_at), grid_spec...  59.3 us
    pallas_call x1, Pallas kernels, chain(): pl.pallas_call(chain_kernel, grid_spec=pltpu.PrefetchScalarGridSpec(num_s...  58.7 us
    pallas_call x1, Pallas kernels, gather_attention(): pl.pallas_call(gather_kernel, in_specs=[vmem] * 13 + [anywhere] * 3, out_...  52.2 us
    pallas_call x1, Pallas kernels, attend(): pl.pallas_call(attend_kernel, grid_spec=pltpu.PrefetchScalarGridSpec(num_...  42.8 us
    ppermute x3, waiting for transfers between devices, swap(): return lax.ppermute(value, 'seq', [(0, 1), (1, 0)])  31.4 us
    pallas_call x1, Pallas kernels, feed_grad(): pl.pallas_call(chip_grad_kernel if direct else feed_grad_kernel, grid=(9,...  22.4 us
    pallas_call x1, Pallas kernels, project(): pl.pallas_call(project_kernel, grid=(halves, micro, sub), in_specs=[token...  15.1 us
  transfers between devices with their start and end apart: 5, of which 2 were waited for; matrix products, arithmetic and copies ran while one was open for 3% of the time, Pallas kernels for 68%

profile of v5, /device:TPU:0, one launch (start us, length us, event | category | flops | bytes accessed | tf_op | source)
XLA Modules:
  0.0 425.1 jit_solution(4617780641579036742)
XLA Ops:
  7.2 2.0 pack_feed.1
  9.3 1.2 broadcast_in_dim.48.refs_3_
  10.5 1.2 broadcast_in_dim.54.refs_9_
  11.7 52.2 %gather.1 = (bf16[16,160,768]{2,1,0:T(8,128)(2,1)}, bf16[2,1,512,768]{3,2,1,0:T(8,128)(2,1)}, s32[2,1,512]{2,1,0:T(1,128)}, s32[2,1,512]{2,1,0:T(1,128)}) custom-call(bf16[48,3072]{1,0:T(8,128)(2,1)} %refs_0_.1, bf16[48,768]{1,0:T(8,128)(2,1)} %refs_1_.1, bf16[48,768]{1,0:T(8,128)(2,1)} %refs_2_.1, bf16[1,192]{1,0:T(2,128)(2,1)} %broadcast_in_dim.48.refs_3_, ...), custom_call_target="tpu_custom_call" | custom-call | tf_op jit(solution)/shard_map/gather/pallas_call | solution.py:185
  64.0 1.0 slice.193
  65.0 0.1 convert_element_type.115
  65.2 0.1 convert_element_type.118
  66.0 0.6 concatenate.104.vec_ref
  66.7 0.1 reshape.343
  66.8 0.6 pad_maximum_fusion.2.bias_ref
  67.5 1.3 copy_bitcast_fusion.2
  68.7 15.1 %project.1 = (bf16[2,2,512,768]{3,2,1,0:T(8,128)(2,1)}, bf16[2,2,512,768]{3,2,1,0:T(8,128)(2,1)}, bf16[2,2,768,512]{3,2,1,0:T(8,128)(2,1)}, bf16[2,2,512,384]{3,...) custom-call(bf16[2,1,512,768]{3,2,1,0:T(8,128)(2,1)} %own_ref.1, ...), custom_call_target="tpu_custom_call" | custom-call | flops 7247757312 | bytes 15728640 | tf_op jit(solution)/shard_map/project/pallas_call | solution.py:381
  83.8 42.8 %attend.1 = (bf16[2,2,512,384]{3,2,1,0:T(8,128)(2,1)}, f32[2,384,1024]{2,1,0:T(8,128)}, f32[2,8,1024]{2,1,0:T(8,128)}) custom-call(s32[2,512]{1,0:T(2,128)} %get-tuple-element.172.own_ref, s32[2,512]{1,0:T(2,128)} %get-tuple-element.171.other_ref, bf16[2,2,512,768]{3,2,1,0:T(8,128)(2,1)} %get-tuple-element.61.qp_ref, ...), custom_call_target="tpu_custom_call" | custom-call | flops 6442450944 | bytes 12582912 | tf_op jit(solution)/shard_map/attend/pallas_call | solution.py:493
  126.6 58.7 %chain.1 = (bf16[1024,768]{1,0:T(8,128)(2,1)}, f32[1024,768]{1,0:T(8,128)}, bf16[1024,4608]{1,0:T(8,128)(2,1)}, bf16[1024,4608]{1,0:T(8,128)(2,1)}, bf16[1024,38...) custom-call(s32[1]{0:T(128)} %bitcast.side_ref, bf16[1024,768]{1,0:T(8,128)(2,1)} %bitcast.58, ...), custom_call_target="tpu_custom_call" | custom-call | flops 22951231488 | bytes 38928384 | tf_op jit(solution)/shard_map/chain/pallas_call | solution.py:828
  185.3 2.1 collective-permute-start
  187.4 22.4 %feed_grad.1 = (bf16[8,432,384]{2,1,0:T(8,128)(2,1)}, bf16[8,432,384]{2,1,0:T(8,128)(2,1)}) custom-call(bf16[1024,4608]{1,0:T(8,128)(2,1)} %get-tuple-element.73.l_ref, bf16[1024,4608]{1,0:T(8,128)(2,1)} %get-tuple-element.74.r_ref), custom_call_target="tpu_custom_call" | custom-call | flops 10871635968 | bytes 29491200 | tf_op jit(solution)/shard_map/feed_grad/pallas_call | solution.py:967
  209.8 0.1 collective-permute-start.1
  209.9 1.3 pad_maximum_fusion.dc_ref
  211.3 33.4 %attend_back.2 = (bf16[2,2,512,2304]{3,2,1,0:T(8,128)(2,1)}, f32[8,2304]{1,0:T(8,128)}) custom-call(s32[2,512]{1,0:T(2,128)} %get-tuple-element.172.own_ref, s32[2,512]{1,0:T(2,128)} %get-tuple-element.171.other_ref, bf16[2,2,512,768]{3,2,1,0:T(8,128)(2,1)} %get-tuple-element.61.qp_ref, bf16[2,2,512,768]{3,2,1,0:T(8,128)(2,1)} %get-tuple-element.62.km_ref, ...), custom_call_target="tpu_custom_call" | custom-call | flops 8053063680 | bytes 12582912 | tf_op jit(solution)/shard_map/attend_back/pallas_call | solution.py:631
  244.6 25.0 %collective-permute-done.1 = bf16[8,432,384]{2,1,0:T(8,128)(2,1)} collective-permute-done((bf16[8,432,384]{2,1,0:T(8,128)(2,1)}, bf16[8,432,384]{2,1,0:T(8,128)(2,1)}, u32[]{:S(2)}, u32[]{:S(2)}) %collective-permute-start.1) | collective-permute-done | bytes 2654240 | tf_op jit(solution)/shard_map/ppermute | solution.py:34
  269.7 3.9 add_convert_fusion
  273.6 0.8 copy-done.8
  274.7 0.1 concatenate.140
  274.8 0.1 concatenate.139
  274.9 0.1 concatenate.138
  275.0 0.1 concatenate.141
  275.1 26.0 %attend_back.3 = (bf16[2,2,512,2304]{3,2,1,0:T(8,128)(2,1)}, f32[8,2304]{1,0:T(8,128)}) custom-call(s32[2,512]{1,0:T(2,128)} %get-tuple-element.172.own_ref, s32[2,512]{1,0:T(2,128)} %get-tuple-element.171.other_ref, bf16[2,2,512,768]{3,2,1,0:T(8,128)(2,1)} %get-tuple-element.61.qp_ref, ...), custom_call_target="tpu_custom_call", output_to_operand_aliasing={{0}: (12, {})} | custom-call | flops 8053063680 | bytes 12582912 | tf_op jit(solution)/shard_map/attend_back/pallas_call | solution.py:631
  301.0 0.9 add.34
  302.3 0.1 concatenate.116
  302.4 0.1 concatenate.113
  302.5 0.1 concatenate.110
  302.7 0.1 concatenate.137
  302.8 0.3 concatenate.132
  303.1 0.8 pad.16.vec_ref
  303.9 95.2 %scatter.1 = (f32[1024,768]{1,0:T(8,128)}, f32[48,3072]{1,0:T(8,128)}, f32[48,768]{1,0:T(8,128)}, f32[48,768]{1,0:T(8,128)}, f32[16,768]{1,0:T(8,128)}) custom-call(bf16[2048,768]{1,0:T(8,128)(2,1)} %bitcast.80, bf16[2048,2304]{1,0:T(8,128)(2,1)} %bitcast.79, bf16[16,16,768]{2,1,0:T(8,128)(2,1)} %pad.16.vec_ref, ...), custom_call_target="tpu_custom_call" | custom-call | flops 7247757312 | bytes 16121856 | tf_op jit(solution)/shard_map/scatter/pallas_call | solution.py:1207
  399.2 1.3 collective-permute-start.2
  400.5 1.4 slice_bitcast_fusion
  401.9 1.3 fusion.3
  403.2 6.4 %collective-permute-done.2 = bf16[432,384]{1,0:T(8,128)(2,1)S(1)} collective-permute-done((bf16[432,384]{1,0:T(8,128)(2,1)}, bf16[432,384]{1,0:T(8,128)(2,1)S(1)}, u32[]{:S(2)}, u32[]{:S(2)}) %collective-permute-start.2) | collective-permute-done | bytes 331808 | tf_op jit(solution)/shard_map/ppermute | solution.py:34
  409.6 1.2 fusion
  410.9 0.9 slice.285
  411.7 0.7 fusion.2
  412.4 0.9 pad_maximum_fusion.1
  413.3 1.1 copy.72
  414.4 1.7 copy.73
  416.1 0.8 copy.74
  416.9 0.7 copy.75
  417.6 0.7 copy.76
  (65 shorter events, 1.9 us)
Async XLA Ops:
  7.2 60.3 %copy-start.9 = (s32[2,1,512]{2,1,0:T(1,128)S(1)}, s32[2,1,512]{2,1,0:T(1,128)}, u32[]{:S(2)}) copy-start(s32[2,1,512]{2,1,0:T(1,128)} %own_group_ref.1) | copy-start | bytes 12292
  7.2 119.4 %all-gather.3.cloned.1.call-start = ((), (), s32[]{:S(2)}) async-start(), calls=%async_computation.2 | async-start | bytes 11280384 | tf_op jit(solution)/shard_map/all_gather | solution.py:1357
  9.3 389.9 %reduce-scatter.2.cloned.1.call-start = ((), (), s32[]{:S(2)}) async-start(), calls=%async_computation.1 | async-start | bytes 2985984 | tf_op jit(solution)/shard_map/reduce_scatter | solution.py:1434
  185.3 24.5 %collective-permute-start = (bf16[1024,384]{1,0:T(8,128)(2,1)}, bf16[1024,384]{1,0:T(8,128)(2,1)S(1)}, u32[]{:S(2)}, u32[]{:S(2)}) collective-permute-start(bf16[1024,384]{1,0:T(8,128)(2,1)} %get-tuple-element.72), channel_id=1, source_target_pairs={{0,16},{16,0},{1,17},{17,1},{2,18},{18,2},{3,19},{19,3},{4,20},{20... | collective-permute-start | bytes 2359304 | tf_op jit(solution)/shard_map/ppermute | solution.py:34
  187.4 22.5 %copy-start.3 = (bf16[1024,384]{1,0:T(8,128)(2,1)S(1)}, bf16[1024,384]{1,0:T(8,128)(2,1)}, u32[]{:S(2)}) copy-start(bf16[1024,384]{1,0:T(8,128)(2,1)} %get-tuple-element.71) | copy-start | bytes 2359300
  209.8 59.9 %collective-permute-start.1 = (bf16[8,432,384]{2,1,0:T(8,128)(2,1)}, bf16[8,432,384]{2,1,0:T(8,128)(2,1)}, u32[]{:S(2)}, u32[]{:S(2)}) collective-permute-start(bf16[8,432,384]{2,1,0:T(8,128)(2,1)} %get-tuple-element.81), channel_id=1, source_target_pairs={{0,16},{16,0},{1,17},{17,1},{2,18},{18,2},{3,19},{19,3},{4,20},{20... | collective-permute-start | bytes 7962632 | tf_op jit(solution)/shard_map/ppermute | solution.py:34
  211.3 58.4 %copy-start.1 = (bf16[8,432,384]{2,1,0:T(8,128)(2,1)S(1)}, bf16[8,432,384]{2,1,0:T(8,128)(2,1)}, u32[]{:S(2)}) copy-start(bf16[8,432,384]{2,1,0:T(8,128)(2,1)} %get-tuple-element.94) | copy-start | bytes 7962628
  273.6 0.8 copy-start.8
  275.1 26.0 %copy-start.7 = (f32[8,2304]{1,0:T(8,128)S(1)}, f32[8,2304]{1,0:T(8,128)}, u32[]{:S(2)}) copy-start(f32[8,2304]{1,0:T(8,128)} %get-tuple-element.85) | copy-start | bytes 221188
  399.2 10.5 %collective-permute-start.2 = (bf16[432,384]{1,0:T(8,128)(2,1)}, bf16[432,384]{1,0:T(8,128)(2,1)S(1)}, u32[]{:S(2)}, u32[]{:S(2)}) collective-permute-start(bf16[432,384]{1,0:T(8,128)(2,1)} %bitcast.62), channel_id=1, source_target_pairs={{0,16},{16,0},{1,17},{17,1},{2,18},{18,2},{3,19},{19,3},{4,20},{20... | collective-permute-start | bytes 995336 | tf_op jit(solution)/shard_map/ppermute | solution.py:34
  403.2 10.1 %copy-start.2 = (bf16[1024,768]{1,0:T(8,128)(2,1)S(1)}, bf16[1024,768]{1,0:T(8,128)(2,1)}, u32[]{:S(2)}) copy-start(bf16[1024,768]{1,0:T(8,128)(2,1)} %get-tuple-element.67) | copy-start | bytes 4718596
  411.7 2.7 copy-start
  414.4 1.7 copy-start.4
  414.4 2.5 copy-start.6
  414.4 3.2 copy-start.5
Sparse Core Ops, SparseCore 0:
  10.3 108.7 all-gather.2
  273.7 97.4 reduce-scatter.1

commit v6 on v5

--- a/solution.py
+++ b/solution.py
@@ -1,5 +1,3 @@
-import functools
-
 import jax
 import jax.numpy as jnp
 from jax import lax
@@ -521,7 +519,6 @@
 
 
 def attend_back_kernel(
-    micro_at,
     own_ref,
     other_ref,
     qp_ref,
@@ -534,9 +531,14 @@
     gk_ref,
     gq_ref,
     kind_ref,
-    *rest,
+    d_ref,
+    db_ref,
+    dqt_sc,
+    dk_sc,
+    dv_sc,
+    delta_sc,
 ):
-    d_ref, db_ref, dqt_sc, dk_sc, dv_sc, delta_sc = rest[-6:]
+    micro_at = pl.program_id(0)
     local, width = qp_ref.shape[1], qp_ref.shape[2]
     half = width // 2
     per = local // BLOCK
@@ -545,7 +547,9 @@
     dk_sc[...] = jnp.zeros_like(dk_sc)
     dv_sc[...] = jnp.zeros_like(dv_sc)
 
-    db_ref[...] = jnp.zeros_like(db_ref)
+    @pl.when(micro_at == 0)
+    def _():
+        db_ref[...] = jnp.zeros_like(db_ref)
 
     lo = low_lanes((BLOCK, 128))
 
@@ -615,33 +619,24 @@
         db_ref[0:1, :] += jnp.sum(d_ref[kh, krows, :].astype(f32), axis=0, keepdims=True)
 
 
-def attend_back(own_groups, other_groups, qp, km, kmt, v, dc, ct, lse, gk, gq, kind_col, micro_at, d_before):
+def attend_back(own_groups, other_groups, qp, km, kmt, v, dc, ct, lse, gk, gq, kind_col):
     halves, micro, local, width = qp.shape
     half = width // 2
     heads = width // 128
     length = halves * local
-
-    def one(array):
-        rest = array.shape[2:]
-        return pl.BlockSpec(
-            (array.shape[0], None) + rest, lambda m, *_: (0, micro_at) + (0,) * len(rest)
-        )
-
-    before = () if d_before is None else (d_before,)
     return pl.pallas_call(
-        functools.partial(attend_back_kernel, micro_at),
+        attend_back_kernel,
         grid_spec=pltpu.PrefetchScalarGridSpec(
             num_scalar_prefetch=2,
-            grid=(1,),
-            in_specs=[one(a) for a in (qp, km, kmt, v, dc)]
+            grid=(micro,),
+            in_specs=[whole_micro(a) for a in (qp, km, kmt, v, dc)]
             + [
-                pl.BlockSpec((None, half, length), lambda m, *_: (micro_at, 0, 0)),
-                pl.BlockSpec((None, 8, length), lambda m, *_: (micro_at, 0, 0)),
+                pl.BlockSpec((None, half, length), lambda m, *_: (m, 0, 0)),
+                pl.BlockSpec((None, 8, length), lambda m, *_: (m, 0, 0)),
             ]
-            + [one(a) for a in (gk, gq, kind_col)]
-            + [pl.BlockSpec(memory_space=pl.ANY)] * len(before),
+            + [whole_micro(a) for a in (gk, gq, kind_col)],
             out_specs=[
-                pl.BlockSpec((halves, None, local, 3 * width), lambda m, *_: (0, micro_at, 0, 0)),
+                pl.BlockSpec((halves, None, local, 3 * width), lambda m, *_: (0, m, 0, 0)),
                 pl.BlockSpec((8, 3 * width), lambda m, *_: (0, 0)),
             ],
             scratch_shapes=[
@@ -657,11 +652,10 @@
         ],
         compiler_params=pltpu.CompilerParams(vmem_limit_bytes=VMEM_LIMIT),
         cost_estimate=cost(
-            heads * length * length * 1280, length * width * 16, heads * length * length
+            micro * heads * length * length * 1280, micro * length * width * 16, micro * heads * length * length
         ),
-        input_output_aliases={12: 0} if before else {},
         name="attend_back",
-    )(own_groups, other_groups, qp, km, kmt, v, dc, ct, lse, gk, gq, kind_col, *before)
+    )(own_groups, other_groups, qp, km, kmt, v, dc, ct, lse, gk, gq, kind_col)
 
 
 def norm_forward(hidden):
@@ -1015,11 +1009,14 @@
     vec_ref,
     w_ref,
     dh_ref,
+    keep_ref,
+    taken_ref,
     dx_ref,
     gq_ref,
     gk_ref,
     gv_ref,
     gvec_ref,
+    feed_ref,
     part,
     from_core,
     from_y,
@@ -1027,8 +1024,19 @@
     from_x,
     out_y,
     out_z,
-    held,
     total,
+    feed_out_y,
+    feed_from_y,
+    feed_out_z,
+    feed_from_z,
+    feed_total,
+    feed_from_x,
+    fy_send,
+    fy_recv,
+    fz_send,
+    fz_recv,
+    fx_send,
+    fx_recv,
     dx_out,
     from_dx,
     d_send,
@@ -1062,9 +1070,31 @@
             partner,
         )
 
+    def z_order(step):
+        return lax.rem(z + 1 + step, 4)
+
+    def feed_chip(rail):
+        return keep_ref[rail].astype(f32) + taken_ref[rail].astype(f32)
+
+    def feed_y(zz):
+        return send(feed_out_y.at[zz], feed_from_y.at[zz], fy_send.at[zz], fy_recv.at[zz], beside)
+
+    def feed_z(zz):
+        return send(
+            feed_out_z.at[zz],
+            feed_from_z.at[z],
+            fz_send.at[zz],
+            fz_recv.at[z],
+            (x, slot_of(zz, y, core)),
+        )
+
     @pl.when(step_at == 0)
     def _():
         greet(all_peers())
+        for step in range(4):
+            zz = z_order(step)
+            feed_out_y[zz] = feed_chip(zz * 2 + 1 - y).astype(bf16)
+            feed_y(zz).start()
 
     columns = pl.ds(pl.multiple_of(step_at * width, 128), width)
     grad = tn(x_ref[...], d_ref[:, columns]).astype(bf16)
@@ -1093,9 +1123,6 @@
 
     @pl.when(step_at == 2)
     def _():
-        def z_order(step):
-            return lax.rem(z + 1 + step, 4)
-
         def y_copy(zz):
             return send(out_y.at[zz], from_y.at[zz], y_send.at[zz], y_recv.at[zz], beside)
 
@@ -1129,24 +1156,41 @@
 
         exchange = send(dx_out, from_dx, d_send, d_recv, across)
         exchange.start()
-        for step in range(4):
-            zz = z_order(step)
-            rail = zz * 2 + y
-            core_wait(rail)
-            held[zz] = part[2 * rail + core].astype(f32) + from_core[rail].astype(f32)
         for step in range(3):
             zz = z_order(step)
-            y_copy(zz).wait_recv()
-            out_z[zz] = (held[zz] + from_y[zz].astype(f32)).astype(bf16)
-            z_copy(zz).start()
+            feed_y(zz).wait_recv()
+            feed_out_z[zz] = (feed_chip(zz * 2 + y) + feed_from_y[zz].astype(f32)).astype(bf16)
+            feed_z(zz).start()
+        for step in range(4):
+            core_wait(z_order(step) * 2 + y)
+
+        def chip(zz):
+            rail = zz * 2 + y
+            return part[2 * rail + core].astype(f32) + from_core[rail].astype(f32)
 
         @pl.loop(0, flat // BLOCK)
         def _(i):
             at = pl.ds(pl.multiple_of(i * BLOCK, BLOCK), BLOCK)
             dx_ref[at, :] = dh_ref[at, :] + input_part(i * BLOCK)
 
+        for step in range(3):
+            zz = z_order(step)
+            y_copy(zz).wait_recv()
+            out_z[zz] = (chip(zz) + from_y[zz].astype(f32)).astype(bf16)
+            z_copy(zz).start()
+        feed_y(z).wait_recv()
+        feed_result = feed_chip(z * 2 + y) + feed_from_y[z].astype(f32)
+        for step in range(3):
+            zz = z_order(step)
+            send(
+                feed_out_z.at[zz], feed_from_z.at[zz], fz_send.at[zz], fz_recv.at[zz], partner
+            ).wait_recv()
+            feed_result = feed_result + feed_from_z[zz].astype(f32)
+        feed_total[...] = feed_result.astype(bf16)
+        feed_last = send(feed_total, feed_from_x, fx_send, fx_recv, across)
+        feed_last.start()
         y_copy(z).wait_recv()
-        result = held[z] + from_y[z].astype(f32)
+        result = chip(z) + from_y[z].astype(f32)
         for step in range(3):
             zz = z_order(step)
             send(out_z.at[zz], from_z.at[zz], z_send.at[zz], z_recv.at[zz], partner).wait_recv()
@@ -1166,10 +1210,16 @@
                 core_copy(chunk, rail).wait_send()
         for step in range(4):
             y_copy(z_order(step)).wait_send()
+            feed_y(z_order(step)).wait_send()
         for step in range(3):
             z_copy(z_order(step)).wait_send()
+            feed_z(z_order(step)).wait_send()
+        first = x == 0
+        feed_last.wait()
+        own_feed, far_feed = feed_total[...].astype(f32), feed_from_x[...].astype(f32)
+        feed_ref[:, :half] = jnp.where(first, own_feed, far_feed)
+        feed_ref[:, half:] = jnp.where(first, far_feed, own_feed)
         last.wait()
-        first = x == 0
         lo = low_lanes((rows, 128))
 
         def ordered(start, size, at):
@@ -1194,7 +1244,7 @@
         gvec_ref[...] = total[3 * rows :, :].astype(f32) + from_x[3 * rows :, :].astype(f32)
 
 
-def scatter_attention(x, d, vectors, weights, dh):
+def scatter_attention(x, d, vectors, weights, dh, keep, taken):
     tokens, width = x.shape
     rows = width // GROUPS
     tall = 3 * rows + 16
@@ -1203,7 +1253,7 @@
     def whole(*dims):
         return pl.BlockSpec(dims, lambda i: (0,) * len(dims), pipeline_mode=pl.Buffered(1))
 
-    outs = (dh.shape, (rows, 4 * width), (rows, width), (rows, width), (16, width))
+    outs = (dh.shape, (rows, 4 * width), (rows, width), (rows, width), (16, width), (9 * rows, width))
     return pl.pallas_call(
         scatter_kernel,
         grid=(3,),
@@ -1213,6 +1263,8 @@
             whole(GROUPS, 16, width),
             whole(*weights.shape),
             whole(*dh.shape),
+            whole(*keep.shape),
+            whole(*keep.shape),
         ],
         out_specs=[whole(*dims) for dims in outs],
         out_shape=[jax.ShapeDtypeStruct(dims, f32) for dims in outs],
@@ -1224,8 +1276,19 @@
             pltpu.VMEM((tall, width), bf16),
             pltpu.VMEM((4, tall, width), bf16),
             pltpu.VMEM((4, tall, width), bf16),
-            pltpu.VMEM((4, tall, width), f32),
             pltpu.VMEM((tall, width), bf16),
+            pltpu.VMEM((4,) + keep.shape[1:], bf16),
+            pltpu.VMEM((4,) + keep.shape[1:], bf16),
+            pltpu.VMEM((4,) + keep.shape[1:], bf16),
+            pltpu.VMEM((4,) + keep.shape[1:], bf16),
+            pltpu.VMEM(keep.shape[1:], bf16),
+            pltpu.VMEM(keep.shape[1:], bf16),
+            sem((4,)),
+            sem((4,)),
+            sem((4,)),
+            sem((4,)),
+            sem,
+            sem,
             pltpu.VMEM(dh.shape, bf16),
             pltpu.VMEM(dh.shape, bf16),
             sem,
@@ -1244,7 +1307,7 @@
         ),
         cost_estimate=cost(2 * tokens * width * width * 3, tokens * width * 8 + width * width * 6),
         name="scatter",
-    )(x, d, vectors, weights, dh)
+    )(x, d, vectors, weights, dh, keep, taken)
 
 
 def input_grad_kernel(d_ref, w_ref, out_ref):
@@ -1414,28 +1477,13 @@
     dc_swapped, feed_part = lax.optimization_barrier((dc_swapped, feed_part))
     dc = jnp.stack([dc_own, dc_swapped]).reshape(2, micro, local, half)
 
-    def mix_back(micro_at, before):
-        return attend_back(
-            own_groups, far_groups, qp, km, kmt, v, dc, ct, lse, gk, gq, kind_col, micro_at, before
-        )
-
-    d, db = None, 0.0
-    for m in range(micro - 1):
-        d, part = mix_back(m, d)
-        db = db + part
-    rails = None
     if direct:
-        rails = [[2 * rail + core for rail in range(8)] for core in range(2)]
         keep, give = feed_part
-        taken, d = lax.optimization_barrier((swap(give), d))
-        feed_part = (keep.astype(f32) + taken.astype(f32)).astype(bf16)
+        taken = swap(give)
     else:
         feed_part = ungroup(feed_part[0], feed_sizes, devices)
-    feed_sum = lax.psum_scatter(
-        feed_part, "shard", scatter_dimension=0, axis_index_groups=rails, tiled=True
-    )[0]
-    d, part = mix_back(micro - 1, d)
-    db = db + part
+        feed_sum = lax.psum_scatter(feed_part, "shard", scatter_dimension=0, tiled=True)[0]
+    d, db = attend_back(own_groups, far_groups, qp, km, kmt, v, dc, ct, lse, gk, gq, kind_col)
 
     query_own = unpair_columns(db[0, : 2 * width].reshape(2, width), head_dim)
     zero = jnp.zeros((half,), f32)
@@ -1465,8 +1513,8 @@
     flat_x = xs.reshape(2 * flat, width)
     flat_d = d.reshape(2 * flat, 3 * width)
     if direct:
-        input_grad, grad_query, grad_key, grad_value, vec_rows = scatter_attention(
-            flat_x, flat_d, grad_vectors, attn_w, dh1
+        input_grad, grad_query, grad_key, grad_value, vec_rows, feed_total = scatter_attention(
+            flat_x, flat_d, grad_vectors, attn_w, dh1, keep, taken
         )
         input_grad = input_grad.reshape(micro, local, width)
         vec_total = vec_rows[0, :piece]
@@ -1485,15 +1533,8 @@
         dx_own = input_grad_part(d, attn_w, 0, f32)
         input_grad = dh1.reshape(micro, local, width) + dx_own + swap(dx_other).astype(f32)
 
-    feed_other = swap(feed_sum)
-    if direct:
-        feed_total = jnp.where(
-            side == 0,
-            jnp.concatenate([feed_sum, feed_other], axis=1),
-            jnp.concatenate([feed_other, feed_sum], axis=1),
-        ).astype(f32)
-    else:
-        feed_total = feed_sum.astype(f32) + feed_other.astype(f32)
+    if not direct:
+        feed_total = feed_sum.astype(f32) + swap(feed_sum).astype(f32)
     grad_down = feed_total[: 4 * rows]
     grad_output = feed_total[4 * rows : 5 * rows]
     grad_up = jnp.concatenate(

time: 426 us -> 406 us (0.953); the launches traced: 425 us -> 399 us
  waiting for transfers between devices: 31.5 us -> 2.24 us
  Pallas kernels: 348 us -> 354 us
  other arithmetic: 9.71 us -> 4.51 us
    ppermute x3 -> x2, waiting for transfers between devices: 31.4 us -> 2.22 us  [swap(): return lax.ppermute(value, 'seq', [(0, 1), (1, 0)])]
    pallas_call x1, Pallas kernels: 95.2 us -> 108 us  [scatter_attention(): pl.pallas_call(scatter_kernel, grid=(3,), in_specs=[whole(tokens, width),...]
    pallas_call x2 -> x1, Pallas kernels: 59.3 us -> 52.7 us  [attend_back(): pl.pallas_call(attend_back_kernel, grid_spec=pltpu.PrefetchScalarGridSpec...]
    convert_element_type x2 -> x0, other arithmetic: 5.15 us -> none  [the longest x1 3.91 us: on_device(): feed_part = (keep.astype(f32) + taken.astype(f32)).astype(bf16)]
  transfers between devices with their start and end apart: 5 -> 3, of which waited for: 2 -> 1; matrix products, arithmetic and copies ran while one was open for 3% -> 3% of each run, Pallas kernels for 68% -> 46%
where the time goes in v6:
time: 406 us; the launch traced here: 399 us
  Pallas kernels  354 us (87%)
  local copies, waits for them, and re-layouts  21.6 us (5%)
  between operations  14.3 us (4%)
  other arithmetic  4.51 us (1%)
    pallas_call x1, Pallas kernels, scatter_attention(): pl.pallas_call(scatter_kernel, grid=(3,), in_specs=[whole(tokens, width),...  108 us
    pallas_call x1, Pallas kernels, chain(): pl.pallas_call(chain_kernel, grid_spec=pltpu.PrefetchScalarGridSpec(num_s...  58.7 us
    pallas_call x1, Pallas kernels, attend_back(): pl.pallas_call(attend_back_kernel, grid_spec=pltpu.PrefetchScalarGridSpec...  52.7 us
    pallas_call x1, Pallas kernels, gather_attention(): pl.pallas_call(gather_kernel, in_specs=[vmem] * 13 + [anywhere] * 3, out_...  52.2 us
    pallas_call x1, Pallas kernels, attend(): pl.pallas_call(attend_kernel, grid_spec=pltpu.PrefetchScalarGridSpec(num_...  42.8 us
    pallas_call x1, Pallas kernels, feed_grad(): pl.pallas_call(chip_grad_kernel if direct else feed_grad_kernel, grid=(9,...  22.5 us
    pallas_call x1, Pallas kernels, project(): pl.pallas_call(project_kernel, grid=(halves, micro, sub), in_specs=[token...  15.1 us
  transfers between devices with their start and end apart: 3, of which 1 were waited for; matrix products, arithmetic and copies ran while one was open for 3% of the time, Pallas kernels for 46%

profile of v6, /device:TPU:0, one launch (start us, length us, event | category | flops | bytes accessed | tf_op | source)
XLA Modules:
  0.0 399.3 jit_solution(2247585079695323197)
XLA Ops:
  7.2 2.0 pack_feed.1
  9.3 1.2 broadcast_in_dim.48.refs_3_
  10.5 1.2 broadcast_in_dim.54.refs_9_
  11.7 52.2 %gather.1 = (bf16[16,160,768]{2,1,0:T(8,128)(2,1)}, bf16[2,1,512,768]{3,2,1,0:T(8,128)(2,1)}, s32[2,1,512]{2,1,0:T(1,128)}, s32[2,1,512]{2,1,0:T(1,128)}) custom-call(bf16[48,3072]{1,0:T(8,128)(2,1)} %refs_0_.1, bf16[48,768]{1,0:T(8,128)(2,1)} %refs_1_.1, bf16[48,768]{1,0:T(8,128)(2,1)} %refs_2_.1, bf16[1,192]{1,0:T(2,128)(2,1)} %broadcast_in_dim.48.refs_3_, ...), custom_call_target="tpu_custom_call" | custom-call | tf_op jit(solution)/shard_map/gather/pallas_call | solution.py:183
  63.9 1.0 slice.193
  65.0 0.1 convert_element_type.103
  65.2 0.1 convert_element_type.106
  65.3 0.1 convert_element_type.105
  66.0 0.6 concatenate.98.vec_ref
  66.7 0.1 reshape.343
  66.8 0.6 pad_maximum_fusion.2.bias_ref
  67.4 1.3 copy_bitcast_fusion.2
  68.7 15.1 %project.1 = (bf16[2,2,512,768]{3,2,1,0:T(8,128)(2,1)}, bf16[2,2,512,768]{3,2,1,0:T(8,128)(2,1)}, bf16[2,2,768,512]{3,2,1,0:T(8,128)(2,1)}, bf16[2,2,512,384]{3,...) custom-call(bf16[2,1,512,768]{3,2,1,0:T(8,128)(2,1)} %own_ref.1, ...), custom_call_target="tpu_custom_call" | custom-call | flops 7247757312 | bytes 15728640 | tf_op jit(solution)/shard_map/project/pallas_call | solution.py:379
  83.7 42.8 %attend.1 = (bf16[2,2,512,384]{3,2,1,0:T(8,128)(2,1)}, f32[2,384,1024]{2,1,0:T(8,128)}, f32[2,8,1024]{2,1,0:T(8,128)}) custom-call(s32[2,512]{1,0:T(2,128)} %get-tuple-element.166.own_ref, s32[2,512]{1,0:T(2,128)} %get-tuple-element.165.other_ref, bf16[2,2,512,768]{3,2,1,0:T(8,128)(2,1)} %get-tuple-element.58.qp_ref, ...), custom_call_target="tpu_custom_call" | custom-call | flops 6442450944 | bytes 12582912 | tf_op jit(solution)/shard_map/attend/pallas_call | solution.py:491
  126.6 58.7 %chain.1 = (bf16[1024,768]{1,0:T(8,128)(2,1)}, f32[1024,768]{1,0:T(8,128)}, bf16[1024,4608]{1,0:T(8,128)(2,1)}, bf16[1024,4608]{1,0:T(8,128)(2,1)}, bf16[1024,38...) custom-call(s32[1]{0:T(128)} %bitcast.side_ref, bf16[1024,768]{1,0:T(8,128)(2,1)} %bitcast.57, ...), custom_call_target="tpu_custom_call" | custom-call | flops 22951231488 | bytes 38928384 | tf_op jit(solution)/shard_map/chain/pallas_call | solution.py:822
  185.3 0.8 convert.64
  186.4 0.1 concatenate.134
  186.4 0.1 concatenate.132
  186.5 0.1 concatenate.131
  186.6 0.1 concatenate.130
  186.7 0.1 concatenate.133
  186.8 2.0 collective-permute-start
  188.8 22.5 %feed_grad.1 = (bf16[8,432,384]{2,1,0:T(8,128)(2,1)}, bf16[8,432,384]{2,1,0:T(8,128)(2,1)}) custom-call(bf16[1024,4608]{1,0:T(8,128)(2,1)} %get-tuple-element.70.l_ref, bf16[1024,4608]{1,0:T(8,128)(2,1)} %get-tuple-element.71.r_ref), custom_call_target="tpu_custom_call" | custom-call | flops 10871635968 | bytes 29491200 | tf_op jit(solution)/shard_map/feed_grad/pallas_call | solution.py:961
  211.4 0.1 collective-permute-start.1
  211.5 1.4 pad_maximum_fusion.dc_ref
  212.9 52.7 %attend_back.1 = (bf16[2,2,512,2304]{3,2,1,0:T(8,128)(2,1)}, f32[8,2304]{1,0:T(8,128)}) custom-call(s32[2,512]{1,0:T(2,128)} %get-tuple-element.166.own_ref, s32[2,512]{1,0:T(2,128)} %get-tuple-element.165.other_ref, bf16[2,2,512,768]{3,2,1,0:T(8,128)(2,1)} %get-tuple-element.58.qp_ref, bf16[2,2,512,768]{3,2,1,0:T(8,128)(2,1)} %get-tuple-element.59.km_ref, ...), custom_call_target="tpu_custom_call" | custom-call | flops 16106127360 | bytes 25165824 | tf_op jit(solution)/shard_map/attend_back/pallas_call | solution.py:627
  265.5 0.8 slice_reduce_fusion
  266.6 0.1 concatenate.101
  266.6 0.1 concatenate.110
  266.7 0.1 concatenate.107
  266.8 0.1 concatenate.104
  266.9 0.7 slice_reduce_fusion.11
  267.7 0.1 concatenate.128
  267.8 0.1 concatenate.129
  267.9 0.3 concatenate.126
  268.2 0.8 pad.16.vec_ref
  269.0 2.2 collective-permute-done.1.taken_ref
  271.2 108.5 %scatter.1 = (f32[1024,768]{1,0:T(8,128)}, f32[48,3072]{1,0:T(8,128)}, f32[48,768]{1,0:T(8,128)}, f32[48,768]{1,0:T(8,128)}, f32[16,768]{1,0:T(8,128)}, /*index=5*/f32[432,768]{1,0:T(8,128)}) custom-call(bf16[2048,768]{1,0:T(8,128)(2,1)} %bitcast.77, bf16[2048,2304]{1,0:T(8,128)(2,1)} %bitcast.76, bf16[16,16,768]{2,1,0:T(8,128)(2,1)} %pad.16.vec_ref, ...), custom_call_target="tpu_custom_call" | custom-call | flops 7247757312 | bytes 16121856 | tf_op jit(solution)/shard_map/scatter/pallas_call | solution.py:1257
  379.8 1.5 fusion.2
  381.2 1.4 slice_bitcast_fusion
  382.6 1.9 slice.243
  384.6 2.1 fusion.1
  386.6 0.9 pad_maximum_fusion.1
  387.5 1.1 copy.70
  388.6 1.7 copy.71
  390.3 0.8 copy.72
  391.1 0.7 copy.73
  391.8 0.7 copy.74
  (50 shorter events, 1.4 us)
Async XLA Ops:
  7.2 60.2 %copy-start.6 = (s32[2,1,512]{2,1,0:T(1,128)S(1)}, s32[2,1,512]{2,1,0:T(1,128)}, u32[]{:S(2)}) copy-start(s32[2,1,512]{2,1,0:T(1,128)} %own_group_ref.1) | copy-start | bytes 12292
  7.2 119.4 %all-gather.3.cloned.1.call-start = ((), (), s32[]{:S(2)}) async-start(), calls=%async_computation | async-start | bytes 11280384 | tf_op jit(solution)/shard_map/all_gather | solution.py:1420
  186.8 24.6 %collective-permute-start = (bf16[1024,384]{1,0:T(8,128)(2,1)}, bf16[1024,384]{1,0:T(8,128)(2,1)S(1)}, u32[]{:S(2)}, u32[]{:S(2)}) collective-permute-start(bf16[1024,384]{1,0:T(8,128)(2,1)} %get-tuple-element.69), channel_id=1, source_target_pairs={{0,16},{16,0},{1,17},{17,1},{2,18},{18,2},{3,19},{19,3},{4,20},{20... | collective-permute-start | bytes 2359304 | tf_op jit(solution)/shard_map/ppermute | solution.py:32
  188.8 22.6 %copy-start.2 = (bf16[1024,384]{1,0:T(8,128)(2,1)S(1)}, bf16[1024,384]{1,0:T(8,128)(2,1)}, u32[]{:S(2)}) copy-start(bf16[1024,384]{1,0:T(8,128)(2,1)} %get-tuple-element.68) | copy-start | bytes 2359300
  211.4 59.9 %collective-permute-start.1 = (bf16[8,432,384]{2,1,0:T(8,128)(2,1)}, bf16[8,432,384]{2,1,0:T(8,128)(2,1)}, u32[]{:S(2)}, u32[]{:S(2)}) collective-permute-start(bf16[8,432,384]{2,1,0:T(8,128)(2,1)} %get-tuple-element.83), channel_id=1, source_target_pairs={{0,16},{16,0},{1,17},{17,1},{2,18},{18,2},{3,19},{19,3},{4,20},{20... | collective-permute-start | bytes 7962632 | tf_op jit(solution)/shard_map/ppermute | solution.py:32
  379.7 7.7 %copy-start.1 = (bf16[1024,768]{1,0:T(8,128)(2,1)S(1)}, bf16[1024,768]{1,0:T(8,128)(2,1)}, u32[]{:S(2)}) copy-start(bf16[1024,768]{1,0:T(8,128)(2,1)} %get-tuple-element.64) | copy-start | bytes 4718596
  384.6 4.1 %copy-start = (f32[1024,768]{1,0:T(8,128)S(1)}, f32[1024,768]{1,0:T(8,128)}, u32[]{:S(2)}) copy-start(f32[1024,768]{1,0:T(8,128)} %get-tuple-element.84) | copy-start | bytes 9437188
  388.6 1.7 copy-start.3
  388.6 2.5 copy-start.5
  388.6 3.2 copy-start.4
Sparse Core Ops, SparseCore 0:
  10.3 108.7 all-gather.2

commit v7 on v6

--- a/solution.py
+++ b/solution.py
@@ -128,16 +128,6 @@
     vec = jnp.concatenate([r[...].astype(f32) for r in vec_refs], axis=1)
     pack_into(x == 0, q_ref, k_ref, v_ref, vec, mine)
     started = []
-    for step in range(1, 4):
-        copy = send(
-            mine,
-            w_ref.at[me],
-            z_send.at[step - 1],
-            z_recv.at[z],
-            (x, slot_of(lax.rem(z + step, 4), y, core)),
-        )
-        copy.start()
-        started.append(copy)
     copy = send(mine, w_ref.at[me], y_send.at[z], y_recv.at[z], beside)
     copy.start()
     started.append(copy)
@@ -147,7 +137,16 @@
     keep = pltpu.make_async_copy(mine, w_ref.at[me], keep_sem)
     keep.start()
     for step in range(1, 4):
-        zz = lax.rem(z + step, 4)
+        copy = send(
+            mine,
+            w_ref.at[me],
+            z_send.at[step - 1],
+            z_recv.at[z],
+            (x, slot_of(lax.rem(z + step, 4), y, core)),
+        )
+        copy.start()
+        started.append(copy)
+        zz = lax.rem(z + 4 - step, 4)
         at = slot_of(zz, y, core)
         held = w_ref.at[at]
         send(held, held, z_send.at[0], z_recv.at[zz], partner).wait_recv()
@@ -158,7 +157,7 @@
             copy.start()
             started.append(copy)
     for step in range(4):
-        zz = lax.rem(z + step, 4)
+        zz = lax.rem(z + 4 - step, 4)
         rail = zz * 2 + 1 - y
         held = w_ref.at[slot_of(zz, 1 - y, core)]
         send(held, held, y_send.at[0], y_recv.at[zz], partner).wait_recv()
@@ -1094,7 +1093,8 @@
         for step in range(4):
             zz = z_order(step)
             feed_out_y[zz] = feed_chip(zz * 2 + 1 - y).astype(bf16)
-            feed_y(zz).start()
+            if step < 2:
+                feed_y(zz).start()
 
     columns = pl.ds(pl.multiple_of(step_at * width, 128), width)
     grad = tn(x_ref[...], d_ref[:, columns]).astype(bf16)
@@ -1142,12 +1142,24 @@
                     partner,
                 ).wait_recv()
 
-        for step in range(4):
-            zz = z_order(step)
-            rail = zz * 2 + 1 - y
-            core_wait(rail)
-            out_y[zz] = (part[2 * rail + core].astype(f32) + from_core[rail].astype(f32)).astype(bf16)
-            y_copy(zz).start()
+        def chip(zz, yy):
+            rail = zz * 2 + yy
+            return part[2 * rail + core].astype(f32) + from_core[rail].astype(f32)
+
+        def feed_forward(zz):
+            feed_y(zz).wait_recv()
+            feed_out_z[zz] = (feed_chip(zz * 2 + y) + feed_from_y[zz].astype(f32)).astype(bf16)
+            feed_z(zz).start()
+
+        def forward(zz):
+            y_copy(zz).wait_recv()
+            out_z[zz] = (chip(zz, y) + from_y[zz].astype(f32)).astype(bf16)
+            z_copy(zz).start()
+
+        feed_forward(z_order(0))
+        feed_forward(z_order(1))
+        feed_y(z_order(2)).start()
+        feed_y(z_order(3)).start()
 
         @pl.loop(0, flat // BLOCK)
         def _(i):
@@ -1156,28 +1168,24 @@
 
         exchange = send(dx_out, from_dx, d_send, d_recv, across)
         exchange.start()
-        for step in range(3):
+        for rail in range(8):
+            core_wait(rail)
+        for step in range(4):
             zz = z_order(step)
-            feed_y(zz).wait_recv()
-            feed_out_z[zz] = (feed_chip(zz * 2 + y) + feed_from_y[zz].astype(f32)).astype(bf16)
-            feed_z(zz).start()
-        for step in range(4):
-            core_wait(z_order(step) * 2 + y)
-
-        def chip(zz):
-            rail = zz * 2 + y
-            return part[2 * rail + core].astype(f32) + from_core[rail].astype(f32)
+            out_y[zz] = chip(zz, 1 - y).astype(bf16)
+        feed_forward(z_order(2))
+        y_copy(z_order(0)).start()
+        y_copy(z_order(1)).start()
 
         @pl.loop(0, flat // BLOCK)
         def _(i):
             at = pl.ds(pl.multiple_of(i * BLOCK, BLOCK), BLOCK)
             dx_ref[at, :] = dh_ref[at, :] + input_part(i * BLOCK)
 
-        for step in range(3):
-            zz = z_order(step)
-            y_copy(zz).wait_recv()
-            out_z[zz] = (chip(zz) + from_y[zz].astype(f32)).astype(bf16)
-            z_copy(zz).start()
+        forward(z_order(0))
+        forward(z_order(1))
+        y_copy(z_order(2)).start()
+        y_copy(z_order(3)).start()
         feed_y(z).wait_recv()
         feed_result = feed_chip(z * 2 + y) + feed_from_y[z].astype(f32)
         for step in range(3):
@@ -1189,8 +1197,9 @@
         feed_total[...] = feed_result.astype(bf16)
         feed_last = send(feed_total, feed_from_x, fx_send, fx_recv, across)
         feed_last.start()
+        forward(z_order(2))
         y_copy(z).wait_recv()
-        result = chip(z) + from_y[z].astype(f32)
+        result = chip(z, y) + from_y[z].astype(f32)
         for step in range(3):
             zz = z_order(step)
             send(out_z.at[zz], from_z.at[zz], z_send.at[zz], z_recv.at[zz], partner).wait_recv()

time: 406 us -> 390 us (0.961); the launches traced: 399 us -> 388 us
  Pallas kernels: 354 us -> 344 us
    pallas_call x1, Pallas kernels: 108 us -> 96.4 us  [scatter_attention(): pl.pallas_call(scatter_kernel, grid=(3,), in_specs=[whole(tokens, width),...]
  transfers between devices with their start and end apart: 3 -> 3, of which waited for: 1 -> 1; matrix products, arithmetic and copies ran while one was open for 3% -> 3% of each run, Pallas kernels for 46% -> 48%
where the time goes in v7:
time: 390 us; the launch traced here: 388 us
  Pallas kernels  344 us (88%)
  local copies, waits for them, and re-layouts  21.7 us (6%)
  between operations  14.3 us (4%)
  other arithmetic  4.51 us (1%)
    pallas_call x1, Pallas kernels, scatter_attention(): pl.pallas_call(scatter_kernel, grid=(3,), in_specs=[whole(tokens, width),...  96.4 us
    pallas_call x1, Pallas kernels, chain(): pl.pallas_call(chain_kernel, grid_spec=pltpu.PrefetchScalarGridSpec(num_s...  58.6 us
    pallas_call x1, Pallas kernels, gather_attention(): pl.pallas_call(gather_kernel, in_specs=[vmem] * 13 + [anywhere] * 3, out_...  54.2 us
    pallas_call x1, Pallas kernels, attend_back(): pl.pallas_call(attend_back_kernel, grid_spec=pltpu.PrefetchScalarGridSpec...  52.6 us
    pallas_call x1, Pallas kernels, attend(): pl.pallas_call(attend_kernel, grid_spec=pltpu.PrefetchScalarGridSpec(num_...  42.8 us
    pallas_call x1, Pallas kernels, feed_grad(): pl.pallas_call(chip_grad_kernel if direct else feed_grad_kernel, grid=(9,...  22.5 us
    pallas_call x1, Pallas kernels, project(): pl.pallas_call(project_kernel, grid=(halves, micro, sub), in_specs=[token...  15.1 us
  transfers between devices with their start and end apart: 3, of which 1 were waited for; matrix products, arithmetic and copies ran while one was open for 3% of the time, Pallas kernels for 48%

profile of v7, /device:TPU:0, one launch (start us, length us, event | category | flops | bytes accessed | tf_op | source)
XLA Modules:
  0.0 388.0 jit_solution(5091142796759377103)
XLA Ops:
  7.2 2.0 pack_feed.1
  9.3 1.2 broadcast_in_dim.48.refs_3_
  10.5 1.2 broadcast_in_dim.54.refs_9_
  11.7 54.2 %gather.1 = (bf16[16,160,768]{2,1,0:T(8,128)(2,1)}, bf16[2,1,512,768]{3,2,1,0:T(8,128)(2,1)}, s32[2,1,512]{2,1,0:T(1,128)}, s32[2,1,512]{2,1,0:T(1,128)}) custom-call(bf16[48,3072]{1,0:T(8,128)(2,1)} %refs_0_.1, bf16[48,768]{1,0:T(8,128)(2,1)} %refs_1_.1, bf16[48,768]{1,0:T(8,128)(2,1)} %refs_2_.1, bf16[1,192]{1,0:T(2,128)(2,1)} %broadcast_in_dim.48.refs_3_, ...), custom_call_target="tpu_custom_call" | custom-call | tf_op jit(solution)/shard_map/gather/pallas_call | solution.py:182
  65.9 1.1 slice.193
  67.1 0.1 convert_element_type.103
  67.2 0.1 convert_element_type.106
  67.3 0.1 convert_element_type.105
  68.1 0.6 concatenate.98.vec_ref
  68.8 0.1 reshape.343
  68.9 0.6 pad_maximum_fusion.2.bias_ref
  69.5 1.3 copy_bitcast_fusion.2
  70.8 15.1 %project.1 = (bf16[2,2,512,768]{3,2,1,0:T(8,128)(2,1)}, bf16[2,2,512,768]{3,2,1,0:T(8,128)(2,1)}, bf16[2,2,768,512]{3,2,1,0:T(8,128)(2,1)}, bf16[2,2,512,384]{3,...) custom-call(bf16[2,1,512,768]{3,2,1,0:T(8,128)(2,1)} %own_ref.1, ...), custom_call_target="tpu_custom_call" | custom-call | flops 7247757312 | bytes 15728640 | tf_op jit(solution)/shard_map/project/pallas_call | solution.py:378
  85.8 42.8 %attend.1 = (bf16[2,2,512,384]{3,2,1,0:T(8,128)(2,1)}, f32[2,384,1024]{2,1,0:T(8,128)}, f32[2,8,1024]{2,1,0:T(8,128)}) custom-call(s32[2,512]{1,0:T(2,128)} %get-tuple-element.166.own_ref, s32[2,512]{1,0:T(2,128)} %get-tuple-element.165.other_ref, bf16[2,2,512,768]{3,2,1,0:T(8,128)(2,1)} %get-tuple-element.58.qp_ref, ...), custom_call_target="tpu_custom_call" | custom-call | flops 6442450944 | bytes 12582912 | tf_op jit(solution)/shard_map/attend/pallas_call | solution.py:490
  128.6 58.6 %chain.1 = (bf16[1024,768]{1,0:T(8,128)(2,1)}, f32[1024,768]{1,0:T(8,128)}, bf16[1024,4608]{1,0:T(8,128)(2,1)}, bf16[1024,4608]{1,0:T(8,128)(2,1)}, bf16[1024,38...) custom-call(s32[1]{0:T(128)} %bitcast.side_ref, bf16[1024,768]{1,0:T(8,128)(2,1)} %bitcast.57, ...), custom_call_target="tpu_custom_call" | custom-call | flops 22951231488 | bytes 38928384 | tf_op jit(solution)/shard_map/chain/pallas_call | solution.py:821
  187.2 0.8 convert.64
  188.3 0.1 concatenate.134
  188.4 0.1 concatenate.132
  188.4 0.1 concatenate.131
  188.5 0.1 concatenate.130
  188.6 0.1 concatenate.133
  188.7 1.0 collective-permute-start
  189.7 22.5 %feed_grad.1 = (bf16[8,432,384]{2,1,0:T(8,128)(2,1)}, bf16[8,432,384]{2,1,0:T(8,128)(2,1)}) custom-call(bf16[1024,4608]{1,0:T(8,128)(2,1)} %get-tuple-element.70.l_ref, bf16[1024,4608]{1,0:T(8,128)(2,1)} %get-tuple-element.71.r_ref), custom_call_target="tpu_custom_call" | custom-call | flops 10871635968 | bytes 29491200 | tf_op jit(solution)/shard_map/feed_grad/pallas_call | solution.py:960
  212.2 1.1 collective-permute-start.1
  213.4 1.4 pad_maximum_fusion.dc_ref
  214.7 52.6 %attend_back.1 = (bf16[2,2,512,2304]{3,2,1,0:T(8,128)(2,1)}, f32[8,2304]{1,0:T(8,128)}) custom-call(s32[2,512]{1,0:T(2,128)} %get-tuple-element.166.own_ref, s32[2,512]{1,0:T(2,128)} %get-tuple-element.165.other_ref, bf16[2,2,512,768]{3,2,1,0:T(8,128)(2,1)} %get-tuple-element.58.qp_ref, bf16[2,2,512,768]{3,2,1,0:T(8,128)(2,1)} %get-tuple-element.59.km_ref, ...), custom_call_target="tpu_custom_call" | custom-call | flops 16106127360 | bytes 25165824 | tf_op jit(solution)/shard_map/attend_back/pallas_call | solution.py:626
  267.4 0.8 slice_reduce_fusion
  268.4 0.1 concatenate.101
  268.5 0.1 concatenate.110
  268.6 0.1 concatenate.107
  268.7 0.1 concatenate.104
  268.8 0.7 slice_reduce_fusion.11
  269.6 0.1 concatenate.128
  269.6 0.1 concatenate.129
  269.8 0.3 concatenate.126
  270.1 0.8 pad.16.vec_ref
  270.9 1.2 collective-permute-done.1.taken_ref
  272.1 96.4 %scatter.1 = (f32[1024,768]{1,0:T(8,128)}, f32[48,3072]{1,0:T(8,128)}, f32[48,768]{1,0:T(8,128)}, f32[48,768]{1,0:T(8,128)}, f32[16,768]{1,0:T(8,128)}, /*index=5*/f32[432,768]{1,0:T(8,128)}) custom-call(bf16[2048,768]{1,0:T(8,128)(2,1)} %bitcast.77, bf16[2048,2304]{1,0:T(8,128)(2,1)} %bitcast.76, bf16[16,16,768]{2,1,0:T(8,128)(2,1)} %pad.16.vec_ref, ...), custom_call_target="tpu_custom_call" | custom-call | flops 7247757312 | bytes 16121856 | tf_op jit(solution)/shard_map/scatter/pallas_call | solution.py:1266
  368.5 1.5 fusion.2
  370.0 1.4 slice_bitcast_fusion
  371.4 1.9 slice.243
  373.3 2.1 fusion.1
  375.4 0.9 pad_maximum_fusion.1
  376.2 1.1 copy.70
  377.4 1.7 copy.71
  379.0 0.8 copy.72
  379.8 0.7 copy.73
  380.5 0.7 copy.74
  (50 shorter events, 1.4 us)
Async XLA Ops:
  7.2 62.3 %copy-start.6 = (s32[2,1,512]{2,1,0:T(1,128)S(1)}, s32[2,1,512]{2,1,0:T(1,128)}, u32[]{:S(2)}) copy-start(s32[2,1,512]{2,1,0:T(1,128)} %own_group_ref.1) | copy-start | bytes 12292
  7.2 121.4 %all-gather.3.cloned.1.call-start = ((), (), s32[]{:S(2)}) async-start(), calls=%async_computation | async-start | bytes 11280384 | tf_op jit(solution)/shard_map/all_gather | solution.py:1429
  188.7 23.5 %collective-permute-start = (bf16[1024,384]{1,0:T(8,128)(2,1)}, bf16[1024,384]{1,0:T(8,128)(2,1)S(1)}, u32[]{:S(2)}, u32[]{:S(2)}) collective-permute-start(bf16[1024,384]{1,0:T(8,128)(2,1)} %get-tuple-element.69), channel_id=1, source_target_pairs={{0,16},{16,0},{1,17},{17,1},{2,18},{18,2},{3,19},{19,3},{4,20},{20... | collective-permute-start | bytes 2359304 | tf_op jit(solution)/shard_map/ppermute | solution.py:32
  189.7 23.7 %copy-start.2 = (bf16[1024,384]{1,0:T(8,128)(2,1)S(1)}, bf16[1024,384]{1,0:T(8,128)(2,1)}, u32[]{:S(2)}) copy-start(bf16[1024,384]{1,0:T(8,128)(2,1)} %get-tuple-element.68) | copy-start | bytes 2359300
  212.2 59.9 %collective-permute-start.1 = (bf16[8,432,384]{2,1,0:T(8,128)(2,1)}, bf16[8,432,384]{2,1,0:T(8,128)(2,1)}, u32[]{:S(2)}, u32[]{:S(2)}) collective-permute-start(bf16[8,432,384]{2,1,0:T(8,128)(2,1)} %get-tuple-element.83), channel_id=1, source_target_pairs={{0,16},{16,0},{1,17},{17,1},{2,18},{18,2},{3,19},{19,3},{4,20},{20... | collective-permute-start | bytes 7962632 | tf_op jit(solution)/shard_map/ppermute | solution.py:32
  368.5 7.7 %copy-start.1 = (bf16[1024,768]{1,0:T(8,128)(2,1)S(1)}, bf16[1024,768]{1,0:T(8,128)(2,1)}, u32[]{:S(2)}) copy-start(bf16[1024,768]{1,0:T(8,128)(2,1)} %get-tuple-element.64) | copy-start | bytes 4718596
  373.3 4.1 %copy-start = (f32[1024,768]{1,0:T(8,128)S(1)}, f32[1024,768]{1,0:T(8,128)}, u32[]{:S(2)}) copy-start(f32[1024,768]{1,0:T(8,128)} %get-tuple-element.84) | copy-start | bytes 9437188
  377.4 1.7 copy-start.3
  377.4 2.5 copy-start.5
  377.4 3.2 copy-start.4
Sparse Core Ops, SparseCore 0:
  10.3 106.5 all-gather.2
